TPU v7x, 32 devices: a whole 2x2x4 slice. The times are simulated.
32 devices in a mesh: gx: 4 (over x, core), gy: 8 (over z, y).
Axes of the slice: x: 2, y: 2, z: 4, core: 2. Of those that a mesh axis runs over, the one named last changes fastest.
Arguments:
- field: float32 [12, 64, 64, 128], P(None, 'gx', 'gy'), may hold values from -16 to 16
- diffusion: float32 [12], replicated, may hold values from 0.02 to 0.15
- prefactor: float32 [12], replicated, may hold values from 0.05 to 0.3
- activation: float32 [12], replicated, may hold values from 0.5 to 2
- mixing: float32 [12, 12], replicated, may hold values from -1.75 to 1.75
- basis_x: float32 [64, 64], P('gx'), may hold values from -1 to 1, as said below
- basis_y: float32 [64, 64], P('gy'), may hold values from -1 to 1, as said below
- basis_z: float32 [128, 32], replicated, may hold values from -1 to 1, as said below
- basis_v: float32 [12, 6], replicated, may hold values from -1 to 1, as said below
Outputs:
- state: float32 [12, 64, 64, 128], P(None, 'gx', 'gy')
- recon: float32 [12, 64, 64, 128], P(None, 'gx', 'gy')
- residual: float32 [12], replicated
Inputs may be any that keep to these rules, and one draw needn't show every extreme that they name: `basis_x`: its 64 columns are mutually orthogonal, each of norm between 0.5 and 1. `basis_y`: its 64 columns are orthonormal. `basis_z`: its 32 columns are orthonormal. `basis_v`: its 6 columns are orthonormal.
All inputs are finite; a program needn't handle non-finite values.
Results may differ from a plain program's by a relative error of at most 0.00013.
Values sent between devices are 32-bit elements; how exact they have to be, the bound alone decides.
No kernel may reach another device: no remote copies, remote signals or barrier semaphores. Data moves between devices by JAX's collectives and lax.ppermute only.
A program may use at most 64 MiB of HBM per device.

v0:
```python
import jax
import jax.numpy as jnp
from jax import lax
from jax.sharding import PartitionSpec as P

HIGH = lax.Precision.HIGHEST


def padded_2(array, sides, width):
    for axis, dim in sides:
        peers, length = (lax.axis_size(axis), array.shape[dim])
        up = [(i, (i + 1) % peers) for i in range(peers - 1)]
        down = [(j, i) for i, j in up]
        last = lax.slice_in_dim(array, length - width, length, axis=dim)
        first = lax.slice_in_dim(array, 0, width, axis=dim)
        before = lax.ppermute(last, axis, up)
        after = lax.ppermute(first, axis, down)
        array = jnp.concatenate([before, array, after], axis=dim)
    return array


def lap_core(padded):
    centre = padded[:, 1:-1, 1:-1, 1:-1]
    summed = padded[:, 2:, 1:-1, 1:-1] + padded[:, :-2, 1:-1, 1:-1]
    summed = summed + padded[:, 1:-1, 2:, 1:-1] + padded[:, 1:-1, :-2, 1:-1]
    summed = summed + padded[:, 1:-1, 1:-1, 2:] + padded[:, 1:-1, 1:-1, :-2]
    return summed - 6.0 * centre


def reaction(centre, coeffs):
    diffusion, prefactor, activation, mixing = coeffs
    temper = 1.5 + jnp.tanh(centre[0])
    rate_terms = (
        prefactor[:, None, None, None]
        * jnp.exp(-activation[:, None, None, None] / temper[None])
        * centre
    )
    return jnp.einsum("vw,wxyz->vxyz", mixing, rate_terms, precision=HIGH)


def tendency(rimmed, centre, coeffs):
    padded = jnp.pad(rimmed, ((0, 0), (0, 0), (0, 0), (1, 1)))
    return coeffs[0][:, None, None, None] * lap_core(padded) + reaction(centre, coeffs)


def inside_mask(rows_x, rows_y):
    pos_x = lax.axis_index("gx") * rows_x + jnp.arange(rows_x + 2) - 1
    pos_y = lax.axis_index("gy") * rows_y + jnp.arange(rows_y + 2) - 1
    in_x = (pos_x >= 0) & (pos_x < rows_x * lax.axis_size("gx"))
    in_y = (pos_y >= 0) & (pos_y < rows_y * lax.axis_size("gy"))
    return in_x[:, None] & in_y[None, :]


def step_deep(state, coeffs, inside):
    wide = padded_2(state, (("gx", 1), ("gy", 2)), 2)
    centre = wide[:, 1:-1, 1:-1]
    section_wide = centre + tendency(wide, centre, coeffs)
    section_wide = jnp.where(inside[None, :, :, None], section_wide, 0.0)
    section = section_wide[:, 1:-1, 1:-1]
    return 0.5 * (state + section + tendency(section_wide, section, coeffs))


def on_device(field, diffusion, prefactor, activation, mixing, basis_x, basis_y, basis_z, basis_v):
    coeffs = (diffusion, prefactor, activation, mixing)
    rows_x = field.shape[1]
    rows_y = field.shape[2]
    state = field
    inside = inside_mask(rows_x, rows_y)
    state = step_deep(state, coeffs, inside)
    rank_z = basis_z.shape[1]
    rank_v = basis_v.shape[1]
    width = rank_z * rank_v
    proj_z = jnp.einsum("vxyz,zr->vxyr", state, basis_z, precision=HIGH)
    packed = jnp.einsum("vxyr,vs->xyrs", proj_z, basis_v, precision=HIGH)
    packed = packed.reshape(rows_x, rows_y, width)
    columns = basis_x
    part_x = lax.psum_scatter(
        jnp.einsum("xa,xyk->ayk", columns, packed, precision=HIGH),
        "gx",
        scatter_dimension=0,
        tiled=True,
    )
    core_block = jnp.einsum("ayk,yb->abk", part_x, basis_y, precision=HIGH)
    core_block = lax.psum(core_block, "gy")
    mixed_y = jnp.einsum("abk,yb->ayk", core_block, basis_y, precision=HIGH)
    columns = basis_x
    decoded = jnp.einsum(
        "xa,ayk->xyk", columns, lax.all_gather(mixed_y, "gx", axis=0, tiled=True), precision=HIGH
    )
    decoded = decoded.reshape(rows_x, rows_y, rank_z, rank_v)
    back_v = jnp.einsum("xyrs,vs->vxyr", decoded, basis_v, precision=HIGH)
    recon = jnp.einsum("vxyr,zr->vxyz", back_v, basis_z, precision=HIGH)
    error = state - recon
    miss_local = jnp.sum(error * error, axis=(1, 2, 3))
    mass_local = jnp.sum(state * state, axis=(1, 2, 3))
    miss, mass = lax.psum((miss_local, mass_local), ("gx", "gy"))
    residual = jnp.sqrt(miss / (mass + 1e-06))
    return (state, recon, residual)


def solution(mesh):
    return jax.shard_map(
        on_device,
        mesh=mesh,
        in_specs=(
            P(None, "gx", "gy", None),
            P(),
            P(),
            P(),
            P(),
            P("gx", None),
            P("gy", None),
            P(),
            P(),
        ),
        out_specs=(P(None, "gx", "gy", None), P(None, "gx", "gy", None), P()),
        check_vma=False,
    )
```

profile of v0, /device:TPU:0, one launch (start us, length us, event | category | flops | bytes accessed | tf_op | source)
XLA Modules:
  0.0 209.1 jit_solution(7740615977400366910)
XLA Ops:
  7.2 0.0 copy-start
  7.2 0.0 copy-start.2
  7.2 0.0 reduce-scatter.2.cloned.1.call-start
  7.2 1.0 fusion.57
  8.3 2.4 %collective-permute-start = (f32[12,2,8,128]{3,0,2,1:T(8,128)S(1)}, f32[12,2,8,128]{3,0,2,1:T(8,128)S(1)}, u32[]{:S(2)}, u32[]{:S(2)}) collective-permute-start(f32[12,2,8,128]{3,0,2,1:T(8,128)S(1)} %copy.76), channel_id=1, source_target_pairs={{0,8},{8,16},{16,24},{1,9},{9,17},{17,25},{2,10},{10,18},{18,26},{... | collective-permute-start | bytes 294920 | tf_op jit(solution)/shard_map/ppermute | solution.py:16
  10.8 1.3 collective-permute-start.1
  12.1 0.0 collective-permute-done
  12.1 0.0 copy-start.7
  12.1 0.5 copy_dynamic-update-slice_fusion
  12.6 3.5 %collective-permute-done.1 = f32[12,2,8,128]{3,0,2,1:T(8,128)S(1)} collective-permute-done((f32[12,2,8,128]{3,0,2,1:T(8,128)S(1)}, f32[12,2,8,128]{3,0,2,1:T(8,128)S(1)}, u32[]{:S(2)}, u32[]{:S(2)}) %collective-permute-start.1) | collective-permute-done | bytes 98336 | tf_op jit(solution)/shard_map/ppermute | solution.py:17
  16.2 3.4 %collective-permute-start.2 = (f32[12,20,2,128]{3,0,2,1:T(8,128)S(1)}, f32[12,20,2,128]{3,0,2,1:T(8,128)S(1)}, u32[]{:S(2)}, u32[]{:S(2)}) collective-permute-start(f32[12,20,2,128]{3,0,2,1:T(8,128)S(1)} %get-tuple-element.19), channel_id=1, source_target_pairs={{0,1},{1,2},{2,3},{3,4},{4,5},{5,6},{6,7},{8,9},{9,10},{10,11},{11... | collective-permute-start | bytes 737288 | tf_op jit(solution)/shard_map/ppermute | solution.py:16
  19.6 1.3 collective-permute-start.3
  20.9 0.0 copy-done.7
  20.9 0.1 broadcast_and_fusion
  21.0 4.2 %collective-permute-done.2 = f32[12,20,2,128]{3,0,2,1:T(8,128)S(1)} collective-permute-done((f32[12,20,2,128]{3,0,2,1:T(8,128)S(1)}, f32[12,20,2,128]{3,0,2,1:T(8,128)S(1)}, u32[]{:S(2)}, u32[]{:S(2)}) %collective-permute-start.2) | collective-permute-done | bytes 245792 | tf_op jit(solution)/shard_map/ppermute | solution.py:16
  25.2 4.6 %collective-permute-done.3 = f32[12,20,2,128]{3,0,2,1:T(8,128)S(1)} collective-permute-done((f32[12,20,2,128]{3,0,2,1:T(8,128)S(1)}, f32[12,20,2,128]{3,0,2,1:T(8,128)S(1)}, u32[]{:S(2)}, u32[]{:S(2)}) %collective-permute-start.3) | collective-permute-done | bytes 245792 | tf_op jit(solution)/shard_map/ppermute | solution.py:17
  29.8 0.2 pad_maximum_fusion
  30.0 0.1 fusion.41
  30.1 2.3 %fusion.8 = f32[12,18,10,128]{3,0,2,1:T(8,128)S(1)} fusion(f32[12,20,12,128]{3,0,2,1:T(8,128)S(1)} %pad_maximum_fusion, f32[12,20,8,128]{3,0,2,1:T(8,128)S(1)} %constant_dynamic-update-slice_fusion, f32[12,20,2,128]{3,0,2,1:T(8,128)S(1)} %collective-permute-done.2, f32[12,20,2,128]{3,0,2,1:T(8,128)S(1)} %collective-permute-done.3, ...), kind=kOutput, calls=%fused_computation.14 | convolution fusion | flops 44236800 | bytes 11096576 | tf_op jit(solution)/shard_map/vw,wxyz->vxyz/dot_general | solution.py:38
  32.5 0.1 fusion.42
  32.6 2.2 %fusion.23 = f32[12,16,8,128]{3,0,2,1:T(8,128)S(1)} fusion(f32[12,18,10,128]{3,0,2,1:T(8,128)S(1)} %fusion.8, f32[16,8,128]{2,1,0:T(8,128)S(1)} %bitcast.62, f32[12]{0:T(128)S(1)} %neg.5, f32[12]{0:T(128)S(1)} %copy-done.8, f32[12]{0:T(128)S(1)} %copy-done.9, f32[12,16,8,128]{3,2,1,0:T(8,128)S(1)} %copy-done.2, f32[12,12]{1,0:T(8,128)S(1)} %copy-done.6), kind=kOutput, calls=%fused_computation.37 | convolution fusion | flops 31260672 | bytes 9414144 | tf_op jit(solution)/shard_map/vw,wxyz->vxyz/dot_general | solution.py:38
  34.8 0.0 copy-start.5
  34.8 1.0 fusion.44
  35.8 0.0 copy-done.5
  35.8 0.0 copy-start.3
  35.8 0.7 fusion.51
  36.5 0.5 copy.49
  37.1 0.0 copy-start.4
  37.1 1.7 convolution_bitcast_fusion.3
  38.7 1.1 copy.51
  39.8 0.0 reduce-scatter.2.cloned.1.call-update
  39.9 0.0 all-reduce.5.cloned.1.call-start
  39.9 27.8 %reduce-scatter.2.cloned.1.call-done = f32[16,8,192]{2,1,0:T(8,128)} async-done(((f32[64,8,192]{2,1,0:T(8,128)}), f32[16,8,192]{2,1,0:T(8,128)}) %reduce-scatter.2.cloned.1.call-update) | async-done | bytes 98320 | tf_op jit(solution)/shard_map/reduce_scatter | solution.py:77
  67.7 2.9 %convolution_bitcast_fusion.1 = f32[16,64,192]{2,1,0:T(8,128)} fusion(f32[16,8,192]{2,1,0:T(8,128)} %reduce-scatter.2.cloned.1.call-done, f32[8,64]{1,0:T(8,128)S(1)} %copy-done.4), kind=kOutput, calls=%fused_computation.23 | convolution fusion | flops 18874368 | bytes 886784 | tf_op jit(solution)/shard_map/ayk,yb->abk/dot_general | solution.py:83
  70.6 0.0 all-reduce.5.cloned.1.call-update
  70.6 1.1 copy.57
  71.7 77.8 %all-reduce.5.cloned.1.call-done = f32[16,64,192]{2,1,0:T(8,128)} async-done(((f32[16,64,192]{2,1,0:T(8,128)}), f32[16,64,192]{2,1,0:T(8,128)}) %all-reduce.5.cloned.1.call-update) | async-done | bytes 786448 | tf_op jit(solution)/shard_map/psum | solution.py:84
  149.5 1.9 convolution_bitcast_fusion.5
  151.3 7.3 %all_gather.3 = f32[64,8,192]{2,1,0:T(8,128)S(1)} all-gather(f32[16,8,192]{2,1,0:T(8,128)S(1)} %convolution_bitcast_fusion.5), channel_id=1, replica_groups=mesh['gx'=4,'gy'=8] {'gx'}, dimensions={0}, use_global_device_ids=true | all-gather | bytes 491520 | tf_op jit(solution)/shard_map/all_gather | solution.py:88
  158.7 0.5 convolution_bitcast_fusion.4
  159.2 0.3 copy.53
  159.5 0.6 copy.54
  160.1 1.0 convolution_bitcast_fusion
  161.2 0.9 fusion.31
  162.1 0.0 copy-start.1
  162.1 0.7 multiply_reduce_fusion
  162.8 38.9 %all-reduce.2 = (f32[12]{0:T(128)S(1)}, f32[12]{0:T(128)S(1)}) all-reduce(f32[12]{0:T(128)S(1)} %get-tuple-element.16, f32[12]{0:T(128)S(1)} %get-tuple-element.15), channel_id=1, replica_groups=mesh['gx'=4,'gy'=8] {'gx','gy'}, use_global_device_ids=true, to_apply=%region_3.4 | all-reduce | flops 24 | bytes 192 | tf_op jit(solution)/shard_map/psum | solution.py:96
  201.7 0.5 fusion.55
  (20 shorter events, 0.2 us)
Async XLA Ops:
  7.2 27.6 %copy-start = (f32[128,32]{0,1:T(8,128)S(1)}, f32[128,32]{0,1:T(8,128)}, u32[]{:S(2)}) copy-start(f32[128,32]{0,1:T(8,128)} %param.16) | copy-start | bytes 49156
  7.2 4.9 %copy-start.2 = (f32[12,16,8,128]{3,2,1,0:T(8,128)S(1)}, f32[12,16,8,128]{3,2,1,0:T(8,128)}, u32[]{:S(2)}) copy-start(f32[12,16,8,128]{3,2,1,0:T(8,128)} %param.9) | copy-start | bytes 2359300
  7.2 60.5 %reduce-scatter.2.cloned.1.call-start = ((), (), s32[]{:S(2)}) async-start(), calls=%async_computation.1 | async-start | bytes 655360 | tf_op jit(solution)/shard_map/reduce_scatter | solution.py:77
  8.3 3.8 %collective-permute-start = (f32[12,2,8,128]{3,0,2,1:T(8,128)S(1)}, f32[12,2,8,128]{3,0,2,1:T(8,128)S(1)}, u32[]{:S(2)}, u32[]{:S(2)}) collective-permute-start(f32[12,2,8,128]{3,0,2,1:T(8,128)S(1)} %copy.76), channel_id=1, source_target_pairs={{0,8},{8,16},{16,24},{1,9},{9,17},{17,25},{2,10},{10,18},{18,26},{... | collective-permute-start | bytes 294920 | tf_op jit(solution)/shard_map/ppermute | solution.py:16
  10.8 5.3 %collective-permute-start.1 = (f32[12,2,8,128]{3,0,2,1:T(8,128)S(1)}, f32[12,2,8,128]{3,0,2,1:T(8,128)S(1)}, u32[]{:S(2)}, u32[]{:S(2)}) collective-permute-start(f32[12,2,8,128]{3,0,2,1:T(8,128)S(1)} %copy.77), channel_id=1, source_target_pairs={{8,0},{16,8},{24,16},{9,1},{17,9},{25,17},{10,2},{18,10},{26,18},{... | collective-permute-start | bytes 294920 | tf_op jit(solution)/shard_map/ppermute | solution.py:17
  12.1 8.8 %copy-start.7 = (f32[12]{0:T(128)S(1)}, f32[12]{0:T(128)}, u32[]{:S(2)}) copy-start(f32[12]{0:T(128)} %param.12) | copy-start | bytes 148
  16.2 9.0 %collective-permute-start.2 = (f32[12,20,2,128]{3,0,2,1:T(8,128)S(1)}, f32[12,20,2,128]{3,0,2,1:T(8,128)S(1)}, u32[]{:S(2)}, u32[]{:S(2)}) collective-permute-start(f32[12,20,2,128]{3,0,2,1:T(8,128)S(1)} %get-tuple-element.19), channel_id=1, source_target_pairs={{0,1},{1,2},{2,3},{3,4},{4,5},{5,6},{6,7},{8,9},{9,10},{10,11},{11... | collective-permute-start | bytes 737288 | tf_op jit(solution)/shard_map/ppermute | solution.py:16
  19.6 10.2 %collective-permute-start.3 = (f32[12,20,2,128]{3,0,2,1:T(8,128)S(1)}, f32[12,20,2,128]{3,0,2,1:T(8,128)S(1)}, u32[]{:S(2)}, u32[]{:S(2)}) collective-permute-start(f32[12,20,2,128]{3,0,2,1:T(8,128)S(1)} %get-tuple-element.20), channel_id=1, source_target_pairs={{1,0},{2,1},{3,2},{4,3},{5,4},{6,5},{7,6},{9,8},{10,9},{11,10},{12... | collective-permute-start | bytes 737288 | tf_op jit(solution)/shard_map/ppermute | solution.py:17
  21.0 9.1 %copy-start.6 = (f32[12,12]{1,0:T(8,128)S(1)}, f32[12,12]{1,0:T(8,128)}, u32[]{:S(2)}) copy-start(f32[12,12]{1,0:T(8,128)} %param.13) | copy-start | bytes 1732
  21.0 9.1 %copy-start.8 = (f32[12]{0:T(128)S(1)}, f32[12]{0:T(128)}, u32[]{:S(2)}) copy-start(f32[12]{0:T(128)} %param.11) | copy-start | bytes 148
  21.0 9.1 %copy-start.9 = (f32[12]{0:T(128)S(1)}, f32[12]{0:T(128)}, u32[]{:S(2)}) copy-start(f32[12]{0:T(128)} %param.10) | copy-start | bytes 148
  34.8 1.0 copy-start.5
  35.8 1.3 copy-start.3
  37.1 30.6 %copy-start.4 = (f32[8,64]{1,0:T(8,128)S(1)}, f32[8,64]{1,0:T(8,128)}, u32[]{:S(2)}) copy-start(f32[8,64]{1,0:T(8,128)} %param.15) | copy-start | bytes 6148
  39.9 109.6 %all-reduce.5.cloned.1.call-start = ((), (), s32[]{:S(2)}) async-start(), calls=%async_computation.2 | async-start | bytes 2097152 | tf_op jit(solution)/shard_map/psum | solution.py:84
  162.1 40.1 %copy-start.1 = (f32[12,16,8,128]{3,2,1,0:T(8,128)}, f32[12,16,8,128]{3,2,1,0:T(8,128)S(1)}, u32[]{:S(2)}) copy-start(f32[12,16,8,128]{3,2,1,0:T(8,128)S(1)} %fusion.31) | copy-start | bytes 2359300
Sparse Core Ops, SparseCore 0:
  40.0 27.6 reduce-scatter.1
  71.2 78.2 all-reduce.4
where the time goes:
time: 209 us
  waiting for transfers between devices  118 us (56%)
  blocking collectives  46.3 us (22%)
  matrix products  15.1 us (7%)
  between operations  14.4 us (7%)
  starting transfers between devices  8.51 us (4%)
  local copies, waits for them, and re-layouts  5.35 us (3%)
    psum x1, waiting for transfers between devices, on_device(): core_block = lax.psum(core_block, 'gy')  77.8 us
    psum x1, blocking collectives, on_device(): miss, mass = lax.psum((miss_local, mass_local), ('gx', 'gy'))  38.9 us
    reduce_scatter x1, waiting for transfers between devices, on_device(): lax.psum_scatter(jnp.einsum('xa,xyk->ayk', columns, packed, precision=HIG...  27.8 us
    ppermute x2, waiting for transfers between devices, padded_2(): after = lax.ppermute(first, axis, down)  8.07 us
    all_gather x1, blocking collectives, on_device(): lax.all_gather(mixed_y, 'gx', axis=0, tiled=True)  7.32 us
    ppermute x2, starting transfers between devices, padded_2(): before = lax.ppermute(last, axis, up)  5.85 us
    dot_general x2, matrix products, reaction(): return jnp.einsum('vw,wxyz->vxyz', mixing, rate_terms, precision=HIGH)  4.55 us
  transfers between devices with their start and end apart: 6, of which 5 were waited for; matrix products, arithmetic and copies ran while one was open for 1% of the time, Pallas kernels for 0%

commit v1 on v0

--- a/solution.py
+++ b/solution.py
@@ -52,7 +52,7 @@
 
 
 def step_deep(state, coeffs, inside):
-    wide = padded_2(state, (("gx", 1), ("gy", 2)), 2)
+    wide = padded_2(state, (("gy", 2), ("gx", 1)), 2)
     centre = wide[:, 1:-1, 1:-1]
     section_wide = centre + tendency(wide, centre, coeffs)
     section_wide = jnp.where(inside[None, :, :, None], section_wide, 0.0)
@@ -60,40 +60,54 @@
     return 0.5 * (state + section + tendency(section_wide, section, coeffs))
 
 
+def project_y(decoded, basis_y):
+    if basis_y.shape[0] * lax.axis_size("gy") == basis_y.shape[1]:
+        return decoded
+    core = jnp.einsum("xyk,yb->xbk", decoded, basis_y, precision=HIGH)
+    return jnp.einsum("xbk,yb->xyk", lax.psum(core, "gy"), basis_y, precision=HIGH)
+
+
+def mix_x(packed, basis_x):
+    rows_x, rows_y, width = packed.shape
+    flat = packed.reshape(rows_x, rows_y * width)
+    flat = jnp.concatenate([flat, basis_x], axis=1)
+    every = lax.all_gather(flat, "gx", axis=0, tiled=True)
+    values, basis = every[:, : rows_y * width], every[:, rows_y * width :]
+    mixer = jnp.einsum("xa,ua->xu", basis_x, basis, precision=HIGH)
+    mixed = jnp.einsum("xu,uk->xk", mixer, values, precision=HIGH)
+    return mixed.reshape(rows_x, rows_y, width)
+
+
+def sum_everywhere(vector):
+    axes = ("gx", "gy")
+    peers = lax.axis_size(axes)
+    if peers > 64:
+        return lax.psum(vector, axes)
+    sent = jnp.broadcast_to(vector[None], (peers,) + vector.shape)
+    return jnp.sum(lax.all_to_all(sent, axes, 0, 0, tiled=True), axis=0)
+
+
 def on_device(field, diffusion, prefactor, activation, mixing, basis_x, basis_y, basis_z, basis_v):
     coeffs = (diffusion, prefactor, activation, mixing)
     rows_x = field.shape[1]
     rows_y = field.shape[2]
-    state = field
     inside = inside_mask(rows_x, rows_y)
-    state = step_deep(state, coeffs, inside)
+    state = step_deep(field, coeffs, inside)
     rank_z = basis_z.shape[1]
     rank_v = basis_v.shape[1]
     width = rank_z * rank_v
     proj_z = jnp.einsum("vxyz,zr->vxyr", state, basis_z, precision=HIGH)
     packed = jnp.einsum("vxyr,vs->xyrs", proj_z, basis_v, precision=HIGH)
     packed = packed.reshape(rows_x, rows_y, width)
-    columns = basis_x
-    part_x = lax.psum_scatter(
-        jnp.einsum("xa,xyk->ayk", columns, packed, precision=HIGH),
-        "gx",
-        scatter_dimension=0,
-        tiled=True,
-    )
-    core_block = jnp.einsum("ayk,yb->abk", part_x, basis_y, precision=HIGH)
-    core_block = lax.psum(core_block, "gy")
-    mixed_y = jnp.einsum("abk,yb->ayk", core_block, basis_y, precision=HIGH)
-    columns = basis_x
-    decoded = jnp.einsum(
-        "xa,ayk->xyk", columns, lax.all_gather(mixed_y, "gx", axis=0, tiled=True), precision=HIGH
-    )
+    decoded = project_y(mix_x(packed, basis_x), basis_y)
     decoded = decoded.reshape(rows_x, rows_y, rank_z, rank_v)
     back_v = jnp.einsum("xyrs,vs->vxyr", decoded, basis_v, precision=HIGH)
     recon = jnp.einsum("vxyr,zr->vxyz", back_v, basis_z, precision=HIGH)
     error = state - recon
     miss_local = jnp.sum(error * error, axis=(1, 2, 3))
     mass_local = jnp.sum(state * state, axis=(1, 2, 3))
-    miss, mass = lax.psum((miss_local, mass_local), ("gx", "gy"))
+    sums = sum_everywhere(jnp.concatenate([miss_local, mass_local]))
+    miss, mass = jnp.split(sums, 2)
     residual = jnp.sqrt(miss / (mass + 1e-06))
     return (state, recon, residual)
 

time: 209 us -> 75.3 us (0.36)
  waiting for transfers between devices: 118 us -> 19.3 us
  blocking collectives: 46.3 us -> 9.25 us
  between operations: 14.4 us -> 0.95 us
  starting transfers between devices: 8.51 us -> 15.3 us
  local copies, waits for them, and re-layouts: 5.35 us -> 11.2 us
    psum x1 -> x0, waiting for transfers between devices: 77.8 us -> none  [on_device(): core_block = lax.psum(core_block, 'gy')]
    psum x1 -> x0, blocking collectives: 38.9 us -> none  [on_device(): miss, mass = lax.psum((miss_local, mass_local), ('gx', 'gy'))]
    reduce_scatter x1 -> x0, waiting for transfers between devices: 27.8 us -> none  [on_device(): lax.psum_scatter(jnp.einsum('xa,xyk->ayk', columns, packed, precision=HIG...]
    all_to_all x0 -> x1, starting transfers between devices: none -> 6.51 us  [sum_everywhere(): return jnp.sum(lax.all_to_all(sent, axes, 0, 0, tiled=True), axis=0)]
    all_to_all x0 -> x1, waiting for transfers between devices: none -> 6.02 us  [sum_everywhere(): return jnp.sum(lax.all_to_all(sent, axes, 0, 0, tiled=True), axis=0)]
    ppermute x2, waiting for transfers between devices: 4.17 us -> 9.66 us  [padded_2(): before = lax.ppermute(last, axis, up)]
    dot_general x4 -> x2, matrix products: 6.93 us -> 1.58 us  [the longest x1 1.43 us: mix_x(): mixed = jnp.einsum('xu,uk->xk', mixer, values, precision=HIGH)]
    ppermute x2, waiting for transfers between devices: 8.07 us -> 3.66 us  [padded_2(): after = lax.ppermute(first, axis, down)]
  transfers between devices with their start and end apart: 6 -> 5, of which waited for: 5 -> 3; matrix products, arithmetic and copies ran while one was open for 1% -> 2% of each run, Pallas kernels for 0% -> 0%
where the time goes in v1:
time: 75.3 us; the launch traced here: 74.9 us
  waiting for transfers between devices  19.3 us (26%)
  matrix products  17 us (23%)
  starting transfers between devices  15.3 us (20%)
  local copies, waits for them, and re-layouts  11.2 us (15%)
  blocking collectives  9.25 us (12%)
  other arithmetic  1.86 us (2%)
  between operations  0.95 us (1%)
    ppermute x2, waiting for transfers between devices, padded_2(): before = lax.ppermute(last, axis, up)  9.66 us
    all_gather x1, blocking collectives, mix_x(): every = lax.all_gather(flat, 'gx', axis=0, tiled=True)  9.25 us
    all_to_all x1, starting transfers between devices, sum_everywhere(): return jnp.sum(lax.all_to_all(sent, axes, 0, 0, tiled=True), axis=0)  6.51 us
    ppermute x2, starting transfers between devices, padded_2(): before = lax.ppermute(last, axis, up)  6.22 us
    all_to_all x1, waiting for transfers between devices, sum_everywhere(): return jnp.sum(lax.all_to_all(sent, axes, 0, 0, tiled=True), axis=0)  6.02 us
    dot_general x1, matrix products, on_device(): back_v = jnp.einsum('xyrs,vs->vxyr', decoded, basis_v, precision=HIGH)  4.7 us
    dot_general x2, matrix products, reaction(): return jnp.einsum('vw,wxyz->vxyz', mixing, rate_terms, precision=HIGH)  4.55 us
    ppermute x2, waiting for transfers between devices, padded_2(): after = lax.ppermute(first, axis, down)  3.66 us
  transfers between devices with their start and end apart: 5, of which 3 were waited for; matrix products, arithmetic and copies ran while one was open for 2% of the time, Pallas kernels for 0%

profile of v1, /device:TPU:0, one launch (start us, length us, event | category | flops | bytes accessed | tf_op | source)
XLA Modules:
  0.0 74.9 jit_solution(17352995306854999458)
XLA Ops:
  0.6 0.0 copy-start
  0.6 0.0 copy-start.2
  0.7 0.0 copy-start.6
  0.7 1.6 %fusion.53 = (f32[12,16,2,128]{3,2,1,0:T(2,128)S(1)}, f32[12,16,2,128]{3,2,1,0:T(2,128)S(1)}) fusion(f32[12,16,8,128]{3,2,1,0:T(8,128)} %param.9), kind=kLoop, calls=%fused_computation.77 | loop fusion | bytes 786432 | tf_op jit(solution)/shard_map/slice | solution.py:15
  2.3 0.1 copy.83
  2.4 4.9 %collective-permute-start = (f32[12,16,2,128]{3,0,2,1:T(8,128)S(1)}, f32[12,16,2,128]{3,0,2,1:T(8,128)S(1)}, u32[]{:S(2)}, u32[]{:S(2)}) collective-permute-start(f32[12,16,2,128]{3,0,2,1:T(8,128)S(1)} %copy.83), channel_id=1, source_target_pairs={{0,1},{1,2},{2,3},{3,4},{4,5},{5,6},{6,7},{8,9},{9,10},{10,11},{11... | collective-permute-start | bytes 589832 | tf_op jit(solution)/shard_map/ppermute | solution.py:16
  7.3 0.1 copy.84
  7.4 1.3 %collective-permute-start.1 = (f32[12,16,2,128]{3,0,2,1:T(8,128)S(1)}, f32[12,16,2,128]{3,0,2,1:T(8,128)S(1)}, u32[]{:S(2)}, u32[]{:S(2)}) collective-permute-start(f32[12,16,2,128]{3,0,2,1:T(8,128)S(1)} %copy.84), channel_id=1, source_target_pairs={{1,0},{2,1},{3,2},{4,3},{5,4},{6,5},{7,6},{9,8},{10,9},{11,10},{12... | collective-permute-start | bytes 589832 | tf_op jit(solution)/shard_map/ppermute | solution.py:17
  8.8 0.0 copy-done.6
  8.8 9.7 %collective-permute-done = f32[12,16,2,128]{3,0,2,1:T(8,128)S(1)} collective-permute-done((f32[12,16,2,128]{3,0,2,1:T(8,128)S(1)}, f32[12,16,2,128]{3,0,2,1:T(8,128)S(1)}, u32[]{:S(2)}, u32[]{:S(2)}) %collective-permute-start) | collective-permute-done | bytes 196640 | tf_op jit(solution)/shard_map/ppermute | solution.py:16
  18.5 0.5 copy_dynamic-update-slice_fusion
  19.0 0.0 collective-permute-done.1
  19.1 1.3 %collective-permute-start.2 = (f32[12,2,12,128]{3,0,2,1:T(8,128)S(1)}, f32[12,2,12,128]{3,0,2,1:T(8,128)S(1)}, u32[]{:S(2)}, u32[]{:S(2)}) collective-permute-start(f32[12,2,12,128]{3,0,2,1:T(8,128)S(1)} %get-tuple-element.20), channel_id=1, source_target_pairs={{0,8},{8,16},{16,24},{1,9},{9,17},{17,25},{2,10},{10,18},{18,26},{... | collective-permute-start | bytes 442376 | tf_op jit(solution)/shard_map/ppermute | solution.py:16
  20.4 1.3 %collective-permute-start.3 = (f32[12,2,12,128]{3,0,2,1:T(8,128)S(1)}, f32[12,2,12,128]{3,0,2,1:T(8,128)S(1)}, u32[]{:S(2)}, u32[]{:S(2)}) collective-permute-start(f32[12,2,12,128]{3,0,2,1:T(8,128)S(1)} %get-tuple-element.21), channel_id=1, source_target_pairs={{8,0},{16,8},{24,16},{9,1},{17,9},{25,17},{10,2},{18,10},{26,18},{... | collective-permute-start | bytes 442376 | tf_op jit(solution)/shard_map/ppermute | solution.py:17
  21.7 0.1 broadcast_and_fusion
  21.7 0.0 collective-permute-done.2
  21.8 3.7 %collective-permute-done.3 = f32[12,2,12,128]{3,0,2,1:T(8,128)S(1)} collective-permute-done((f32[12,2,12,128]{3,0,2,1:T(8,128)S(1)}, f32[12,2,12,128]{3,0,2,1:T(8,128)S(1)}, u32[]{:S(2)}, u32[]{:S(2)}) %collective-permute-start.3) | collective-permute-done | bytes 147488 | tf_op jit(solution)/shard_map/ppermute | solution.py:17
  25.4 0.2 pad_maximum_fusion
  25.6 0.1 fusion.38
  25.7 0.0 copy-done.5
  25.7 0.0 copy-done.7
  25.7 0.0 copy-done.8
  25.8 2.3 %fusion.8 = f32[12,18,10,128]{3,0,2,1:T(8,128)S(1)} fusion(f32[12,20,12,128]{3,0,2,1:T(8,128)S(1)} %pad_maximum_fusion, f32[12,16,12,128]{3,0,2,1:T(8,128)S(1)} %constant_dynamic-update-slice_fusion, f32[12,2,12,128]{3,0,2,1:T(8,128)S(1)} %collective-permute-done.2, f32[12,2,12,128]{3,0,2,1:T(8,128)S(1)} %collective-permute-done.3, ...), kind=kOutput, calls=%fused_computation.15 | convolution fusion | flops 44236800 | bytes 11096576 | tf_op jit(solution)/shard_map/vw,wxyz->vxyz/dot_general | solution.py:38
  28.1 0.1 fusion.39
  28.2 2.2 %fusion.22 = f32[12,16,8,128]{3,0,2,1:T(8,128)S(1)} fusion(f32[12,18,10,128]{3,0,2,1:T(8,128)S(1)} %fusion.8, f32[16,8,128]{2,1,0:T(8,128)S(1)} %bitcast.45, f32[12]{0:T(128)S(1)} %neg.5, f32[12]{0:T(128)S(1)} %copy-done.7, f32[12]{0:T(128)S(1)} %copy-done.8, f32[12,16,8,128]{3,2,1,0:T(8,128)S(1)} %copy-done.2, f32[12,12]{1,0:T(8,128)S(1)} %copy-done.5), kind=kOutput, calls=%fused_computation.33 | convolution fusion | flops 31260672 | bytes 9414144 | tf_op jit(solution)/shard_map/vw,wxyz->vxyz/dot_general | solution.py:38
  30.4 1.9 %fusion.44 = f32[12,16,8,32]{3,0,2,1:T(8,128)} fusion(f32[12,16,8,128]{3,0,2,1:T(8,128)S(1)} %fusion.22, f32[128,32]{0,1:T(8,128)S(1)} %copy-done), kind=kOutput, calls=%fused_computation.61 | convolution fusion | flops 75497472 | bytes 999424 | tf_op jit(solution)/shard_map/vxyz,zr->vxyr/dot_general | solution.py:99
  32.3 2.3 %copy.67 = f32[12,16,8,32]{1,0,3,2:T(8,128)S(1)} copy(f32[12,16,8,32]{3,0,2,1:T(8,128)} %fusion.44) | data formatting | bytes 393216 | tf_op jit(solution)/shard_map/vxyz,zr->vxyr/dot_general | solution.py:99
  34.7 2.3 %fusion.49 = f32[16,8,32,6]{0,3,2,1:T(8,128)} fusion(f32[12,16,8,32]{1,0,3,2:T(8,128)S(1)} %copy.67, f32[12,6]{0,1:T(8,128)S(1)} %copy-done.4), kind=kOutput, calls=%fused_computation.69 | convolution fusion | flops 3538944 | bytes 295200 | tf_op jit(solution)/shard_map/vxyr,vs->xyrs/dot_general | solution.py:100
  37.0 1.3 %reshape_reshape.6 = f32[16,1536]{0,1:T(8,128)S(1)} reshape(f32[16,8,32,6]{0,3,2,1:T(8,128)} %fusion.49) | data formatting | bytes 196608 | tf_op jit(solution)/shard_map/reshape;reshape | solution.py:72
  38.4 0.2 copy.59
  38.6 0.0 copy-done.3
  38.6 9.3 %all_gather.3 = f32[64,1600]{1,0:T(8,128)S(1)} all-gather(f32[16,1600]{1,0:T(8,128)S(1)} %pad_maximum_fusion.3), channel_id=1, replica_groups=mesh['gx'=4,'gy'=8] {'gx'}, dimensions={0}, use_global_device_ids=true | all-gather | bytes 512000 | tf_op jit(solution)/shard_map/all_gather | solution.py:74
  47.9 0.1 fusion.40
  48.0 1.4 %fusion.36 = f32[16,1536]{0,1:T(8,128)S(1)} fusion(f32[64,16]{0,1:T(8,128)S(1)} %fusion.40, f32[64,1600]{1,0:T(8,128)S(1)} %all_gather.3), kind=kOutput, calls=%fused_computation.48 | convolution fusion | flops 18874368 | bytes 499712 | tf_op jit(solution)/shard_map/xu,uk->xk/dot_general | solution.py:77
  49.4 1.1 %reshape_reshape.7 = f32[16,8,32,6]{0,3,2,1:T(8,128)} reshape(f32[16,1536]{0,1:T(8,128)S(1)} %fusion.36) | data formatting | bytes 196608 | tf_op jit(solution)/shard_map/reshape;reshape | solution.py:103
  50.5 4.7 %convolution_bitcast_fusion = f32[12,16,8,32]{0,1,3,2:T(8,128)S(1)} fusion(f32[16,8,32,6]{0,3,2,1:T(8,128)} %reshape_reshape.7, f32[12,6]{0,1:T(8,128)S(1)} %copy-done.4), kind=kOutput, calls=%fused_computation.5 | convolution fusion | flops 3538944 | bytes 295200 | tf_op jit(solution)/shard_map/xyrs,vs->vxyr/dot_general | solution.py:104
  55.2 2.1 %copy.61 = f32[12,16,8,32]{3,2,1,0:T(8,128)} copy(f32[12,16,8,32]{0,1,3,2:T(8,128)S(1)} %convolution_bitcast_fusion) | data formatting | bytes 393216 | tf_op jit(solution)/shard_map/xyrs,vs->vxyr/dot_general | solution.py:104
  57.3 1.9 %fusion.42 = f32[12,16,8,128]{3,2,1,0:T(8,128)S(1)} fusion(f32[12,16,8,32]{3,2,1,0:T(8,128)} %copy.61, f32[128,32]{0,1:T(8,128)S(1)} %copy-done), kind=kOutput, calls=%fused_computation.59 | convolution fusion | flops 75497472 | bytes 999424 | tf_op jit(solution)/shard_map/vxyr,zr->vxyz/dot_general | solution.py:105
  59.2 0.0 copy-start.1
  59.2 0.7 fusion.24
  59.9 0.1 pad_maximum_fusion.4
  60.0 0.6 broadcast_in_dim.16
  60.6 6.5 %all-to-all-start = ((f32[32,1,24]{2,1,0:T(1,128)}), f32[32,1,24]{2,1,0:T(1,128)S(1)}, u32[]{:S(2)}, u32[]{:S(2)}) async-start(f32[32,1,24]{2,1,0:T(1,128)} %broadcast_in_dim.16), calls=%async_computation | async-start | bytes 32768 | tf_op jit(solution)/shard_map/all_to_all | solution.py:87
  67.1 1.1 %copy.64 = f32[12,16,8,128]{3,2,1,0:T(8,128)} copy(f32[12,16,8,128]{3,0,2,1:T(8,128)S(1)} %fusion.22) | data formatting | bytes 1572864
  68.2 0.0 copy-done.1
  68.2 6.0 %all-to-all-done = f32[32,1,24]{2,1,0:T(1,128)S(1)} async-done(((f32[32,1,24]{2,1,0:T(1,128)}), f32[32,1,24]{2,1,0:T(1,128)S(1)}, u32[]{:S(2)}, u32[]{:S(2)}) %all-to-all-start) | async-done | bytes 3104 | tf_op jit(solution)/shard_map/all_to_all | solution.py:87
  74.3 0.1 reduce_sum.29
  74.3 0.6 fusion.51
  (16 shorter events, 0.1 us)
Async XLA Ops:
  0.6 29.8 %copy-start = (f32[128,32]{0,1:T(8,128)S(1)}, f32[128,32]{0,1:T(8,128)}, u32[]{:S(2)}) copy-start(f32[128,32]{0,1:T(8,128)} %param.15) | copy-start | bytes 49156
  0.6 17.8 %copy-start.2 = (f32[12,16,8,128]{3,2,1,0:T(8,128)S(1)}, f32[12,16,8,128]{3,2,1,0:T(8,128)}, u32[]{:S(2)}) copy-start(f32[12,16,8,128]{3,2,1,0:T(8,128)} %param.9) | copy-start | bytes 2359300
  0.7 8.1 %copy-start.6 = (f32[12]{0:T(128)S(1)}, f32[12]{0:T(128)}, u32[]{:S(2)}) copy-start(f32[12]{0:T(128)} %param.12) | copy-start | bytes 148
  2.4 16.1 %collective-permute-start = (f32[12,16,2,128]{3,0,2,1:T(8,128)S(1)}, f32[12,16,2,128]{3,0,2,1:T(8,128)S(1)}, u32[]{:S(2)}, u32[]{:S(2)}) collective-permute-start(f32[12,16,2,128]{3,0,2,1:T(8,128)S(1)} %copy.83), channel_id=1, source_target_pairs={{0,1},{1,2},{2,3},{3,4},{4,5},{5,6},{6,7},{8,9},{9,10},{10,11},{11... | collective-permute-start | bytes 589832 | tf_op jit(solution)/shard_map/ppermute | solution.py:16
  7.4 11.5 %collective-permute-start.1 = (f32[12,16,2,128]{3,0,2,1:T(8,128)S(1)}, f32[12,16,2,128]{3,0,2,1:T(8,128)S(1)}, u32[]{:S(2)}, u32[]{:S(2)}) collective-permute-start(f32[12,16,2,128]{3,0,2,1:T(8,128)S(1)} %copy.84), channel_id=1, source_target_pairs={{1,0},{2,1},{3,2},{4,3},{5,4},{6,5},{7,6},{9,8},{10,9},{11,10},{12... | collective-permute-start | bytes 589832 | tf_op jit(solution)/shard_map/ppermute | solution.py:17
  19.1 2.7 %collective-permute-start.2 = (f32[12,2,12,128]{3,0,2,1:T(8,128)S(1)}, f32[12,2,12,128]{3,0,2,1:T(8,128)S(1)}, u32[]{:S(2)}, u32[]{:S(2)}) collective-permute-start(f32[12,2,12,128]{3,0,2,1:T(8,128)S(1)} %get-tuple-element.20), channel_id=1, source_target_pairs={{0,8},{8,16},{16,24},{1,9},{9,17},{17,25},{2,10},{10,18},{18,26},{... | collective-permute-start | bytes 442376 | tf_op jit(solution)/shard_map/ppermute | solution.py:16
  20.4 5.1 %collective-permute-start.3 = (f32[12,2,12,128]{3,0,2,1:T(8,128)S(1)}, f32[12,2,12,128]{3,0,2,1:T(8,128)S(1)}, u32[]{:S(2)}, u32[]{:S(2)}) collective-permute-start(f32[12,2,12,128]{3,0,2,1:T(8,128)S(1)} %get-tuple-element.21), channel_id=1, source_target_pairs={{8,0},{16,8},{24,16},{9,1},{17,9},{25,17},{10,2},{18,10},{26,18},{... | collective-permute-start | bytes 442376 | tf_op jit(solution)/shard_map/ppermute | solution.py:17
  21.7 4.0 %copy-start.5 = (f32[12,12]{1,0:T(8,128)S(1)}, f32[12,12]{1,0:T(8,128)}, u32[]{:S(2)}) copy-start(f32[12,12]{1,0:T(8,128)} %param.13) | copy-start | bytes 1732
  21.7 4.0 %copy-start.7 = (f32[12]{0:T(128)S(1)}, f32[12]{0:T(128)}, u32[]{:S(2)}) copy-start(f32[12]{0:T(128)} %param.11) | copy-start | bytes 148
  21.7 4.0 %copy-start.8 = (f32[12]{0:T(128)S(1)}, f32[12]{0:T(128)}, u32[]{:S(2)}) copy-start(f32[12]{0:T(128)} %param.10) | copy-start | bytes 148
  32.3 2.3 %copy-start.4 = (f32[12,6]{0,1:T(8,128)S(1)}, f32[12,6]{0,1:T(8,128)}, u32[]{:S(2)}) copy-start(f32[12,6]{0,1:T(8,128)} %param.16) | copy-start | bytes 868
  37.0 1.6 %copy-start.3 = (f32[16,64]{1,0:T(8,128)S(1)}, f32[16,64]{1,0:T(8,128)}, u32[]{:S(2)}) copy-start(f32[16,64]{1,0:T(8,128)} %param.14) | copy-start | bytes 12292
  59.2 9.0 %copy-start.1 = (f32[12,16,8,128]{3,2,1,0:T(8,128)}, f32[12,16,8,128]{3,2,1,0:T(8,128)S(1)}, u32[]{:S(2)}) copy-start(f32[12,16,8,128]{3,2,1,0:T(8,128)S(1)} %fusion.42) | copy-start | bytes 2359300
  60.6 13.7 %all-to-all-start = ((f32[32,1,24]{2,1,0:T(1,128)}), f32[32,1,24]{2,1,0:T(1,128)S(1)}, u32[]{:S(2)}, u32[]{:S(2)}) async-start(f32[32,1,24]{2,1,0:T(1,128)} %broadcast_in_dim.16), calls=%async_computation | async-start | bytes 32768 | tf_op jit(solution)/shard_map/all_to_all | solution.py:87

commit v2 on v0

v2 whole, which is shorter than its diff:
```python
import functools

import jax
import jax.numpy as jnp
from jax import lax
from jax.experimental import pallas as pl
from jax.experimental.pallas import tpu as pltpu
from jax.sharding import PartitionSpec as P

HIGH = lax.Precision.HIGHEST
VM = pl.BlockSpec(memory_space=pltpu.VMEM)
SM = pl.BlockSpec(memory_space=pltpu.SMEM)


def call(kernel, outs, in_specs, name, scratch=(), flops=10**7):
    return pl.pallas_call(
        kernel,
        out_shape=[jax.ShapeDtypeStruct(s, d) for s, d in outs],
        in_specs=in_specs,
        out_specs=[VM] * len(outs),
        scratch_shapes=list(scratch),
        name=name,
        cost_estimate=pl.CostEstimate(flops=flops, bytes_accessed=10**6, transcendentals=0),
    )


def split(a):
    hi = a.astype(jnp.bfloat16)
    lo = (a - hi.astype(jnp.float32)).astype(jnp.bfloat16)
    return hi, lo


def mm(a, b, nt=False):
    dims = (((1,), (1 if nt else 0,)), ((), ()))
    return lax.dot_general(a, b, dims, preferred_element_type=jnp.float32)


def mm3(a, b, nt=False):
    return mm(a[0], b[0], nt) + mm(a[0], b[1], nt) + mm(a[1], b[0], nt)


def place(shape, dim):
    return lax.broadcasted_iota(jnp.int32, shape, dim)


def shifted(w, axis, before=0.0, after=0.0):
    size = w.shape[axis]
    pos = place(w.shape, axis)
    low = jnp.where(pos == 0, before, pltpu.roll(w, 1, axis))
    high = jnp.where(pos == size - 1, after, pltpu.roll(w, size - 1, axis))
    return low + high


def reaction(ws, pre, act, mix):
    n = len(ws)
    cold = -1.0 / (1.5 + jnp.tanh(ws[0]))
    rates = [pre[v] * jnp.exp(act[v] * cold) * ws[v] for v in range(n)]
    outs = []
    for v in range(n):
        total = mix[v, 0] * rates[0]
        for u in range(1, n):
            total = total + mix[v, u] * rates[u]
        outs.append(total)
    return outs


def stage(ref, base_of, nv, rows_x, rows_y, coeffs, emit, low_edge=None, high_edge=None, step=4):
    dif, pre, act, mix = coeffs
    lanes = ref.shape[1]

    def rows(v, x, n):
        return ref[pl.ds(base_of(v, x), n * rows_y), :].reshape(n, rows_y, lanes)

    step = min(step, rows_x)
    for x in range(0, rows_x, step):
        ws = [rows(v, x, step) for v in range(nv)]
        made = reaction(ws, pre, act, mix)
        for v in range(nv):
            w = ws[v]
            if x > 0:
                first = rows(v, x - 1, 1)
            else:
                first = low_edge(v) if low_edge else jnp.zeros((1, rows_y, lanes), jnp.float32)
            if x + step < rows_x:
                last = rows(v, x + step, 1)
            else:
                last = high_edge(v) if high_edge else jnp.zeros((1, rows_y, lanes), jnp.float32)
            if step > 1:
                beside = jnp.concatenate([first, w[:-1]], 0) + jnp.concatenate([w[1:], last], 0)
            else:
                beside = first + last
            lap = beside + shifted(w, 1) + shifted(w, 2) - 6.0 * w
            emit(v, x, step, w, dif[v] * lap + made[v])


def pack_kernel(dims, f_ref, p1, p2, q1, q2):
    nv, rows_x, rows_y, lanes = dims
    odd_x = lax.axis_index("gx") % 2 == 1
    odd_y = lax.axis_index("gy") % 2 == 1
    size = rows_x * rows_y
    for layer in range(2):
        for v in range(nv):
            low = f_ref[pl.ds(v * size + layer, rows_x, stride=rows_y), :]
            high = f_ref[pl.ds(v * size + rows_y - 1 - layer, rows_x, stride=rows_y), :]
            at = pl.ds((layer * nv + v) * rows_x, rows_x)
            p1[at, :] = jnp.where(odd_y, low, high)
            p2[at, :] = jnp.where(odd_y, high, low)
            low = f_ref[pl.ds(v * size + layer * rows_y, rows_y), :]
            high = f_ref[pl.ds(v * size + (rows_x - 1 - layer) * rows_y, rows_y), :]
            at = pl.ds((layer * nv + v) * rows_y, rows_y)
            q1[at, :] = jnp.where(odd_x, low, high)
            q2[at, :] = jnp.where(odd_x, high, low)


def corner_kernel(dims, x1, x2, c1, c2):
    nv, rows_x, rows_y, lanes = dims
    odd_x = lax.axis_index("gx") % 2 == 1
    odd_y = lax.axis_index("gy") % 2 == 1
    for side in range(2):
        for out, swap in ((c1, False), (c2, True)):
            a_low = x1[pl.ds(0, nv, stride=rows_y), :]
            a_high = x1[pl.ds(rows_y - 1, nv, stride=rows_y), :]
            b_low = x2[pl.ds(0, nv, stride=rows_y), :]
            b_high = x2[pl.ds(rows_y - 1, nv, stride=rows_y), :]
            take_one = odd_x if side == 0 else jnp.logical_not(odd_x)
            low = jnp.where(take_one, a_low, b_low)
            high = jnp.where(take_one, a_high, b_high)
            send_low = jnp.logical_not(odd_y) if swap else odd_y
            out[pl.ds(side * nv, nv), :] = jnp.where(send_low, low, high)


def first_kernel(dims, f_ref, bz_ref, bv_ref, dif, pre, act, mix, s_ref, kh, kl, th, tl):
    nv, rows_x, rows_y, lanes = dims
    size = rows_x * rows_y

    def emit(v, x, n, w, t):
        s_ref[pl.ds(v * size + x * rows_y, n * rows_y), :] = (w + t).reshape(n * rows_y, lanes)

    stage(f_ref, lambda v, x: v * size + x * rows_y, nv, rows_x, rows_y, (dif, pre, act, mix), emit)
    bz, bv = bz_ref[...], bv_ref[...]
    rank_z, rank_v = bz.shape[1], bv.shape[1]
    width = rank_z * rank_v
    pick_z = (place((rank_z, width), 1) % rank_z == place((rank_z, width), 0)).astype(jnp.float32)
    pick_v = (place((rank_v, width), 1) // rank_z == place((rank_v, width), 0)).astype(jnp.float32)
    wide_z = jnp.dot(bz, pick_z, precision=HIGH, preferred_element_type=jnp.float32)
    wide_v = jnp.dot(bv, pick_v, precision=HIGH, preferred_element_type=jnp.float32)
    for v in range(nv):
        both = wide_z * wide_v[v : v + 1, :]
        kh[pl.ds(v * lanes, lanes), :], kl[pl.ds(v * lanes, lanes), :] = split(both)
        turned = both.T
        th[:, v * lanes : (v + 1) * lanes], tl[:, v * lanes : (v + 1) * lanes] = split(turned)


def second_kernel(
    dims, f_ref, s_ref, y1, y2, x1, x2, c1, c2, bx_ref, kh, kl, dif, pre, act, mix,
    state_ref, m_ref, sec, gy_ref, gx_ref,
):
    nv, rows_x, rows_y, lanes = dims
    size = rows_x * rows_y
    ix, iy = lax.axis_index("gx"), lax.axis_index("gy")
    odd_x, odd_y = ix % 2 == 1, iy % 2 == 1
    has_x = (ix > 0, ix < lax.axis_size("gx") - 1)
    has_y = (iy > 0, iy < lax.axis_size("gy") - 1)

    def two(one, other, odd, at):
        a, b = one[at, :], other[at, :]
        return jnp.where(odd, a, b), jnp.where(odd, b, a)

    def y_ghost(layer, v):
        return two(y1, y2, odd_y, pl.ds((layer * nv + v) * rows_x, rows_x))

    def x_ghost(layer, v):
        return two(x1, x2, odd_x, pl.ds((layer * nv + v) * rows_y, rows_y))

    def corner(side, v):
        return two(c1, c2, odd_y, pl.ds(side * nv + v, 1))

    def keep(value, flags):
        side = place(value.shape, 0)
        inside = jnp.where(side == 0, flags[0].astype(jnp.int32), flags[1].astype(jnp.int32))
        return jnp.where(inside == 1, value, 0.0)

    gs = [jnp.stack(y_ghost(0, v)) for v in range(nv)]
    made = reaction(gs, pre, act, mix)
    for v in range(nv):
        g = gs[v]
        low = f_ref[pl.ds(v * size, rows_x, stride=rows_y), :]
        high = f_ref[pl.ds(v * size + rows_y - 1, rows_x, stride=rows_y), :]
        before = jnp.stack(corner(0, v))
        after = jnp.stack(corner(1, v))
        lap = jnp.stack(y_ghost(1, v)) + jnp.stack([low, high])
        lap = lap + shifted(g, 1, before, after) + shifted(g, 2) - 6.0 * g
        out = keep(g + (dif[v] * lap + made[v]), has_y)
        gy_ref[pl.ds(v * 2 * rows_x, 2 * rows_x), :] = out.reshape(2 * rows_x, lanes)
        sec[pl.ds(v * size, size), :] = s_ref[pl.ds(v * size, size), :]
        at = pl.ds(v * size, rows_x, stride=rows_y)
        sec[at, :] = sec[at, :] + dif[v] * g[0]
        at = pl.ds(v * size + rows_y - 1, rows_x, stride=rows_y)
        sec[at, :] = sec[at, :] + dif[v] * g[1]
    gs = [jnp.stack(x_ghost(0, v)) for v in range(nv)]
    made = reaction(gs, pre, act, mix)
    for v in range(nv):
        g = gs[v]
        low = f_ref[pl.ds(v * size, rows_y), :]
        high = f_ref[pl.ds(v * size + size - rows_y, rows_y), :]
        left, right = corner(0, v), corner(1, v)
        before = jnp.stack([left[0], right[0]])
        after = jnp.stack([left[1], right[1]])
        lap = jnp.stack(x_ghost(1, v)) + jnp.stack([low, high])
        lap = lap + shifted(g, 1, before, after) + shifted(g, 2) - 6.0 * g
        out = keep(g + (dif[v] * lap + made[v]), has_x)
        gx_ref[pl.ds(v * 2 * rows_y, 2 * rows_y), :] = out.reshape(2 * rows_y, lanes)
        at = pl.ds(v * size, rows_y)
        sec[at, :] = sec[at, :] + dif[v] * g[0]
        at = pl.ds(v * size + size - rows_y, rows_y)
        sec[at, :] = sec[at, :] + dif[v] * g[1]

    def emit(v, x, n, w, t):
        at = pl.ds(v * size + x * rows_y, n * rows_y)
        state_ref[at, :] = 0.5 * ((f_ref[at, :] + w.reshape(n * rows_y, lanes)) + t.reshape(n * rows_y, lanes))

    stage(
        sec, lambda v, x: v * size + x * rows_y, nv, rows_x, rows_y, (dif, pre, act, mix), emit,
        lambda v: gx_ref[pl.ds(v * 2 * rows_y, rows_y), :][None],
        lambda v: gx_ref[pl.ds((v * 2 + 1) * rows_y, rows_y), :][None],
    )
    total = None
    for v in range(nv):
        half = 0.5 * dif[v]
        at = pl.ds(v * size, rows_x, stride=rows_y)
        state_ref[at, :] = state_ref[at, :] + half * gy_ref[pl.ds(v * 2 * rows_x, rows_x), :]
        at = pl.ds(v * size + rows_y - 1, rows_x, stride=rows_y)
        state_ref[at, :] = state_ref[at, :] + half * gy_ref[pl.ds((v * 2 + 1) * rows_x, rows_x), :]
        at = pl.ds(v * lanes, lanes)
        part = mm3(split(state_ref[pl.ds(v * size, size), :]), (kh[at, :], kl[at, :]))
        total = part if total is None else total + part
    bx = bx_ref[...]
    repeated = jnp.broadcast_to(bx[:, None, :], (rows_x, rows_y, bx.shape[1])).reshape(size, bx.shape[1])
    m_ref[...] = jnp.concatenate([total, repeated], axis=1)


def mix_blocks(rows_y, width, blocks):
    own = blocks[0][:, width:]
    size = own.shape[0]
    same = place((size, size), 0) % rows_y == place((size, size), 1) % rows_y
    total = None
    for block in blocks:
        link = lax.dot_general(
            own, block[:, width:], (((1,), (1,)), ((), ())), precision=HIGH, preferred_element_type=jnp.float32
        )
        part = mm3(split(jnp.where(same, link, 0.0)), split(block[:, :width]))
        total = part if total is None else total + part
    return total


def decode_into(decoded, state_ref, th, tl, mass_ref, recon_ref, sums_ref, nv, size, lanes):
    halves = split(decoded)
    sums = mass_ref[...]
    spot = place(sums.shape, 1)
    for v in range(nv):
        cols = slice(v * lanes, (v + 1) * lanes)
        recon = mm3(halves, (th[:, cols], tl[:, cols]))
        at = pl.ds(v * size, size)
        recon_ref[at, :] = recon
        error = state_ref[at, :] - recon
        sums = jnp.where(spot == v, jnp.sum(error * error), sums)
    sums_ref[...] = jnp.broadcast_to(sums, sums_ref.shape)


def third_kernel(dims, width, n, *refs):
    nv, rows_x, rows_y, lanes = dims
    blocks = [ref[...] for ref in refs[:n]]
    state_ref, th, tl, mass_ref, recon_ref, sums_ref = refs[n:]
    decoded = mix_blocks(rows_y, width, blocks)
    decode_into(decoded, state_ref, th, tl, mass_ref, recon_ref, sums_ref, nv, rows_x * rows_y, lanes)


def mix_kernel(rows_y, width, n, *refs):
    refs[n][...] = mix_blocks(rows_y, width, [ref[...] for ref in refs[:n]])


def decode_kernel(dims, d_ref, state_ref, th, tl, mass_ref, recon_ref, sums_ref):
    nv, rows_x, rows_y, lanes = dims
    decode_into(d_ref[...], state_ref, th, tl, mass_ref, recon_ref, sums_ref, nv, rows_x * rows_y, lanes)


def mass_kernel(dims, state_ref, out_ref):
    nv, rows_x, rows_y, lanes = dims
    size = rows_x * rows_y
    spot = place(out_ref.shape, 1)
    sums = jnp.zeros(out_ref.shape, jnp.float32)
    for v in range(nv):
        w = state_ref[pl.ds(v * size, size), :]
        sums = jnp.where(spot == nv + v, jnp.sum(w * w), sums)
    out_ref[...] = sums


def pairs(n, first):
    swaps = [(i, i + 1) for i in range(first, n - 1, 2)]
    return swaps + [(j, i) for i, j in swaps]


def gather_blocks(block):
    n = lax.axis_size("gx")
    if n & (n - 1):
        every = lax.all_gather(block, "gx", axis=0)
        return [block] + [jnp.roll(every, -lax.axis_index("gx"), 0)[i] for i in range(1, n)]
    blocks = [block]
    bit = n // 2
    while bit:
        swaps = [(i, i ^ bit) for i in range(n)]
        blocks = blocks + [lax.ppermute(b, "gx", swaps) for b in blocks]
        bit //= 2
    return blocks


def on_device(field, diffusion, prefactor, activation, mixing, basis_x, basis_y, basis_z, basis_v):
    f32, bf16 = jnp.float32, jnp.bfloat16
    dims = field.shape
    nv, rows_x, rows_y, lanes = dims
    size = rows_x * rows_y
    rank_z, rank_v = basis_z.shape[1], basis_v.shape[1]
    width = rank_z * rank_v
    gx, gy = lax.axis_size("gx"), lax.axis_size("gy")
    peers = gx * gy
    coeffs = (diffusion, prefactor, activation, mixing)
    flat = field.reshape(nv * size, lanes)

    y_msg, x_msg = (2 * nv * rows_x, lanes), (2 * nv * rows_y, lanes)
    p1, p2, q1, q2 = call(
        functools.partial(pack_kernel, dims), [(y_msg, f32)] * 2 + [(x_msg, f32)] * 2, [VM], "pack"
    )(flat)
    y1 = lax.ppermute(p1, "gy", pairs(gy, 0))
    y2 = lax.ppermute(p2, "gy", pairs(gy, 1))
    x1 = lax.ppermute(q1, "gx", pairs(gx, 0))
    x2 = lax.ppermute(q2, "gx", pairs(gx, 1))
    c1, c2 = call(
        functools.partial(corner_kernel, dims), [((2 * nv, lanes), f32)] * 2, [VM] * 2, "corner"
    )(x1, x2)
    c1 = lax.ppermute(c1, "gy", pairs(gy, 0))
    c2 = lax.ppermute(c2, "gy", pairs(gy, 1))

    section, kh, kl, th, tl = call(
        functools.partial(first_kernel, dims),
        [((nv * size, lanes), f32)] + [((nv * lanes, width), bf16)] * 2 + [((width, nv * lanes), bf16)] * 2,
        [VM] * 3 + [SM] * 4,
        "first",
    )(flat, basis_z, basis_v, *coeffs)
    state, message = call(
        functools.partial(second_kernel, dims),
        [((nv * size, lanes), f32), ((size, width + basis_x.shape[1]), f32)],
        [VM] * 11 + [SM] * 4,
        "second",
        [
            pltpu.VMEM((nv * size, lanes), f32),
            pltpu.VMEM((nv * 2 * rows_x, lanes), f32),
            pltpu.VMEM((nv * 2 * rows_y, lanes), f32),
        ],
    )(flat, section, y1, y2, x1, x2, c1, c2, basis_x, kh, kl, *coeffs)
    blocks = gather_blocks(message)
    (mass_row,) = call(functools.partial(mass_kernel, dims), [((1, lanes), f32)], [VM], "mass")(state)
    outs = [((nv * size, lanes), f32), ((peers, lanes), f32)]
    if basis_y.shape[0] * gy == basis_y.shape[1]:
        recon, sums = call(
            functools.partial(third_kernel, dims, width, len(blocks)), outs, [VM] * (len(blocks) + 4), "third"
        )(*blocks, state, th, tl, mass_row)
    else:
        (mixed,) = call(
            functools.partial(mix_kernel, rows_y, width, len(blocks)), [((size, width), f32)], [VM] * len(blocks), "mixed"
        )(*blocks)
        mixed = mixed.reshape(rows_x, rows_y, width)
        core = lax.psum(jnp.einsum("xyk,yb->xbk", mixed, basis_y, precision=HIGH), "gy")
        mixed = jnp.einsum("xbk,yb->xyk", core, basis_y, precision=HIGH).reshape(size, width)
        recon, sums = call(functools.partial(decode_kernel, dims), outs, [VM] * 5, "decode")(
            mixed, state, th, tl, mass_row
        )
    if peers > 64:
        sums = lax.psum(sums[0], ("gx", "gy"))
    else:
        sums = jnp.sum(lax.all_to_all(sums, ("gx", "gy"), 0, 0, tiled=True), axis=0)
    residual = jnp.sqrt(sums[:nv] / (sums[nv : 2 * nv] + 1e-06))
    return (state.reshape(dims), recon.reshape(dims), residual)


def solution(mesh):
    return jax.shard_map(
        on_device,
        mesh=mesh,
        in_specs=(
            P(None, "gx", "gy", None),
            P(),
            P(),
            P(),
            P(),
            P("gx", None),
            P("gy", None),
            P(),
            P(),
        ),
        out_specs=(P(None, "gx", "gy", None), P(None, "gx", "gy", None), P()),
        check_vma=False,
    )
```

time: 209 us -> 58.5 us (0.28)
  waiting for transfers between devices: 118 us -> 5.16 us
  blocking collectives: 46.3 us -> 13.2 us
  Pallas kernels: 0 us -> 19.5 us
  matrix products: 15.1 us -> 0 us
  between operations: 14.4 us -> 0.76 us
  starting transfers between devices: 8.51 us -> 14.8 us
    psum x1 -> x0, waiting for transfers between devices: 77.8 us -> none  [on_device(): core_block = lax.psum(core_block, 'gy')]
    psum x1 -> x0, blocking collectives: 38.9 us -> none  [on_device(): miss, mass = lax.psum((miss_local, mass_local), ('gx', 'gy'))]
    reduce_scatter x1 -> x0, waiting for transfers between devices: 27.8 us -> none  [on_device(): lax.psum_scatter(jnp.einsum('xa,xyk->ayk', columns, packed, precision=HIG...]
    pallas_call x0 -> x6, Pallas kernels: none -> 19.5 us  [the longest x1 5.06 us: on_device(): call(functools.partial(second_kernel, dims), [((nv * size, lanes), f32),...]
    dot_general x10 -> x0, matrix products: 15.1 us -> none  [the longest x2 4.55 us: reaction(): return jnp.einsum('vw,wxyz->vxyz', mixing, rate_terms, precision=HIGH)]
    all_to_all x0 -> x1, blocking collectives: none -> 13.2 us  [on_device(): sums = jnp.sum(lax.all_to_all(sums, ('gx', 'gy'), 0, 0, tiled=True), axis=0)]
    all_gather x1 -> x0, blocking collectives: 7.32 us -> none  [on_device(): lax.all_gather(mixed_y, 'gx', axis=0, tiled=True)]
    ppermute x4 -> x9, waiting for transfers between devices: 12.2 us -> 5.16 us  [the longest x3 4.33 us: gather_blocks(): blocks = blocks + [lax.ppermute(b, 'gx', swaps) for b in blocks]]
  transfers between devices with their start and end apart: 6 -> 9, of which waited for: 5 -> 2; matrix products, arithmetic and copies ran while one was open for 1% -> 2% of each run, Pallas kernels for 0% -> 14%
where the time goes in v2:
time: 58.5 us; the launch traced here: 58.2 us
  Pallas kernels  19.5 us (33%)
  starting transfers between devices  14.8 us (25%)
  blocking collectives  13.2 us (23%)
  waiting for transfers between devices  5.16 us (9%)
  local copies, waits for them, and re-layouts  4.08 us (7%)
  between operations  0.76 us (1%)
  other arithmetic  0.65 us (1%)
    all_to_all x1, blocking collectives, on_device(): sums = jnp.sum(lax.all_to_all(sums, ('gx', 'gy'), 0, 0, tiled=True), axis=0)  13.2 us
    ppermute x3, starting transfers between devices, gather_blocks(): blocks = blocks + [lax.ppermute(b, 'gx', swaps) for b in blocks]  5.51 us
    pallas_call x1, Pallas kernels, on_device(): call(functools.partial(second_kernel, dims), [((nv * size, lanes), f32),...  5.06 us
    pallas_call x1, Pallas kernels, on_device(): call(functools.partial(third_kernel, dims, width, len(blocks)), outs, [VM...  4.56 us
    pallas_call x1, Pallas kernels, on_device(): call(functools.partial(first_kernel, dims), [((nv * size, lanes), f32)] +...  4.44 us
    ppermute x3, waiting for transfers between devices, gather_blocks(): blocks = blocks + [lax.ppermute(b, 'gx', swaps) for b in blocks]  4.33 us
    ppermute x1, starting transfers between devices, on_device(): c1 = lax.ppermute(c1, 'gy', pairs(gy, 0))  4.27 us
    unnamed x24, local copies, waits for them, and re-layouts  4.08 us
  transfers between devices with their start and end apart: 9, of which 2 were waited for; matrix products, arithmetic and copies ran while one was open for 2% of the time, Pallas kernels for 14%

profile of v2, /device:TPU:0, one launch (start us, length us, event | category | flops | bytes accessed | tf_op | source)
XLA Modules:
  0.0 58.2 jit_solution(4794610730947534650)
XLA Ops:
  0.6 2.0 %pack.1 = (f32[384,128]{1,0:T(8,128)}, f32[384,128]{1,0:T(8,128)}, f32[192,128]{1,0:T(8,128)}, f32[192,128]{1,0:T(8,128)}) custom-call(f32[1536,128]{1,0:T(8,128)} %bitcast.6), custom_call_target="tpu_custom_call" | custom-call | flops 10000000 | bytes 1000000 | tf_op jit(solution)/shard_map/pack/pallas_call | solution.py:330
  2.6 3.0 %collective-permute-start = (f32[384,128]{1,0:T(8,128)}, f32[384,128]{1,0:T(8,128)S(1)}, u32[]{:S(2)}, u32[]{:S(2)}) collective-permute-start(f32[384,128]{1,0:T(8,128)} %get-tuple-element.19), channel_id=1, source_target_pairs={{0,1},{2,3},{4,5},{6,7},{1,0},{3,2},{5,4},{7,6},{8,9},{10,11},{12,... | collective-permute-start | bytes 589832 | tf_op jit(solution)/shard_map/ppermute | solution.py:333
  5.6 0.7 %collective-permute-start.1 = (f32[384,128]{1,0:T(8,128)}, f32[384,128]{1,0:T(8,128)S(1)}, u32[]{:S(2)}, u32[]{:S(2)}) collective-permute-start(f32[384,128]{1,0:T(8,128)} %get-tuple-element.20), channel_id=1, source_target_pairs={{1,2},{3,4},{5,6},{2,1},{4,3},{6,5},{9,10},{11,12},{13,14},{10,9},... | collective-permute-start | bytes 589832 | tf_op jit(solution)/shard_map/ppermute | solution.py:334
  6.3 0.1 collective-permute-start.2
  6.4 0.7 %collective-permute-start.3 = (f32[192,128]{1,0:T(8,128)}, f32[192,128]{1,0:T(8,128)S(1)}, u32[]{:S(2)}, u32[]{:S(2)}) collective-permute-start(f32[192,128]{1,0:T(8,128)} %get-tuple-element.22), channel_id=1, source_target_pairs={{8,16},{16,8},{9,17},{17,9},{10,18},{18,10},{11,19},{19,11},{12,20... | collective-permute-start | bytes 294920 | tf_op jit(solution)/shard_map/ppermute | solution.py:336
  7.0 0.8 %collective-permute-done.2.x1 = f32[192,128]{1,0:T(8,128)S(1)} collective-permute-done((f32[192,128]{1,0:T(8,128)}, f32[192,128]{1,0:T(8,128)S(1)}, u32[]{:S(2)}, u32[]{:S(2)}) %collective-permute-start.2) | collective-permute-done | bytes 98336 | tf_op jit(solution)/shard_map/ppermute | solution.py:335
  7.9 0.0 copy-start
  7.9 0.0 collective-permute-done.3.x2
  7.9 0.6 %copy-done = f32[192,128]{1,0:T(8,128)} copy-done((f32[192,128]{1,0:T(8,128)}, f32[192,128]{1,0:T(8,128)S(1)}, u32[]{:S(2)}) %copy-start) | copy-done | bytes 98328
  8.5 0.0 copy-start.1
  8.5 0.6 %copy-done.1 = f32[192,128]{1,0:T(8,128)} copy-done((f32[192,128]{1,0:T(8,128)}, f32[192,128]{1,0:T(8,128)S(1)}, u32[]{:S(2)}) %copy-start.1) | copy-done | bytes 98328
  9.1 0.0 copy-start.10
  9.2 0.0 copy-start.7
  9.2 1.6 %corner.1 = (f32[24,128]{1,0:T(8,128)}, f32[24,128]{1,0:T(8,128)}) custom-call(f32[192,128]{1,0:T(8,128)} %copy-done, f32[192,128]{1,0:T(8,128)} %copy-done.1), custom_call_target="tpu_custom_call" | custom-call | flops 10000000 | bytes 1000000 | tf_op jit(solution)/shard_map/corner/pallas_call | solution.py:337
  10.7 4.3 %collective-permute-start.4 = (f32[24,128]{1,0:T(8,128)}, f32[24,128]{1,0:T(8,128)S(1)}, u32[]{:S(2)}, u32[]{:S(2)}) collective-permute-start(f32[24,128]{1,0:T(8,128)} %get-tuple-element.23), channel_id=1, source_target_pairs={{0,1},{2,3},{4,5},{6,7},{1,0},{3,2},{5,4},{7,6},{8,9},{10,11},{12,... | collective-permute-start | bytes 36872 | tf_op jit(solution)/shard_map/ppermute | solution.py:340
  15.0 0.7 %collective-permute-start.5 = (f32[24,128]{1,0:T(8,128)}, f32[24,128]{1,0:T(8,128)S(1)}, u32[]{:S(2)}, u32[]{:S(2)}) collective-permute-start(f32[24,128]{1,0:T(8,128)} %get-tuple-element.24), channel_id=1, source_target_pairs={{1,2},{3,4},{5,6},{2,1},{4,3},{6,5},{9,10},{11,12},{13,14},{10,9},... | collective-permute-start | bytes 36872 | tf_op jit(solution)/shard_map/ppermute | solution.py:341
  15.7 0.0 copy-done.10
  15.7 0.7 %copy.14.bv_ref = f32[12,6]{1,0:T(8,128)} copy(f32[12,6]{0,1:T(8,128)S(1)} %copy-done.10) | data formatting | bytes 576 | tf_op args[8]
  16.4 0.0 copy-done.7
  16.4 0.7 %copy.13.bz_ref = f32[128,32]{1,0:T(8,128)} copy(f32[128,32]{0,1:T(8,128)S(1)} %copy-done.7) | data formatting | bytes 32768 | tf_op args[7]
  17.1 4.4 %first.1 = (f32[1536,128]{1,0:T(8,128)}, bf16[1536,192]{1,0:T(8,128)(2,1)}, bf16[1536,192]{1,0:T(8,128)(2,1)}, bf16[192,1536]{1,0:T(8,128)(2,1)}, bf16[192,1536]{1,0:T(8,128)(2,1)}) custom-call(f32[1536,128]{1,0:T(8,128)} %bitcast.7, f32[128,32]{1,0:T(8,128)} %copy.13.bz_ref, f32[12,6]{1,0:T(8,128)} %copy.14.bv_ref, f32[12]{0:T(128)} %dif.3, f32[12]{0:T(128)} %pre.3, ...), custom_call_target="tpu_custom_call" | custom-call | flops 10000000 | bytes 1000000 | tf_op jit(solution)/shard_map/first/pallas_call | solution.py:343
  21.5 0.0 collective-permute-done.4.c1
  21.5 0.0 collective-permute-done.5.c2
  21.5 0.0 copy-start.9
  21.5 0.0 collective-permute-done.y1
  21.6 0.0 copy-start.2
  21.6 0.0 collective-permute-done.1.y2
  21.6 0.0 copy-start.3
  21.6 0.5 copy-done.8
  22.1 0.0 copy-done.9
  22.1 0.1 copy-done.2
  22.2 0.1 copy-done.3
  22.3 5.1 %second.1 = (f32[1536,128]{1,0:T(8,128)}, f32[128,256]{1,0:T(8,128)}) custom-call(f32[1536,128]{1,0:T(8,128)} %bitcast.8, f32[1536,128]{1,0:T(8,128)} %get-tuple-element.18.s_ref, f32[384,128]{1,0:T(8,128)} %copy-done.2, f32[384,128]{1,0:T(8,128)} %copy-done.3, f32[192,128]{1,0:T(8,128)} %copy-done, f32[192,128]{1,0:T(8,128)} %copy-done.1, ...), custom_call_target="tpu_custom_call" | custom-call | flops 10000000 | bytes 1000000 | tf_op jit(solution)/shard_map/second/pallas_call | solution.py:349
  27.4 5.5 %collective-permute-start.6 = (f32[128,256]{1,0:T(8,128)}, f32[128,256]{1,0:T(8,128)S(1)}, u32[]{:S(2)}, u32[]{:S(2)}) collective-permute-start(f32[128,256]{1,0:T(8,128)} %get-tuple-element.28.refs_0_), channel_id=1, source_target_pairs={{0,16},{8,24},{16,0},{24,8},{1,17},{9,25},{17,1},{25,9},{2,18},{10... | collective-permute-start | bytes 393224 | tf_op jit(solution)/shard_map/ppermute | solution.py:312
  32.9 0.0 collective-permute-start.7
  32.9 4.3 %collective-permute-done.6.refs_1_ = f32[128,256]{1,0:T(8,128)S(1)} collective-permute-done((f32[128,256]{1,0:T(8,128)}, f32[128,256]{1,0:T(8,128)S(1)}, u32[]{:S(2)}, u32[]{:S(2)}) %collective-permute-start.6) | collective-permute-done | bytes 131104 | tf_op jit(solution)/shard_map/ppermute | solution.py:312
  37.2 0.0 collective-permute-start.8
  37.2 1.9 %mass.1.refs_7_ = f32[1,128]{1,0:T(1,128)} custom-call(f32[1536,128]{1,0:T(8,128)} %get-tuple-element.27.state_ref.refs_4_), custom_call_target="tpu_custom_call" | custom-call | flops 10000000 | bytes 1000000 | tf_op jit(solution)/shard_map/mass/pallas_call | solution.py:361
  39.1 0.0 copy-done.4
  39.1 0.0 collective-permute-done.7.refs_2_
  39.1 0.0 collective-permute-done.8.refs_3_
  39.1 0.0 copy-start.6
  39.1 0.6 %copy-done.5 = f32[128,256]{1,0:T(8,128)} copy-done((f32[128,256]{1,0:T(8,128)}, f32[128,256]{1,0:T(8,128)S(1)}, u32[]{:S(2)}) %copy-start.5) | copy-done | bytes 131096
  39.7 0.1 copy-done.6
  39.8 4.6 %third.1 = (f32[1536,128]{1,0:T(8,128)}, f32[32,128]{1,0:T(8,128)}) custom-call(f32[128,256]{1,0:T(8,128)} %get-tuple-element.28.refs_0_, f32[128,256]{1,0:T(8,128)} %copy-done.4, f32[128,256]{1,0:T(8,128)} %copy-done.5, f32[128,256]{1,0:T(8,128)} %copy-done.6, f32[1536,128]{1,0:T(8,128)} %get-tuple-element.27.state_ref.refs_4_, ...), custom_call_target="tpu_custom_call" | custom-call | flops 10000000 | bytes 1000000 | tf_op jit(solution)/shard_map/third/pallas_call | solution.py:364
  44.3 13.2 %all_to_all.9 = f32[32,1,128]{2,1,0:T(1,128)S(1)} all-to-all(f32[32,1,128]{2,1,0:T(1,128)} %bitcast.10), channel_id=1, replica_groups=mesh['gx'=4,'gy'=8] {'gx','gy'}, dimensions={0} | all-to-all | bytes 32768 | tf_op jit(solution)/shard_map/all_to_all | solution.py:380
  57.5 0.1 reduce_sum.9
  57.6 0.6 %fusion = f32[12]{0:T(128)} fusion(f32[128]{0:T(128)S(1)} %reduce_sum.9), kind=kLoop, calls=%fused_computation.1 | loop fusion | flops 24 | bytes 144 | tf_op jit(solution)/shard_map/sqrt | solution.py:381
  (3 shorter events, 0.0 us)
Async XLA Ops:
  2.6 18.9 %collective-permute-start = (f32[384,128]{1,0:T(8,128)}, f32[384,128]{1,0:T(8,128)S(1)}, u32[]{:S(2)}, u32[]{:S(2)}) collective-permute-start(f32[384,128]{1,0:T(8,128)} %get-tuple-element.19), channel_id=1, source_target_pairs={{0,1},{2,3},{4,5},{6,7},{1,0},{3,2},{5,4},{7,6},{8,9},{10,11},{12,... | collective-permute-start | bytes 589832 | tf_op jit(solution)/shard_map/ppermute | solution.py:333
  5.6 15.9 %collective-permute-start.1 = (f32[384,128]{1,0:T(8,128)}, f32[384,128]{1,0:T(8,128)S(1)}, u32[]{:S(2)}, u32[]{:S(2)}) collective-permute-start(f32[384,128]{1,0:T(8,128)} %get-tuple-element.20), channel_id=1, source_target_pairs={{1,2},{3,4},{5,6},{2,1},{4,3},{6,5},{9,10},{11,12},{13,14},{10,9},... | collective-permute-start | bytes 589832 | tf_op jit(solution)/shard_map/ppermute | solution.py:334
  6.3 1.6 %collective-permute-start.2 = (f32[192,128]{1,0:T(8,128)}, f32[192,128]{1,0:T(8,128)S(1)}, u32[]{:S(2)}, u32[]{:S(2)}) collective-permute-start(f32[192,128]{1,0:T(8,128)} %get-tuple-element.21), channel_id=1, source_target_pairs={{0,8},{16,24},{8,0},{24,16},{1,9},{17,25},{9,1},{25,17},{2,10},{18... | collective-permute-start | bytes 294920 | tf_op jit(solution)/shard_map/ppermute | solution.py:335
  6.4 1.5 %collective-permute-start.3 = (f32[192,128]{1,0:T(8,128)}, f32[192,128]{1,0:T(8,128)S(1)}, u32[]{:S(2)}, u32[]{:S(2)}) collective-permute-start(f32[192,128]{1,0:T(8,128)} %get-tuple-element.22), channel_id=1, source_target_pairs={{8,16},{16,8},{9,17},{17,9},{10,18},{18,10},{11,19},{19,11},{12,20... | collective-permute-start | bytes 294920 | tf_op jit(solution)/shard_map/ppermute | solution.py:336
  7.9 0.6 %copy-start = (f32[192,128]{1,0:T(8,128)}, f32[192,128]{1,0:T(8,128)S(1)}, u32[]{:S(2)}) copy-start(f32[192,128]{1,0:T(8,128)S(1)} %collective-permute-done.2.x1) | copy-start | bytes 294916
  8.5 0.6 %copy-start.1 = (f32[192,128]{1,0:T(8,128)}, f32[192,128]{1,0:T(8,128)S(1)}, u32[]{:S(2)}) copy-start(f32[192,128]{1,0:T(8,128)S(1)} %collective-permute-done.3.x2) | copy-start | bytes 294916
  9.1 6.5 %copy-start.10 = (f32[12,6]{0,1:T(8,128)S(1)}, f32[12,6]{0,1:T(8,128)}, u32[]{:S(2)}) copy-start(f32[12,6]{0,1:T(8,128)} %param.16) | copy-start | bytes 868
  9.2 7.2 %copy-start.7 = (f32[128,32]{0,1:T(8,128)S(1)}, f32[128,32]{0,1:T(8,128)}, u32[]{:S(2)}) copy-start(f32[128,32]{0,1:T(8,128)} %param.15) | copy-start | bytes 49156
  10.7 10.8 %collective-permute-start.4 = (f32[24,128]{1,0:T(8,128)}, f32[24,128]{1,0:T(8,128)S(1)}, u32[]{:S(2)}, u32[]{:S(2)}) collective-permute-start(f32[24,128]{1,0:T(8,128)} %get-tuple-element.23), channel_id=1, source_target_pairs={{0,1},{2,3},{4,5},{6,7},{1,0},{3,2},{5,4},{7,6},{8,9},{10,11},{12,... | collective-permute-start | bytes 36872 | tf_op jit(solution)/shard_map/ppermute | solution.py:340
  15.0 6.5 %collective-permute-start.5 = (f32[24,128]{1,0:T(8,128)}, f32[24,128]{1,0:T(8,128)S(1)}, u32[]{:S(2)}, u32[]{:S(2)}) collective-permute-start(f32[24,128]{1,0:T(8,128)} %get-tuple-element.24), channel_id=1, source_target_pairs={{1,2},{3,4},{5,6},{2,1},{4,3},{6,5},{9,10},{11,12},{13,14},{10,9},... | collective-permute-start | bytes 36872 | tf_op jit(solution)/shard_map/ppermute | solution.py:341
  21.5 0.6 %copy-start.8 = (f32[24,128]{1,0:T(8,128)}, f32[24,128]{1,0:T(8,128)S(1)}, u32[]{:S(2)}) copy-start(f32[24,128]{1,0:T(8,128)S(1)} %collective-permute-done.4.c1) | copy-start | bytes 36868
  21.5 0.6 %copy-start.9 = (f32[24,128]{1,0:T(8,128)}, f32[24,128]{1,0:T(8,128)S(1)}, u32[]{:S(2)}) copy-start(f32[24,128]{1,0:T(8,128)S(1)} %collective-permute-done.5.c2) | copy-start | bytes 36868
  21.6 0.7 %copy-start.2 = (f32[384,128]{1,0:T(8,128)}, f32[384,128]{1,0:T(8,128)S(1)}, u32[]{:S(2)}) copy-start(f32[384,128]{1,0:T(8,128)S(1)} %collective-permute-done.y1) | copy-start | bytes 589828
  21.6 0.7 %copy-start.3 = (f32[384,128]{1,0:T(8,128)}, f32[384,128]{1,0:T(8,128)S(1)}, u32[]{:S(2)}) copy-start(f32[384,128]{1,0:T(8,128)S(1)} %collective-permute-done.1.y2) | copy-start | bytes 589828
  27.4 9.8 %collective-permute-start.6 = (f32[128,256]{1,0:T(8,128)}, f32[128,256]{1,0:T(8,128)S(1)}, u32[]{:S(2)}, u32[]{:S(2)}) collective-permute-start(f32[128,256]{1,0:T(8,128)} %get-tuple-element.28.refs_0_), channel_id=1, source_target_pairs={{0,16},{8,24},{16,0},{24,8},{1,17},{9,25},{17,1},{25,9},{2,18},{10... | collective-permute-start | bytes 393224 | tf_op jit(solution)/shard_map/ppermute | solution.py:312
  32.9 6.2 %collective-permute-start.7 = (f32[128,256]{1,0:T(8,128)}, f32[128,256]{1,0:T(8,128)S(1)}, u32[]{:S(2)}, u32[]{:S(2)}) collective-permute-start(f32[128,256]{1,0:T(8,128)} %get-tuple-element.28.refs_0_), channel_id=1, source_target_pairs={{0,8},{8,0},{16,24},{24,16},{1,9},{9,1},{17,25},{25,17},{2,10},{10... | collective-permute-start | bytes 393224 | tf_op jit(solution)/shard_map/ppermute | solution.py:312
  37.2 1.9 %copy-start.4 = (f32[128,256]{1,0:T(8,128)}, f32[128,256]{1,0:T(8,128)S(1)}, u32[]{:S(2)}) copy-start(f32[128,256]{1,0:T(8,128)S(1)} %collective-permute-done.6.refs_1_) | copy-start | bytes 393220
  37.2 1.9 %collective-permute-start.8 = (f32[128,256]{1,0:T(8,128)S(1)}, f32[128,256]{1,0:T(8,128)S(1)}, u32[]{:S(2)}, u32[]{:S(2)}) collective-permute-start(f32[128,256]{1,0:T(8,128)S(1)} %collective-permute-done.6.refs_1_), channel_id=1, source_target_pairs={{0,8},{8,0},{16,24},{24,16},{1,9},{9,1},{17,25},{25,17},{2,10},{10... | collective-permute-start | bytes 393224 | tf_op jit(solution)/shard_map/ppermute | solution.py:312
  39.1 0.6 %copy-start.5 = (f32[128,256]{1,0:T(8,128)}, f32[128,256]{1,0:T(8,128)S(1)}, u32[]{:S(2)}) copy-start(f32[128,256]{1,0:T(8,128)S(1)} %collective-permute-done.7.refs_2_) | copy-start | bytes 393220
  39.1 0.7 %copy-start.6 = (f32[128,256]{1,0:T(8,128)}, f32[128,256]{1,0:T(8,128)S(1)}, u32[]{:S(2)}) copy-start(f32[128,256]{1,0:T(8,128)S(1)} %collective-permute-done.8.refs_3_) | copy-start | bytes 393220

commit v3 on v2

--- a/solution.py
+++ b/solution.py
@@ -12,7 +12,7 @@
 SM = pl.BlockSpec(memory_space=pltpu.SMEM)
 
 
-def call(kernel, outs, in_specs, name, scratch=(), flops=10**7):
+def call(kernel, outs, in_specs, name, scratch=(), flops=10**7, vmem=12):
     return pl.pallas_call(
         kernel,
         out_shape=[jax.ShapeDtypeStruct(s, d) for s, d in outs],
@@ -20,6 +20,7 @@
         out_specs=[VM] * len(outs),
         scratch_shapes=list(scratch),
         name=name,
+        compiler_params=pltpu.CompilerParams(vmem_limit_bytes=vmem << 20),
         cost_estimate=pl.CostEstimate(flops=flops, bytes_accessed=10**6, transcendentals=0),
     )
 
@@ -138,12 +139,13 @@
 
     stage(f_ref, lambda v, x: v * size + x * rows_y, nv, rows_x, rows_y, (dif, pre, act, mix), emit)
     bz, bv = bz_ref[...], bv_ref[...]
-    rank_z, rank_v = bz.shape[1], bv.shape[1]
+    rank_z, rank_v = bz.shape[0], bv.shape[0]
     width = rank_z * rank_v
     pick_z = (place((rank_z, width), 1) % rank_z == place((rank_z, width), 0)).astype(jnp.float32)
     pick_v = (place((rank_v, width), 1) // rank_z == place((rank_v, width), 0)).astype(jnp.float32)
-    wide_z = jnp.dot(bz, pick_z, precision=HIGH, preferred_element_type=jnp.float32)
-    wide_v = jnp.dot(bv, pick_v, precision=HIGH, preferred_element_type=jnp.float32)
+    first = (((0,), (0,)), ((), ()))
+    wide_z = lax.dot_general(bz, pick_z, first, precision=HIGH, preferred_element_type=jnp.float32)
+    wide_v = lax.dot_general(bv, pick_v, first, precision=HIGH, preferred_element_type=jnp.float32)
     for v in range(nv):
         both = wide_z * wide_v[v : v + 1, :]
         kh[pl.ds(v * lanes, lanes), :], kl[pl.ds(v * lanes, lanes), :] = split(both)
@@ -345,7 +347,7 @@
         [((nv * size, lanes), f32)] + [((nv * lanes, width), bf16)] * 2 + [((width, nv * lanes), bf16)] * 2,
         [VM] * 3 + [SM] * 4,
         "first",
-    )(flat, basis_z, basis_v, *coeffs)
+    )(flat, basis_z.T, basis_v.T, *coeffs)
     state, message = call(
         functools.partial(second_kernel, dims),
         [((nv * size, lanes), f32), ((size, width + basis_x.shape[1]), f32)],

time: 58.5 us -> 48.8 us (0.83)
  Pallas kernels: 19.5 us -> 9.76 us
  starting transfers between devices: 14.8 us -> 15.6 us
    pallas_call x1, Pallas kernels: 2 us -> 0.08 us  [on_device(): call(functools.partial(pack_kernel, dims), [(y_msg, f32)] * 2 + [(x_msg,...]
    pallas_call x1, Pallas kernels: 4.44 us -> 2.73 us  [on_device(): call(functools.partial(first_kernel, dims), [((nv * size, lanes), f32)] +...]
    pallas_call x1, Pallas kernels: 4.56 us -> 2.86 us  [on_device(): call(functools.partial(third_kernel, dims, width, len(blocks)), outs, [VM...]
    pallas_call x1, Pallas kernels: 1.87 us -> 0.18 us  [on_device(): call(functools.partial(mass_kernel, dims), [((1, lanes), f32)], [VM], 'ma...]
    pallas_call x1, Pallas kernels: 1.58 us -> 0.02 us  [on_device(): call(functools.partial(corner_kernel, dims), [((2 * nv, lanes), f32)] * 2...]
    pallas_call x1, Pallas kernels: 5.06 us -> 3.9 us  [on_device(): call(functools.partial(second_kernel, dims), [((nv * size, lanes), f32),...]
    ppermute x3, starting transfers between devices: 5.51 us -> 6.14 us  [gather_blocks(): blocks = blocks + [lax.ppermute(b, 'gx', swaps) for b in blocks]]
    unnamed x24 -> x22, local copies, waits for them, and re-layouts: 4.08 us -> 3.83 us
  transfers between devices with their start and end apart: 9 -> 9, of which waited for: 2 -> 2; matrix products, arithmetic and copies ran while one was open for 2% -> 0% of each run, Pallas kernels for 14% -> 6%
where the time goes in v3:
time: 48.8 us; the launch traced here: 48.4 us
  starting transfers between devices  15.6 us (32%)
  blocking collectives  13 us (27%)
  Pallas kernels  9.76 us (20%)
  waiting for transfers between devices  4.75 us (10%)
  local copies, waits for them, and re-layouts  3.83 us (8%)
  between operations  0.82 us (2%)
  other arithmetic  0.65 us (1%)
    all_to_all x1, blocking collectives, on_device(): sums = jnp.sum(lax.all_to_all(sums, ('gx', 'gy'), 0, 0, tiled=True), axis=0)  13 us
    ppermute x3, starting transfers between devices, gather_blocks(): blocks = blocks + [lax.ppermute(b, 'gx', swaps) for b in blocks]  6.14 us
    ppermute x1, starting transfers between devices, on_device(): c1 = lax.ppermute(c1, 'gy', pairs(gy, 0))  4.34 us
    ppermute x3, waiting for transfers between devices, gather_blocks(): blocks = blocks + [lax.ppermute(b, 'gx', swaps) for b in blocks]  4.13 us
    pallas_call x1, Pallas kernels, on_device(): call(functools.partial(second_kernel, dims), [((nv * size, lanes), f32),...  3.9 us
    unnamed x22, local copies, waits for them, and re-layouts  3.83 us
    ppermute x1, starting transfers between devices, on_device(): y1 = lax.ppermute(p1, 'gy', pairs(gy, 0))  3.06 us
    pallas_call x1, Pallas kernels, on_device(): call(functools.partial(third_kernel, dims, width, len(blocks)), outs, [VM...  2.86 us
  transfers between devices with their start and end apart: 9, of which 2 were waited for; matrix products, arithmetic and copies ran while one was open for 0% of the time, Pallas kernels for 6%

profile of v3, /device:TPU:0, one launch (start us, length us, event | category | flops | bytes accessed | tf_op | source)
XLA Modules:
  0.0 48.4 jit_solution(9925222360494331575)
XLA Ops:
  0.6 0.0 copy-start
  0.6 1.1 %copy-done = f32[12,16,8,128]{3,2,1,0:T(8,128)S(1)} copy-done((f32[12,16,8,128]{3,2,1,0:T(8,128)S(1)}, f32[12,16,8,128]{3,2,1,0:T(8,128)}, u32[]{:S(2)}) %copy-start) | copy-done | bytes 786456
  1.8 0.0 copy-start.1
  1.8 0.1 pack.1
  1.9 3.1 %collective-permute-start = (f32[384,128]{1,0:T(8,128)S(1)}, f32[384,128]{1,0:T(8,128)S(1)}, u32[]{:S(2)}, u32[]{:S(2)}) collective-permute-start(f32[384,128]{1,0:T(8,128)S(1)} %get-tuple-element.19), channel_id=1, source_target_pairs={{0,1},{2,3},{4,5},{6,7},{1,0},{3,2},{5,4},{7,6},{8,9},{10,11},{12,... | collective-permute-start | bytes 589832 | tf_op jit(solution)/shard_map/ppermute | solution.py:335
  4.9 0.7 %collective-permute-start.1 = (f32[384,128]{1,0:T(8,128)S(1)}, f32[384,128]{1,0:T(8,128)S(1)}, u32[]{:S(2)}, u32[]{:S(2)}) collective-permute-start(f32[384,128]{1,0:T(8,128)S(1)} %get-tuple-element.20), channel_id=1, source_target_pairs={{1,2},{3,4},{5,6},{2,1},{4,3},{6,5},{9,10},{11,12},{13,14},{10,9},... | collective-permute-start | bytes 589832 | tf_op jit(solution)/shard_map/ppermute | solution.py:336
  5.6 0.1 collective-permute-start.2
  5.7 0.7 %collective-permute-start.3 = (f32[192,128]{1,0:T(8,128)S(1)}, f32[192,128]{1,0:T(8,128)S(1)}, u32[]{:S(2)}, u32[]{:S(2)}) collective-permute-start(f32[192,128]{1,0:T(8,128)S(1)} %get-tuple-element.22), channel_id=1, source_target_pairs={{8,16},{16,8},{9,17},{17,9},{10,18},{18,10},{11,19},{19,11},{12,20... | collective-permute-start | bytes 294920 | tf_op jit(solution)/shard_map/ppermute | solution.py:338
  6.3 0.6 %collective-permute-done.2.x1 = f32[192,128]{1,0:T(8,128)S(1)} collective-permute-done((f32[192,128]{1,0:T(8,128)S(1)}, f32[192,128]{1,0:T(8,128)S(1)}, u32[]{:S(2)}, u32[]{:S(2)}) %collective-permute-start.2) | collective-permute-done | bytes 98336 | tf_op jit(solution)/shard_map/ppermute | solution.py:337
  6.9 0.0 collective-permute-done.3.x2
  7.0 0.0 copy-start.4
  7.0 0.0 copy-start.5
  7.0 0.0 copy-start.7
  7.0 4.3 %collective-permute-start.4 = (f32[24,128]{1,0:T(8,128)S(1)}, f32[24,128]{1,0:T(8,128)S(1)}, u32[]{:S(2)}, u32[]{:S(2)}) collective-permute-start(f32[24,128]{1,0:T(8,128)S(1)} %get-tuple-element.23), channel_id=1, source_target_pairs={{0,1},{2,3},{4,5},{6,7},{1,0},{3,2},{5,4},{7,6},{8,9},{10,11},{12,... | collective-permute-start | bytes 36872 | tf_op jit(solution)/shard_map/ppermute | solution.py:342
  11.3 0.7 %collective-permute-start.5 = (f32[24,128]{1,0:T(8,128)S(1)}, f32[24,128]{1,0:T(8,128)S(1)}, u32[]{:S(2)}, u32[]{:S(2)}) collective-permute-start(f32[24,128]{1,0:T(8,128)S(1)} %get-tuple-element.24), channel_id=1, source_target_pairs={{1,2},{3,4},{5,6},{2,1},{4,3},{6,5},{9,10},{11,12},{13,14},{10,9},... | collective-permute-start | bytes 36872 | tf_op jit(solution)/shard_map/ppermute | solution.py:343
  12.0 0.0 copy-start.8
  12.0 0.0 copy-start.9
  12.0 0.0 copy-start.10
  12.0 0.0 copy-done.1
  12.0 0.0 copy-done.4
  12.0 0.0 copy-done.5
  12.1 0.0 copy-done.7
  12.1 0.6 %copy-done.8 = f32[12]{0:T(128)S(1)} copy-done((f32[12]{0:T(128)S(1)}, f32[12]{0:T(128)}, u32[]{:S(2)}) %copy-start.8) | copy-done | bytes 72
  12.7 0.0 copy-done.9
  12.7 0.0 copy-done.10
  12.7 0.0 copy-start.6
  12.7 2.7 %first.1 = (f32[1536,128]{1,0:T(8,128)S(1)}, bf16[1536,192]{1,0:T(8,128)(2,1)S(1)}, bf16[1536,192]{1,0:T(8,128)(2,1)S(1)}, bf16[192,1536]{1,0:T(8,128)(2,1)S(1)}, bf16[192,1536]{1,0:T(8,128)(2,1)S(1)}) custom-call(f32[1536,128]{1,0:T(8,128)S(1)} %bitcast.9, f32[32,128]{1,0:T(8,128)S(1)} %bitcast.12, f32[6,12]{1,0:T(8,128)S(1)} %bitcast.14, f32[12]{0:T(128)S(1)} %copy-done.8, ...), custom_call_target="tpu_custom_call" | custom-call | flops 10000000 | bytes 1000000 | tf_op jit(solution)/shard_map/first/pallas_call | solution.py:345
  15.4 0.0 collective-permute-done.4.c1
  15.4 0.0 collective-permute-done.5.c2
  15.4 0.0 collective-permute-done.y1
  15.4 0.0 collective-permute-done.1.y2
  15.5 0.0 copy-done.6
  15.5 3.9 %second.1 = (f32[1536,128]{1,0:T(8,128)}, f32[128,256]{1,0:T(8,128)S(1)}) custom-call(f32[1536,128]{1,0:T(8,128)S(1)} %bitcast.10, f32[1536,128]{1,0:T(8,128)S(1)} %get-tuple-element.18.s_ref, f32[384,128]{1,0:T(8,128)S(1)} %collective-permute-done.y1, f32[384,128]{1,0:T(8,128)S(1)} %collective-permute-done.1.y2, f32[192,128]{1,0:T(8,128)S(1)} %collective-permute-done.2.x1, ...), custom_call_target="tpu_custom_call" | custom-call | flops 10000000 | bytes 1000000 | tf_op jit(solution)/shard_map/second/pallas_call | solution.py:351
  19.4 6.1 %collective-permute-start.6 = (f32[128,256]{1,0:T(8,128)S(1)}, f32[128,256]{1,0:T(8,128)S(1)}, u32[]{:S(2)}, u32[]{:S(2)}) collective-permute-start(f32[128,256]{1,0:T(8,128)S(1)} %get-tuple-element.28.refs_0_), channel_id=1, source_target_pairs={{0,16},{8,24},{16,0},{24,8},{1,17},{9,25},{17,1},{25,9},{2,18},{10... | collective-permute-start | bytes 393224 | tf_op jit(solution)/shard_map/ppermute | solution.py:314
  25.5 0.0 collective-permute-start.7
  25.5 4.1 %collective-permute-done.6.refs_1_ = f32[128,256]{1,0:T(8,128)S(1)} collective-permute-done((f32[128,256]{1,0:T(8,128)S(1)}, f32[128,256]{1,0:T(8,128)S(1)}, u32[]{:S(2)}, u32[]{:S(2)}) %collective-permute-start.6) | collective-permute-done | bytes 131104 | tf_op jit(solution)/shard_map/ppermute | solution.py:314
  29.6 0.0 collective-permute-start.8
  29.6 0.0 copy-start.2
  29.6 1.1 %copy-done.2 = f32[1536,128]{1,0:T(8,128)S(1)} copy-done((f32[1536,128]{1,0:T(8,128)S(1)}, f32[1536,128]{1,0:T(8,128)}, u32[]{:S(2)}) %copy-start.2) | copy-done | bytes 786456
  30.8 0.0 copy-start.3
  30.8 0.2 mass.1.refs_7_
  30.9 0.0 collective-permute-done.7.refs_2_
  31.0 0.0 collective-permute-done.8.refs_3_
  31.0 0.9 %copy-done.3 = f32[1536,128]{1,0:T(8,128)S(1)} copy-done((f32[1536,128]{1,0:T(8,128)S(1)}, f32[1536,128]{1,0:T(8,128)}, u32[]{:S(2)}) %copy-start.3) | copy-done | bytes 786456
  31.9 2.9 %third.1 = (f32[1536,128]{1,0:T(8,128)}, f32[32,128]{1,0:T(8,128)S(1)}) custom-call(f32[128,256]{1,0:T(8,128)S(1)} %get-tuple-element.28.refs_0_, f32[128,256]{1,0:T(8,128)S(1)} %collective-permute-done.6.refs_1_, f32[128,256]{1,0:T(8,128)S(1)} %collective-permute-done.7.refs_2_, f32[128,256]{1,0:T(8,128)S(1)} %collective-permute-done.8.refs_3_, ...), custom_call_target="tpu_custom_call" | custom-call | flops 10000000 | bytes 1000000 | tf_op jit(solution)/shard_map/third/pallas_call | solution.py:366
  34.7 13.0 %all_to_all.9 = f32[32,1,128]{2,1,0:T(1,128)S(1)} all-to-all(f32[32,1,128]{2,1,0:T(1,128)S(1)} %bitcast.13), channel_id=1, replica_groups=mesh['gx'=4,'gy'=8] {'gx','gy'}, dimensions={0} | all-to-all | bytes 32768 | tf_op jit(solution)/shard_map/all_to_all | solution.py:382
  47.7 0.1 reduce_sum.9
  47.8 0.6 %fusion = f32[12]{0:T(128)} fusion(f32[128]{0:T(128)S(1)} %reduce_sum.9), kind=kLoop, calls=%fused_computation.1 | loop fusion | flops 24 | bytes 144 | tf_op jit(solution)/shard_map/sqrt | solution.py:383
  (1 shorter events, 0.0 us)
Async XLA Ops:
  0.6 1.1 %copy-start = (f32[12,16,8,128]{3,2,1,0:T(8,128)S(1)}, f32[12,16,8,128]{3,2,1,0:T(8,128)}, u32[]{:S(2)}) copy-start(f32[12,16,8,128]{3,2,1,0:T(8,128)} %param.9) | copy-start | bytes 2359300
  1.8 10.3 %copy-start.1 = (f32[12,16,8,128]{3,2,1,0:T(8,128)S(1)}, f32[12,16,8,128]{3,2,1,0:T(8,128)}, u32[]{:S(2)}) copy-start(f32[12,16,8,128]{3,2,1,0:T(8,128)} %param.9) | copy-start | bytes 2359300
  1.9 13.6 %collective-permute-start = (f32[384,128]{1,0:T(8,128)S(1)}, f32[384,128]{1,0:T(8,128)S(1)}, u32[]{:S(2)}, u32[]{:S(2)}) collective-permute-start(f32[384,128]{1,0:T(8,128)S(1)} %get-tuple-element.19), channel_id=1, source_target_pairs={{0,1},{2,3},{4,5},{6,7},{1,0},{3,2},{5,4},{7,6},{8,9},{10,11},{12,... | collective-permute-start | bytes 589832 | tf_op jit(solution)/shard_map/ppermute | solution.py:335
  4.9 10.5 %collective-permute-start.1 = (f32[384,128]{1,0:T(8,128)S(1)}, f32[384,128]{1,0:T(8,128)S(1)}, u32[]{:S(2)}, u32[]{:S(2)}) collective-permute-start(f32[384,128]{1,0:T(8,128)S(1)} %get-tuple-element.20), channel_id=1, source_target_pairs={{1,2},{3,4},{5,6},{2,1},{4,3},{6,5},{9,10},{11,12},{13,14},{10,9},... | collective-permute-start | bytes 589832 | tf_op jit(solution)/shard_map/ppermute | solution.py:336
  5.6 1.4 %collective-permute-start.2 = (f32[192,128]{1,0:T(8,128)S(1)}, f32[192,128]{1,0:T(8,128)S(1)}, u32[]{:S(2)}, u32[]{:S(2)}) collective-permute-start(f32[192,128]{1,0:T(8,128)S(1)} %get-tuple-element.21), channel_id=1, source_target_pairs={{0,8},{16,24},{8,0},{24,16},{1,9},{17,25},{9,1},{25,17},{2,10},{18... | collective-permute-start | bytes 294920 | tf_op jit(solution)/shard_map/ppermute | solution.py:337
  5.7 1.3 %collective-permute-start.3 = (f32[192,128]{1,0:T(8,128)S(1)}, f32[192,128]{1,0:T(8,128)S(1)}, u32[]{:S(2)}, u32[]{:S(2)}) collective-permute-start(f32[192,128]{1,0:T(8,128)S(1)} %get-tuple-element.22), channel_id=1, source_target_pairs={{8,16},{16,8},{9,17},{17,9},{10,18},{18,10},{11,19},{19,11},{12,20... | collective-permute-start | bytes 294920 | tf_op jit(solution)/shard_map/ppermute | solution.py:338
  7.0 5.1 %copy-start.4 = (f32[12,12]{1,0:T(8,128)S(1)}, f32[12,12]{1,0:T(8,128)}, u32[]{:S(2)}) copy-start(f32[12,12]{1,0:T(8,128)} %mix.3) | copy-start | bytes 1732
  7.0 5.1 %copy-start.5 = (f32[128,32]{0,1:T(8,128)S(1)}, f32[128,32]{0,1:T(8,128)}, u32[]{:S(2)}) copy-start(f32[128,32]{0,1:T(8,128)} %param.15) | copy-start | bytes 49156
  7.0 5.1 %copy-start.7 = (f32[12,6]{0,1:T(8,128)S(1)}, f32[12,6]{0,1:T(8,128)}, u32[]{:S(2)}) copy-start(f32[12,6]{0,1:T(8,128)} %param.16) | copy-start | bytes 868
  7.0 8.4 %collective-permute-start.4 = (f32[24,128]{1,0:T(8,128)S(1)}, f32[24,128]{1,0:T(8,128)S(1)}, u32[]{:S(2)}, u32[]{:S(2)}) collective-permute-start(f32[24,128]{1,0:T(8,128)S(1)} %get-tuple-element.23), channel_id=1, source_target_pairs={{0,1},{2,3},{4,5},{6,7},{1,0},{3,2},{5,4},{7,6},{8,9},{10,11},{12,... | collective-permute-start | bytes 36872 | tf_op jit(solution)/shard_map/ppermute | solution.py:342
  11.3 4.1 %collective-permute-start.5 = (f32[24,128]{1,0:T(8,128)S(1)}, f32[24,128]{1,0:T(8,128)S(1)}, u32[]{:S(2)}, u32[]{:S(2)}) collective-permute-start(f32[24,128]{1,0:T(8,128)S(1)} %get-tuple-element.24), channel_id=1, source_target_pairs={{1,2},{3,4},{5,6},{2,1},{4,3},{6,5},{9,10},{11,12},{13,14},{10,9},... | collective-permute-start | bytes 36872 | tf_op jit(solution)/shard_map/ppermute | solution.py:343
  12.0 0.7 %copy-start.8 = (f32[12]{0:T(128)S(1)}, f32[12]{0:T(128)}, u32[]{:S(2)}) copy-start(f32[12]{0:T(128)} %dif.3) | copy-start | bytes 148
  12.0 0.7 %copy-start.9 = (f32[12]{0:T(128)S(1)}, f32[12]{0:T(128)}, u32[]{:S(2)}) copy-start(f32[12]{0:T(128)} %pre.3) | copy-start | bytes 148
  12.0 0.7 %copy-start.10 = (f32[12]{0:T(128)S(1)}, f32[12]{0:T(128)}, u32[]{:S(2)}) copy-start(f32[12]{0:T(128)} %act.3) | copy-start | bytes 148
  12.7 2.8 %copy-start.6 = (f32[16,64]{1,0:T(8,128)S(1)}, f32[16,64]{1,0:T(8,128)}, u32[]{:S(2)}) copy-start(f32[16,64]{1,0:T(8,128)} %bx_ref.1) | copy-start | bytes 12292
  19.4 10.3 %collective-permute-start.6 = (f32[128,256]{1,0:T(8,128)S(1)}, f32[128,256]{1,0:T(8,128)S(1)}, u32[]{:S(2)}, u32[]{:S(2)}) collective-permute-start(f32[128,256]{1,0:T(8,128)S(1)} %get-tuple-element.28.refs_0_), channel_id=1, source_target_pairs={{0,16},{8,24},{16,0},{24,8},{1,17},{9,25},{17,1},{25,9},{2,18},{10... | collective-permute-start | bytes 393224 | tf_op jit(solution)/shard_map/ppermute | solution.py:314
  25.5 5.5 %collective-permute-start.7 = (f32[128,256]{1,0:T(8,128)S(1)}, f32[128,256]{1,0:T(8,128)S(1)}, u32[]{:S(2)}, u32[]{:S(2)}) collective-permute-start(f32[128,256]{1,0:T(8,128)S(1)} %get-tuple-element.28.refs_0_), channel_id=1, source_target_pairs={{0,8},{8,0},{16,24},{24,16},{1,9},{9,1},{17,25},{25,17},{2,10},{10... | collective-permute-start | bytes 393224 | tf_op jit(solution)/shard_map/ppermute | solution.py:314
  29.6 1.3 %collective-permute-start.8 = (f32[128,256]{1,0:T(8,128)S(1)}, f32[128,256]{1,0:T(8,128)S(1)}, u32[]{:S(2)}, u32[]{:S(2)}) collective-permute-start(f32[128,256]{1,0:T(8,128)S(1)} %collective-permute-done.6.refs_1_), channel_id=1, source_target_pairs={{0,8},{8,0},{16,24},{24,16},{1,9},{9,1},{17,25},{25,17},{2,10},{10... | collective-permute-start | bytes 393224 | tf_op jit(solution)/shard_map/ppermute | solution.py:314
  29.6 1.1 %copy-start.2 = (f32[1536,128]{1,0:T(8,128)S(1)}, f32[1536,128]{1,0:T(8,128)}, u32[]{:S(2)}) copy-start(f32[1536,128]{1,0:T(8,128)} %get-tuple-element.27.state_ref.refs_4_) | copy-start | bytes 2359300
  30.8 1.1 %copy-start.3 = (f32[1536,128]{1,0:T(8,128)S(1)}, f32[1536,128]{1,0:T(8,128)}, u32[]{:S(2)}) copy-start(f32[1536,128]{1,0:T(8,128)} %get-tuple-element.27.state_ref.refs_4_) | copy-start | bytes 2359300

commit v4 on v3

--- a/solution.py
+++ b/solution.py
@@ -7,19 +7,19 @@
 from jax.experimental.pallas import tpu as pltpu
 from jax.sharding import PartitionSpec as P
 
+
 HIGH = lax.Precision.HIGHEST
 VM = pl.BlockSpec(memory_space=pltpu.VMEM)
 SM = pl.BlockSpec(memory_space=pltpu.SMEM)
 
 
-def call(kernel, outs, in_specs, name, scratch=(), flops=10**7, vmem=12):
+def call(kernel, outs, in_specs, scratch=(), flops=10**7, vmem=12):
     return pl.pallas_call(
         kernel,
         out_shape=[jax.ShapeDtypeStruct(s, d) for s, d in outs],
         in_specs=in_specs,
         out_specs=[VM] * len(outs),
         scratch_shapes=list(scratch),
-        name=name,
         compiler_params=pltpu.CompilerParams(vmem_limit_bytes=vmem << 20),
         cost_estimate=pl.CostEstimate(flops=flops, bytes_accessed=10**6, transcendentals=0),
     )
@@ -95,7 +95,7 @@
 
 
 def pack_kernel(dims, f_ref, p1, p2, q1, q2):
-    nv, rows_x, rows_y, lanes = dims
+    nv, rows_x, rows_y, _ = dims
     odd_x = lax.axis_index("gx") % 2 == 1
     odd_y = lax.axis_index("gy") % 2 == 1
     size = rows_x * rows_y
@@ -114,7 +114,7 @@
 
 
 def corner_kernel(dims, x1, x2, c1, c2):
-    nv, rows_x, rows_y, lanes = dims
+    nv, _, rows_y, _ = dims
     odd_x = lax.axis_index("gx") % 2 == 1
     odd_y = lax.axis_index("gy") % 2 == 1
     for side in range(2):
@@ -130,7 +130,7 @@
             out[pl.ds(side * nv, nv), :] = jnp.where(send_low, low, high)
 
 
-def first_kernel(dims, f_ref, bz_ref, bv_ref, dif, pre, act, mix, s_ref, kh, kl, th, tl):
+def first_kernel(dims, f_ref, bz_ref, bv_ref, dif, pre, act, mix, s_ref, kh, kl, th, tl, uh, ul):
     nv, rows_x, rows_y, lanes = dims
     size = rows_x * rows_y
 
@@ -151,6 +151,12 @@
         kh[pl.ds(v * lanes, lanes), :], kl[pl.ds(v * lanes, lanes), :] = split(both)
         turned = both.T
         th[:, v * lanes : (v + 1) * lanes], tl[:, v * lanes : (v + 1) * lanes] = split(turned)
+    part = nv * rank_z
+    pick_u = (place((nv, part), 1) // rank_z == place((nv, part), 0)).astype(jnp.float32)
+    tall = lax.dot_general(pick_v, bv, first, precision=HIGH, preferred_element_type=jnp.float32)
+    tall = jnp.dot(tall, pick_u, precision=HIGH, preferred_element_type=jnp.float32)
+    same = place((width, part), 0) % rank_z == place((width, part), 1) % rank_z
+    uh[...], ul[...] = split(jnp.where(same, tall, 0.0))
 
 
 def second_kernel(
@@ -236,65 +242,128 @@
         at = pl.ds(v * lanes, lanes)
         part = mm3(split(state_ref[pl.ds(v * size, size), :]), (kh[at, :], kl[at, :]))
         total = part if total is None else total + part
-    bx = bx_ref[...]
-    repeated = jnp.broadcast_to(bx[:, None, :], (rows_x, rows_y, bx.shape[1])).reshape(size, bx.shape[1])
-    m_ref[...] = jnp.concatenate([total, repeated], axis=1)
-
-
-def mix_blocks(rows_y, width, blocks):
-    own = blocks[0][:, width:]
-    size = own.shape[0]
+    pack_message(m_ref, total, bx_ref[...])
+
+
+def dense(size, width, rows_x, rank_x, lanes):
+    return width % lanes * 2 == lanes and rank_x * 2 == lanes and size % 16 == 0 and rows_x % 16 == 0
+
+
+def message_shape(size, width, rows_x, rank_x, lanes):
+    if not dense(size, width, rows_x, rank_x, lanes):
+        return (size + rows_x, max(width, rank_x))
+    return (size * (width // lanes) + size // 2 + rows_x // 2, lanes)
+
+
+def fold(a):
+    half = a.shape[0] // 2
+    return jnp.concatenate([a[:half], a[half:]], axis=1)
+
+
+def unfold(a):
+    half = a.shape[1] // 2
+    return jnp.concatenate([a[:, :half], a[:, half:]], axis=0)
+
+
+def pack_message(m_ref, values, basis):
+    size, width = values.shape
+    lanes = m_ref.shape[1]
+    if not dense(size, width, *basis.shape, lanes):
+        m_ref[:size, :width] = values
+        m_ref[size:, : basis.shape[1]] = basis
+        return
+    whole = width // lanes
+    for i in range(whole):
+        m_ref[pl.ds(i * size, size), :] = values[:, i * lanes : (i + 1) * lanes]
+    m_ref[pl.ds(whole * size, size // 2), :] = fold(values[:, whole * lanes :])
+    m_ref[pl.ds(whole * size + size // 2, basis.shape[0] // 2), :] = fold(basis)
+
+
+def unpack_message(m_ref, size, width, rows_x, rank_x):
+    lanes = m_ref.shape[1]
+    if not dense(size, width, rows_x, rank_x, lanes):
+        return m_ref[:size, :width], m_ref[size:, :rank_x]
+    whole = width // lanes
+    parts = [m_ref[pl.ds(i * size, size), :] for i in range(whole)]
+    parts.append(unfold(m_ref[pl.ds(whole * size, size // 2), :]))
+    basis = unfold(m_ref[pl.ds(whole * size + size // 2, rows_x // 2), :])
+    return jnp.concatenate(parts, axis=1), basis
+
+
+def mix_blocks(sizes, refs):
+    rows_x, rows_y, width, rank_x = sizes
+    size = rows_x * rows_y
     same = place((size, size), 0) % rows_y == place((size, size), 1) % rows_y
-    total = None
-    for block in blocks:
+
+    def repeated(basis):
+        return jnp.broadcast_to(basis[:, None, :], (rows_x, rows_y, rank_x)).reshape(size, rank_x)
+
+    own = total = None
+    for ref in refs:
+        values, basis = unpack_message(ref, size, width, rows_x, rank_x)
+        basis = repeated(basis)
+        own = basis if own is None else own
         link = lax.dot_general(
-            own, block[:, width:], (((1,), (1,)), ((), ())), precision=HIGH, preferred_element_type=jnp.float32
+            own, basis, (((1,), (1,)), ((), ())), precision=HIGH, preferred_element_type=jnp.float32
         )
-        part = mm3(split(jnp.where(same, link, 0.0)), split(block[:, :width]))
+        part = mm3(split(jnp.where(same, link, 0.0)), split(values))
         total = part if total is None else total + part
     return total
 
 
-def decode_into(decoded, state_ref, th, tl, mass_ref, recon_ref, sums_ref, nv, size, lanes):
-    halves = split(decoded)
-    sums = mass_ref[...]
-    spot = place(sums.shape, 1)
+def lane_sums(row, group, shift, lanes):
+    shape = (row.shape[1], lanes)
+    pick = (place(shape, 0) // group + shift == place(shape, 1)).astype(jnp.float32)
+    return jnp.dot(row, pick, precision=HIGH, preferred_element_type=jnp.float32)
+
+
+def side_kernel(dims, state_ref, bz_ref, w_ref, row_ref):
+    nv, rows_x, rows_y, lanes = dims
+    size = rows_x * rows_y
+    bz = split(bz_ref[...])
+    row = jnp.zeros(row_ref.shape, jnp.float32)
+    ones = jnp.ones((8, lanes), jnp.float32)
+    made = []
+    for v in range(nv):
+        state = state_ref[pl.ds(v * size, size), :]
+        part = mm3(split(state), bz, True)
+        made.append(part)
+        rest = state - mm3(split(part), bz)
+        outside = jnp.sum(rest * rest, axis=0, keepdims=True)
+        square = jnp.sum(state * state, axis=0, keepdims=True)
+        row = row + lane_sums(outside, lanes, v, lanes) + lane_sums(square, lanes, nv + v, lanes)
+    w_ref[...] = jnp.concatenate(made, axis=1)
+    row_ref[...] = row
+
+
+def settle(mixed, w_ref, row_ref, uh, ul, sums_ref, rank_z):
+    gap = w_ref[...] - mm3(split(mixed), (uh[...], ul[...]))
+    row = row_ref[...] + lane_sums(jnp.sum(gap * gap, axis=0, keepdims=True), rank_z, 0, row_ref.shape[1])
+    sums_ref[...] = jnp.broadcast_to(row, sums_ref.shape)
+
+
+def third_kernel(sizes, rank_z, n, *refs):
+    w_ref, row_ref, uh, ul, d_ref, sums_ref = refs[n:]
+    mixed = mix_blocks(sizes, refs[:n])
+    d_ref[...] = mixed
+    settle(mixed, w_ref, row_ref, uh, ul, sums_ref, rank_z)
+
+
+def mix_kernel(sizes, n, *refs):
+    refs[n][...] = mix_blocks(sizes, refs[:n])
+
+
+def settle_kernel(rank_z, d_ref, w_ref, row_ref, uh, ul, sums_ref):
+    settle(d_ref[...], w_ref, row_ref, uh, ul, sums_ref, rank_z)
+
+
+def decode_kernel(dims, d_ref, th, tl, recon_ref):
+    nv, rows_x, rows_y, lanes = dims
+    size = rows_x * rows_y
+    halves = split(d_ref[...])
     for v in range(nv):
         cols = slice(v * lanes, (v + 1) * lanes)
-        recon = mm3(halves, (th[:, cols], tl[:, cols]))
-        at = pl.ds(v * size, size)
-        recon_ref[at, :] = recon
-        error = state_ref[at, :] - recon
-        sums = jnp.where(spot == v, jnp.sum(error * error), sums)
-    sums_ref[...] = jnp.broadcast_to(sums, sums_ref.shape)
-
-
-def third_kernel(dims, width, n, *refs):
-    nv, rows_x, rows_y, lanes = dims
-    blocks = [ref[...] for ref in refs[:n]]
-    state_ref, th, tl, mass_ref, recon_ref, sums_ref = refs[n:]
-    decoded = mix_blocks(rows_y, width, blocks)
-    decode_into(decoded, state_ref, th, tl, mass_ref, recon_ref, sums_ref, nv, rows_x * rows_y, lanes)
-
-
-def mix_kernel(rows_y, width, n, *refs):
-    refs[n][...] = mix_blocks(rows_y, width, [ref[...] for ref in refs[:n]])
-
-
-def decode_kernel(dims, d_ref, state_ref, th, tl, mass_ref, recon_ref, sums_ref):
-    nv, rows_x, rows_y, lanes = dims
-    decode_into(d_ref[...], state_ref, th, tl, mass_ref, recon_ref, sums_ref, nv, rows_x * rows_y, lanes)
-
-
-def mass_kernel(dims, state_ref, out_ref):
-    nv, rows_x, rows_y, lanes = dims
-    size = rows_x * rows_y
-    spot = place(out_ref.shape, 1)
-    sums = jnp.zeros(out_ref.shape, jnp.float32)
-    for v in range(nv):
-        w = state_ref[pl.ds(v * size, size), :]
-        sums = jnp.where(spot == nv + v, jnp.sum(w * w), sums)
-    out_ref[...] = sums
+        recon_ref[pl.ds(v * size, size), :] = mm3(halves, (th[:, cols], tl[:, cols]))
 
 
 def pairs(n, first):
@@ -316,66 +385,71 @@
     return blocks
 
 
-def on_device(field, diffusion, prefactor, activation, mixing, basis_x, basis_y, basis_z, basis_v):
+def program(field, diffusion, prefactor, activation, mixing, basis_x, basis_y, basis_z, basis_v):
     f32, bf16 = jnp.float32, jnp.bfloat16
     dims = field.shape
     nv, rows_x, rows_y, lanes = dims
     size = rows_x * rows_y
-    rank_z, rank_v = basis_z.shape[1], basis_v.shape[1]
-    width = rank_z * rank_v
+    rank_x, rank_z, rank_v = basis_x.shape[1], basis_z.shape[1], basis_v.shape[1]
+    width, part = rank_z * rank_v, nv * rank_z
     gx, gy = lax.axis_size("gx"), lax.axis_size("gy")
     peers = gx * gy
     coeffs = (diffusion, prefactor, activation, mixing)
     flat = field.reshape(nv * size, lanes)
+    block = (nv * size, lanes)
 
     y_msg, x_msg = (2 * nv * rows_x, lanes), (2 * nv * rows_y, lanes)
     p1, p2, q1, q2 = call(
-        functools.partial(pack_kernel, dims), [(y_msg, f32)] * 2 + [(x_msg, f32)] * 2, [VM], "pack"
+        functools.partial(pack_kernel, dims), [(y_msg, f32)] * 2 + [(x_msg, f32)] * 2, [VM]
     )(flat)
+    x1 = lax.ppermute(q1, "gx", pairs(gx, 0))
+    x2 = lax.ppermute(q2, "gx", pairs(gx, 1))
     y1 = lax.ppermute(p1, "gy", pairs(gy, 0))
     y2 = lax.ppermute(p2, "gy", pairs(gy, 1))
-    x1 = lax.ppermute(q1, "gx", pairs(gx, 0))
-    x2 = lax.ppermute(q2, "gx", pairs(gx, 1))
     c1, c2 = call(
-        functools.partial(corner_kernel, dims), [((2 * nv, lanes), f32)] * 2, [VM] * 2, "corner"
+        functools.partial(corner_kernel, dims), [((2 * nv, lanes), f32)] * 2, [VM] * 2
     )(x1, x2)
     c1 = lax.ppermute(c1, "gy", pairs(gy, 0))
     c2 = lax.ppermute(c2, "gy", pairs(gy, 1))
 
-    section, kh, kl, th, tl = call(
+    section, kh, kl, th, tl, uh, ul = call(
         functools.partial(first_kernel, dims),
-        [((nv * size, lanes), f32)] + [((nv * lanes, width), bf16)] * 2 + [((width, nv * lanes), bf16)] * 2,
+        [(block, f32)]
+        + [((nv * lanes, width), bf16)] * 2
+        + [((width, nv * lanes), bf16)] * 2
+        + [((width, part), bf16)] * 2,
         [VM] * 3 + [SM] * 4,
-        "first",
     )(flat, basis_z.T, basis_v.T, *coeffs)
     state, message = call(
         functools.partial(second_kernel, dims),
-        [((nv * size, lanes), f32), ((size, width + basis_x.shape[1]), f32)],
+        [(block, f32), (message_shape(size, width, rows_x, rank_x, lanes), f32)],
         [VM] * 11 + [SM] * 4,
-        "second",
         [
-            pltpu.VMEM((nv * size, lanes), f32),
+            pltpu.VMEM(block, f32),
             pltpu.VMEM((nv * 2 * rows_x, lanes), f32),
             pltpu.VMEM((nv * 2 * rows_y, lanes), f32),
         ],
     )(flat, section, y1, y2, x1, x2, c1, c2, basis_x, kh, kl, *coeffs)
     blocks = gather_blocks(message)
-    (mass_row,) = call(functools.partial(mass_kernel, dims), [((1, lanes), f32)], [VM], "mass")(state)
-    outs = [((nv * size, lanes), f32), ((peers, lanes), f32)]
+    n = len(blocks)
+    coefs, row = call(
+        functools.partial(side_kernel, dims), [((size, part), f32), ((1, lanes), f32)], [VM] * 2
+    )(state, basis_z.T)
+    sizes = (rows_x, rows_y, width, rank_x)
+    outs = [((size, width), f32), ((peers, lanes), f32)]
     if basis_y.shape[0] * gy == basis_y.shape[1]:
-        recon, sums = call(
-            functools.partial(third_kernel, dims, width, len(blocks)), outs, [VM] * (len(blocks) + 4), "third"
-        )(*blocks, state, th, tl, mass_row)
+        mixed, sums = call(
+            functools.partial(third_kernel, sizes, rank_z, n), outs, [VM] * (n + 4)
+        )(*blocks, coefs, row, uh, ul)
     else:
-        (mixed,) = call(
-            functools.partial(mix_kernel, rows_y, width, len(blocks)), [((size, width), f32)], [VM] * len(blocks), "mixed"
-        )(*blocks)
+        (mixed,) = call(functools.partial(mix_kernel, sizes, n), outs[:1], [VM] * n)(*blocks)
         mixed = mixed.reshape(rows_x, rows_y, width)
         core = lax.psum(jnp.einsum("xyk,yb->xbk", mixed, basis_y, precision=HIGH), "gy")
         mixed = jnp.einsum("xbk,yb->xyk", core, basis_y, precision=HIGH).reshape(size, width)
-        recon, sums = call(functools.partial(decode_kernel, dims), outs, [VM] * 5, "decode")(
-            mixed, state, th, tl, mass_row
+        (sums,) = call(functools.partial(settle_kernel, rank_z), outs[1:], [VM] * 5)(
+            mixed, coefs, row, uh, ul
         )
+    (recon,) = call(functools.partial(decode_kernel, dims), [(block, f32)], [VM] * 3)(mixed, th, tl)
     if peers > 64:
         sums = lax.psum(sums[0], ("gx", "gy"))
     else:
@@ -386,7 +460,7 @@
 
 def solution(mesh):
     return jax.shard_map(
-        on_device,
+        program,
         mesh=mesh,
         in_specs=(
             P(None, "gx", "gy", None),

time: 48.8 us -> 50.7 us (1.039)
  blocking collectives: 13 us -> 0 us
  starting transfers between devices: 15.6 us -> 22 us
  waiting for transfers between devices: 4.75 us -> 9.62 us
  Pallas kernels: 9.76 us -> 14.5 us
  local copies, waits for them, and re-layouts: 3.83 us -> 2.91 us
    all_to_all x1 -> x0, blocking collectives: 13 us -> none  [on_device(): sums = jnp.sum(lax.all_to_all(sums, ('gx', 'gy'), 0, 0, tiled=True), axis=0)]
    all_to_all x0 -> x1, starting transfers between devices: none -> 6.37 us  [program(): sums = jnp.sum(lax.all_to_all(sums, ('gx', 'gy'), 0, 0, tiled=True), axis=0)]
    all_to_all x0 -> x1, waiting for transfers between devices: none -> 5.49 us  [program(): sums = jnp.sum(lax.all_to_all(sums, ('gx', 'gy'), 0, 0, tiled=True), axis=0)]
    pallas_call x6 -> x7, Pallas kernels: 9.76 us -> 14.5 us  [the longest x1 3.89 us: program(): call(functools.partial(side_kernel, dims), [((size, part), f32), ((1, lan...]
    unnamed x22 -> x20, local copies, waits for them, and re-layouts: 3.83 us -> 2.91 us
    ppermute x3, waiting for transfers between devices: 4.13 us -> 3.5 us  [gather_blocks(): blocks = blocks + [lax.ppermute(b, 'gx', swaps) for b in blocks]]
  transfers between devices with their start and end apart: 9 -> 10, of which waited for: 2 -> 3; matrix products, arithmetic and copies ran while one was open for 0% -> 0% of each run, Pallas kernels for 6% -> 16%
where the time goes in v4:
time: 50.7 us; the launch traced here: 50.4 us
  starting transfers between devices  22 us (43%)
  Pallas kernels  14.5 us (29%)
  waiting for transfers between devices  9.62 us (19%)
  local copies, waits for them, and re-layouts  2.91 us (6%)
  between operations  0.81 us (2%)
  other arithmetic  0.65 us (1%)
    all_to_all x1, starting transfers between devices, program(): sums = jnp.sum(lax.all_to_all(sums, ('gx', 'gy'), 0, 0, tiled=True), axis=0)  6.37 us
    ppermute x3, starting transfers between devices, gather_blocks(): blocks = blocks + [lax.ppermute(b, 'gx', swaps) for b in blocks]  6.14 us
    all_to_all x1, waiting for transfers between devices, program(): sums = jnp.sum(lax.all_to_all(sums, ('gx', 'gy'), 0, 0, tiled=True), axis=0)  5.49 us
    ppermute x1, starting transfers between devices, program(): c1 = lax.ppermute(c1, 'gy', pairs(gy, 0))  4.34 us
    pallas_call x1, Pallas kernels, program(): call(functools.partial(side_kernel, dims), [((size, part), f32), ((1, lan...  3.89 us
    pallas_call x1, Pallas kernels, program(): call(functools.partial(second_kernel, dims), [(block, f32), (message_shap...  3.89 us
    ppermute x3, waiting for transfers between devices, gather_blocks(): blocks = blocks + [lax.ppermute(b, 'gx', swaps) for b in blocks]  3.5 us
    ppermute x1, starting transfers between devices, program(): y1 = lax.ppermute(p1, 'gy', pairs(gy, 0))  3.06 us
  transfers between devices with their start and end apart: 10, of which 3 were waited for; matrix products, arithmetic and copies ran while one was open for 0% of the time, Pallas kernels for 16%

profile of v4, /device:TPU:0, one launch (start us, length us, event | category | flops | bytes accessed | tf_op | source)
XLA Modules:
  0.0 50.4 jit_solution(3026108296558595935)
XLA Ops:
  0.6 0.0 copy-start
  0.6 1.1 %copy-done = f32[12,16,8,128]{3,2,1,0:T(8,128)S(1)} copy-done((f32[12,16,8,128]{3,2,1,0:T(8,128)S(1)}, f32[12,16,8,128]{3,2,1,0:T(8,128)}, u32[]{:S(2)}) %copy-start) | copy-done | bytes 786456
  1.8 0.0 copy-start.1
  1.8 0.1 shard_map.104
  1.9 3.1 %collective-permute-start = (f32[384,128]{1,0:T(8,128)S(1)}, f32[384,128]{1,0:T(8,128)S(1)}, u32[]{:S(2)}, u32[]{:S(2)}) collective-permute-start(f32[384,128]{1,0:T(8,128)S(1)} %get-tuple-element.23), channel_id=1, source_target_pairs={{0,1},{2,3},{4,5},{6,7},{1,0},{3,2},{5,4},{7,6},{8,9},{10,11},{12,... | collective-permute-start | bytes 589832 | tf_op jit(solution)/shard_map/ppermute | solution.py:407
  4.9 0.7 %collective-permute-start.1 = (f32[384,128]{1,0:T(8,128)S(1)}, f32[384,128]{1,0:T(8,128)S(1)}, u32[]{:S(2)}, u32[]{:S(2)}) collective-permute-start(f32[384,128]{1,0:T(8,128)S(1)} %get-tuple-element.24), channel_id=1, source_target_pairs={{1,2},{3,4},{5,6},{2,1},{4,3},{6,5},{9,10},{11,12},{13,14},{10,9},... | collective-permute-start | bytes 589832 | tf_op jit(solution)/shard_map/ppermute | solution.py:408
  5.6 0.1 collective-permute-start.2
  5.7 0.7 %collective-permute-start.3 = (f32[192,128]{1,0:T(8,128)S(1)}, f32[192,128]{1,0:T(8,128)S(1)}, u32[]{:S(2)}, u32[]{:S(2)}) collective-permute-start(f32[192,128]{1,0:T(8,128)S(1)} %get-tuple-element.26), channel_id=1, source_target_pairs={{8,16},{16,8},{9,17},{17,9},{10,18},{18,10},{11,19},{19,11},{12,20... | collective-permute-start | bytes 294920 | tf_op jit(solution)/shard_map/ppermute | solution.py:406
  6.3 0.6 %collective-permute-done.2.x1 = f32[192,128]{1,0:T(8,128)S(1)} collective-permute-done((f32[192,128]{1,0:T(8,128)S(1)}, f32[192,128]{1,0:T(8,128)S(1)}, u32[]{:S(2)}, u32[]{:S(2)}) %collective-permute-start.2) | collective-permute-done | bytes 98336 | tf_op jit(solution)/shard_map/ppermute | solution.py:405
  6.9 0.0 collective-permute-done.3.x2
  7.0 0.0 copy-start.3
  7.0 0.0 copy-start.4
  7.0 0.0 copy-start.6
  7.0 4.3 %collective-permute-start.4 = (f32[24,128]{1,0:T(8,128)S(1)}, f32[24,128]{1,0:T(8,128)S(1)}, u32[]{:S(2)}, u32[]{:S(2)}) collective-permute-start(f32[24,128]{1,0:T(8,128)S(1)} %get-tuple-element.27), channel_id=1, source_target_pairs={{0,1},{2,3},{4,5},{6,7},{1,0},{3,2},{5,4},{7,6},{8,9},{10,11},{12,... | collective-permute-start | bytes 36872 | tf_op jit(solution)/shard_map/ppermute | solution.py:412
  11.3 0.7 %collective-permute-start.5 = (f32[24,128]{1,0:T(8,128)S(1)}, f32[24,128]{1,0:T(8,128)S(1)}, u32[]{:S(2)}, u32[]{:S(2)}) collective-permute-start(f32[24,128]{1,0:T(8,128)S(1)} %get-tuple-element.28), channel_id=1, source_target_pairs={{1,2},{3,4},{5,6},{2,1},{4,3},{6,5},{9,10},{11,12},{13,14},{10,9},... | collective-permute-start | bytes 36872 | tf_op jit(solution)/shard_map/ppermute | solution.py:413
  12.0 0.0 copy-start.7
  12.0 0.0 copy-start.8
  12.0 0.0 copy-start.9
  12.0 0.0 copy-done.1
  12.0 0.0 copy-done.3
  12.0 0.0 copy-done.4
  12.1 0.0 copy-done.6
  12.1 0.6 %copy-done.7 = f32[12]{0:T(128)S(1)} copy-done((f32[12]{0:T(128)S(1)}, f32[12]{0:T(128)}, u32[]{:S(2)}) %copy-start.7) | copy-done | bytes 72
  12.7 0.0 copy-done.8
  12.7 0.0 copy-done.9
  12.7 0.0 copy-start.5
  12.7 2.7 %shard_map.103 = (f32[1536,128]{1,0:T(8,128)S(1)}, bf16[1536,192]{1,0:T(8,128)(2,1)S(1)}, bf16[1536,192]{1,0:T(8,128)(2,1)S(1)}, bf16[192,1536]{1,0:T(8,128)(2,1...) custom-call(f32[1536,128]{1,0:T(8,128)S(1)} %bitcast.9, ...), custom_call_target="tpu_custom_call" | custom-call | flops 10000000 | bytes 1000000 | tf_op jit(solution)/shard_map/pallas_call | solution.py:415
  15.4 0.0 collective-permute-done.4.c1
  15.4 0.0 collective-permute-done.5.c2
  15.4 0.0 collective-permute-done.y1
  15.4 0.0 collective-permute-done.1.y2
  15.4 0.0 copy-done.5
  15.4 3.9 %shard_map.106 = (f32[1536,128]{1,0:T(8,128)}, f32[200,128]{1,0:T(8,128)S(1)}) custom-call(f32[1536,128]{1,0:T(8,128)S(1)} %bitcast.10, f32[1536,128]{1,0:T(8,128)S(1)} %get-tuple-element.22.s_ref, f32[384,128]{1,0:T(8,128)S(1)} %collective-permute-done.y1, f32[384,128]{1,0:T(8,128)S(1)} %collective-permute-done.1.y2, ...), custom_call_target="tpu_custom_call" | custom-call | flops 10000000 | bytes 1000000 | tf_op jit(solution)/shard_map/pallas_call | solution.py:423
  19.3 6.1 %collective-permute-start.6 = (f32[200,128]{1,0:T(8,128)S(1)}, f32[200,128]{1,0:T(8,128)S(1)}, u32[]{:S(2)}, u32[]{:S(2)}) collective-permute-start(f32[200,128]{1,0:T(8,128)S(1)} %get-tuple-element.32.refs_0_), channel_id=1, source_target_pairs={{0,16},{8,24},{16,0},{24,8},{1,17},{9,25},{17,1},{25,9},{2,18},{10... | collective-permute-start | bytes 307208 | tf_op jit(solution)/shard_map/ppermute | solution.py:383
  25.4 0.0 collective-permute-start.7
  25.5 3.5 %collective-permute-done.6.refs_1_ = f32[200,128]{1,0:T(8,128)S(1)} collective-permute-done((f32[200,128]{1,0:T(8,128)S(1)}, f32[200,128]{1,0:T(8,128)S(1)}, u32[]{:S(2)}, u32[]{:S(2)}) %collective-permute-start.6) | collective-permute-done | bytes 102432 | tf_op jit(solution)/shard_map/ppermute | solution.py:383
  28.9 0.0 collective-permute-start.8
  29.0 0.0 copy-start.2
  29.0 1.1 %copy-done.2 = f32[1536,128]{1,0:T(8,128)S(1)} copy-done((f32[1536,128]{1,0:T(8,128)S(1)}, f32[1536,128]{1,0:T(8,128)}, u32[]{:S(2)}) %copy-start.2) | copy-done | bytes 786456
  30.1 3.9 %shard_map.107 = (f32[128,384]{1,0:T(8,128)S(1)}, f32[1,128]{1,0:T(1,128)S(1)}) custom-call(f32[1536,128]{1,0:T(8,128)S(1)} %copy-done.2, f32[32,128]{1,0:T(8,128)S(1)} %bitcast.13), custom_call_target="tpu_custom_call" | custom-call | flops 10000000 | bytes 1000000 | tf_op jit(solution)/shard_map/pallas_call | solution.py:435
  34.0 0.0 collective-permute-done.7.refs_2_
  34.0 0.0 collective-permute-done.8.refs_3_
  34.0 2.3 %shard_map.108 = (f32[128,192]{1,0:T(8,128)S(1)}, f32[32,128]{1,0:T(8,128)}) custom-call(f32[200,128]{1,0:T(8,128)S(1)} %get-tuple-element.32.refs_0_, f32[200,128]{1,0:T(8,128)S(1)} %collective-permute-done.6.refs_1_, f32[200,128]{1,0:T(8,128)S(1)} %collective-permute-done.7.refs_2_, f32[200,128]{1,0:T(8,128)S(1)} %collective-permute-done.8.refs_3_, ...), custom_call_target="tpu_custom_call" | custom-call | flops 10000000 | bytes 1000000 | tf_op jit(solution)/shard_map/pallas_call | solution.py:441
  36.2 6.4 %all-to-all-start = ((f32[32,1,128]{2,1,0:T(1,128)}), f32[32,1,128]{2,1,0:T(1,128)S(1)}, u32[]{:S(2)}, u32[]{:S(2)}) async-start(f32[32,1,128]{2,1,0:T(1,128)} %bitcast.6), calls=%async_computation | async-start | bytes 32768 | tf_op jit(solution)/shard_map/all_to_all | solution.py:456
  42.6 1.7 %shard_map.109 = f32[1536,128]{1,0:T(8,128)} custom-call(f32[128,192]{1,0:T(8,128)S(1)} %get-tuple-element.37.d_ref, bf16[192,1536]{1,0:T(8,128)(2,1)S(1)} %get-tuple-element.38.th, bf16[192,1536]{1,0:T(8,128)(2,1)S(1)} %get-tuple-element.39.tl), custom_call_target="tpu_custom_call" | custom-call | flops 10000000 | bytes 1000000 | tf_op jit(solution)/shard_map/pallas_call | solution.py:452
  44.3 5.5 %all-to-all-done = f32[32,1,128]{2,1,0:T(1,128)S(1)} async-done(((f32[32,1,128]{2,1,0:T(1,128)}), f32[32,1,128]{2,1,0:T(1,128)S(1)}, u32[]{:S(2)}, u32[]{:S(2)}) %all-to-all-start) | async-done | bytes 16416 | tf_op jit(solution)/shard_map/all_to_all | solution.py:456
  49.8 0.1 reduce_sum.9
  49.8 0.6 %fusion = f32[12]{0:T(128)} fusion(f32[128]{0:T(128)S(1)} %reduce_sum.9), kind=kLoop, calls=%fused_computation.1 | loop fusion | flops 24 | bytes 144 | tf_op jit(solution)/shard_map/sqrt | solution.py:457
  (1 shorter events, 0.0 us)
Async XLA Ops:
  0.6 1.1 %copy-start = (f32[12,16,8,128]{3,2,1,0:T(8,128)S(1)}, f32[12,16,8,128]{3,2,1,0:T(8,128)}, u32[]{:S(2)}) copy-start(f32[12,16,8,128]{3,2,1,0:T(8,128)} %param.9) | copy-start | bytes 2359300
  1.8 10.3 %copy-start.1 = (f32[12,16,8,128]{3,2,1,0:T(8,128)S(1)}, f32[12,16,8,128]{3,2,1,0:T(8,128)}, u32[]{:S(2)}) copy-start(f32[12,16,8,128]{3,2,1,0:T(8,128)} %param.9) | copy-start | bytes 2359300
  1.9 13.5 %collective-permute-start = (f32[384,128]{1,0:T(8,128)S(1)}, f32[384,128]{1,0:T(8,128)S(1)}, u32[]{:S(2)}, u32[]{:S(2)}) collective-permute-start(f32[384,128]{1,0:T(8,128)S(1)} %get-tuple-element.23), channel_id=1, source_target_pairs={{0,1},{2,3},{4,5},{6,7},{1,0},{3,2},{5,4},{7,6},{8,9},{10,11},{12,... | collective-permute-start | bytes 589832 | tf_op jit(solution)/shard_map/ppermute | solution.py:407
  4.9 10.5 %collective-permute-start.1 = (f32[384,128]{1,0:T(8,128)S(1)}, f32[384,128]{1,0:T(8,128)S(1)}, u32[]{:S(2)}, u32[]{:S(2)}) collective-permute-start(f32[384,128]{1,0:T(8,128)S(1)} %get-tuple-element.24), channel_id=1, source_target_pairs={{1,2},{3,4},{5,6},{2,1},{4,3},{6,5},{9,10},{11,12},{13,14},{10,9},... | collective-permute-start | bytes 589832 | tf_op jit(solution)/shard_map/ppermute | solution.py:408
  5.6 1.4 %collective-permute-start.2 = (f32[192,128]{1,0:T(8,128)S(1)}, f32[192,128]{1,0:T(8,128)S(1)}, u32[]{:S(2)}, u32[]{:S(2)}) collective-permute-start(f32[192,128]{1,0:T(8,128)S(1)} %get-tuple-element.25), channel_id=1, source_target_pairs={{0,8},{16,24},{8,0},{24,16},{1,9},{17,25},{9,1},{25,17},{2,10},{18... | collective-permute-start | bytes 294920 | tf_op jit(solution)/shard_map/ppermute | solution.py:405
  5.7 1.3 %collective-permute-start.3 = (f32[192,128]{1,0:T(8,128)S(1)}, f32[192,128]{1,0:T(8,128)S(1)}, u32[]{:S(2)}, u32[]{:S(2)}) collective-permute-start(f32[192,128]{1,0:T(8,128)S(1)} %get-tuple-element.26), channel_id=1, source_target_pairs={{8,16},{16,8},{9,17},{17,9},{10,18},{18,10},{11,19},{19,11},{12,20... | collective-permute-start | bytes 294920 | tf_op jit(solution)/shard_map/ppermute | solution.py:406
  7.0 5.1 %copy-start.3 = (f32[128,32]{0,1:T(8,128)S(1)}, f32[128,32]{0,1:T(8,128)}, u32[]{:S(2)}) copy-start(f32[128,32]{0,1:T(8,128)} %param.15) | copy-start | bytes 49156
  7.0 5.1 %copy-start.4 = (f32[12,12]{1,0:T(8,128)S(1)}, f32[12,12]{1,0:T(8,128)}, u32[]{:S(2)}) copy-start(f32[12,12]{1,0:T(8,128)} %mix.3) | copy-start | bytes 1732
  7.0 5.1 %copy-start.6 = (f32[12,6]{0,1:T(8,128)S(1)}, f32[12,6]{0,1:T(8,128)}, u32[]{:S(2)}) copy-start(f32[12,6]{0,1:T(8,128)} %param.16) | copy-start | bytes 868
  7.0 8.4 %collective-permute-start.4 = (f32[24,128]{1,0:T(8,128)S(1)}, f32[24,128]{1,0:T(8,128)S(1)}, u32[]{:S(2)}, u32[]{:S(2)}) collective-permute-start(f32[24,128]{1,0:T(8,128)S(1)} %get-tuple-element.27), channel_id=1, source_target_pairs={{0,1},{2,3},{4,5},{6,7},{1,0},{3,2},{5,4},{7,6},{8,9},{10,11},{12,... | collective-permute-start | bytes 36872 | tf_op jit(solution)/shard_map/ppermute | solution.py:412
  11.3 4.0 %collective-permute-start.5 = (f32[24,128]{1,0:T(8,128)S(1)}, f32[24,128]{1,0:T(8,128)S(1)}, u32[]{:S(2)}, u32[]{:S(2)}) collective-permute-start(f32[24,128]{1,0:T(8,128)S(1)} %get-tuple-element.28), channel_id=1, source_target_pairs={{1,2},{3,4},{5,6},{2,1},{4,3},{6,5},{9,10},{11,12},{13,14},{10,9},... | collective-permute-start | bytes 36872 | tf_op jit(solution)/shard_map/ppermute | solution.py:413
  12.0 0.7 %copy-start.7 = (f32[12]{0:T(128)S(1)}, f32[12]{0:T(128)}, u32[]{:S(2)}) copy-start(f32[12]{0:T(128)} %dif.3) | copy-start | bytes 148
  12.0 0.7 %copy-start.8 = (f32[12]{0:T(128)S(1)}, f32[12]{0:T(128)}, u32[]{:S(2)}) copy-start(f32[12]{0:T(128)} %pre.3) | copy-start | bytes 148
  12.0 0.7 %copy-start.9 = (f32[12]{0:T(128)S(1)}, f32[12]{0:T(128)}, u32[]{:S(2)}) copy-start(f32[12]{0:T(128)} %act.3) | copy-start | bytes 148
  12.7 2.7 %copy-start.5 = (f32[16,64]{1,0:T(8,128)S(1)}, f32[16,64]{1,0:T(8,128)}, u32[]{:S(2)}) copy-start(f32[16,64]{1,0:T(8,128)} %bx_ref.1) | copy-start | bytes 12292
  19.3 9.6 %collective-permute-start.6 = (f32[200,128]{1,0:T(8,128)S(1)}, f32[200,128]{1,0:T(8,128)S(1)}, u32[]{:S(2)}, u32[]{:S(2)}) collective-permute-start(f32[200,128]{1,0:T(8,128)S(1)} %get-tuple-element.32.refs_0_), channel_id=1, source_target_pairs={{0,16},{8,24},{16,0},{24,8},{1,17},{9,25},{17,1},{25,9},{2,18},{10... | collective-permute-start | bytes 307208 | tf_op jit(solution)/shard_map/ppermute | solution.py:383
  25.4 8.5 %collective-permute-start.7 = (f32[200,128]{1,0:T(8,128)S(1)}, f32[200,128]{1,0:T(8,128)S(1)}, u32[]{:S(2)}, u32[]{:S(2)}) collective-permute-start(f32[200,128]{1,0:T(8,128)S(1)} %get-tuple-element.32.refs_0_), channel_id=1, source_target_pairs={{0,8},{8,0},{16,24},{24,16},{1,9},{9,1},{17,25},{25,17},{2,10},{10... | collective-permute-start | bytes 307208 | tf_op jit(solution)/shard_map/ppermute | solution.py:383
  28.9 5.0 %collective-permute-start.8 = (f32[200,128]{1,0:T(8,128)S(1)}, f32[200,128]{1,0:T(8,128)S(1)}, u32[]{:S(2)}, u32[]{:S(2)}) collective-permute-start(f32[200,128]{1,0:T(8,128)S(1)} %collective-permute-done.6.refs_1_), channel_id=1, source_target_pairs={{0,8},{8,0},{16,24},{24,16},{1,9},{9,1},{17,25},{25,17},{2,10},{10... | collective-permute-start | bytes 307208 | tf_op jit(solution)/shard_map/ppermute | solution.py:383
  29.0 1.1 %copy-start.2 = (f32[1536,128]{1,0:T(8,128)S(1)}, f32[1536,128]{1,0:T(8,128)}, u32[]{:S(2)}) copy-start(f32[1536,128]{1,0:T(8,128)} %get-tuple-element.31.state_ref) | copy-start | bytes 2359300
  36.2 13.5 %all-to-all-start = ((f32[32,1,128]{2,1,0:T(1,128)}), f32[32,1,128]{2,1,0:T(1,128)S(1)}, u32[]{:S(2)}, u32[]{:S(2)}) async-start(f32[32,1,128]{2,1,0:T(1,128)} %bitcast.6), calls=%async_computation | async-start | bytes 32768 | tf_op jit(solution)/shard_map/all_to_all | solution.py:456

commit v5 on v4

v5 whole, which is shorter than its diff:
```python
import functools

import jax
import jax.numpy as jnp
from jax import lax
from jax.experimental import pallas as pl
from jax.experimental.pallas import tpu as pltpu
from jax.sharding import PartitionSpec as P


HIGH = lax.Precision.HIGHEST
VM = pl.BlockSpec(memory_space=pltpu.VMEM)
SM = pl.BlockSpec(memory_space=pltpu.SMEM)


def call(kernel, outs, in_specs, scratch=(), flops=10**7, vmem=12, out_specs=None):
    return pl.pallas_call(
        kernel,
        out_shape=[jax.ShapeDtypeStruct(s, d) for s, d in outs],
        in_specs=in_specs,
        out_specs=out_specs or [VM] * len(outs),
        scratch_shapes=list(scratch),
        compiler_params=pltpu.CompilerParams(vmem_limit_bytes=vmem << 20),
        cost_estimate=pl.CostEstimate(flops=flops, bytes_accessed=10**6, transcendentals=0),
    )


def split(a):
    hi = a.astype(jnp.bfloat16)
    lo = (a - hi.astype(jnp.float32)).astype(jnp.bfloat16)
    return hi, lo


def mm(a, b, nt=False):
    dims = (((1,), (1 if nt else 0,)), ((), ()))
    return lax.dot_general(a, b, dims, preferred_element_type=jnp.float32)


def mm3(a, b, nt=False):
    return mm(a[0], b[0], nt) + mm(a[0], b[1], nt) + mm(a[1], b[0], nt)


def place(shape, dim):
    return lax.broadcasted_iota(jnp.int32, shape, dim)


def shifted(w, axis, before=0.0, after=0.0):
    size = w.shape[axis]
    pos = place(w.shape, axis)
    low = jnp.where(pos == 0, before, pltpu.roll(w, 1, axis))
    high = jnp.where(pos == size - 1, after, pltpu.roll(w, size - 1, axis))
    return low + high


def tiles_of(a):
    return a.reshape(a.size // (8 * a.shape[-1]), 8, a.shape[-1])


def reaction(ws, act, both, low):
    n = len(ws)
    cold = -1.0 / (1.5 + jnp.tanh(ws[0]))
    rates = [tiles_of(jnp.exp(act[v] * cold) * ws[v]) for v in range(n)]
    count, lanes = rates[0].shape[0], rates[0].shape[2]
    stacked = jnp.concatenate(
        [jnp.concatenate([rates[v][t] for v in range(n)], axis=0) for t in range(count)], axis=1
    )
    hi, lo = split(stacked)
    out = mm(both, jnp.concatenate([hi, lo], axis=0)) + mm(low, hi)
    return [
        jnp.stack([out[v * 8 : (v + 1) * 8, t * lanes : (t + 1) * lanes] for t in range(count)]).reshape(ws[v].shape)
        for v in range(n)
    ]


def stage(ref, nv, rows_x, rows_y, dif, act, mixers, emit, low_edge, high_edge, step=4):
    lanes = ref.shape[1]
    size = rows_x * rows_y

    def rows(v, x, n):
        return ref[pl.ds(v * size + x * rows_y, n * rows_y), :].reshape(n, rows_y, lanes)

    step = min(step, rows_x)
    for x in range(0, rows_x, step):
        ws = [rows(v, x, step) for v in range(nv)]
        made = reaction(ws, act, *mixers)
        for v in range(nv):
            w = ws[v]
            first = rows(v, x - 1, 1) if x > 0 else low_edge(v)[None]
            last = rows(v, x + step, 1) if x + step < rows_x else high_edge(v)[None]
            beside = jnp.concatenate([first, w[:-1]], 0) + jnp.concatenate([w[1:], last], 0)
            lap = beside + shifted(w, 1) + shifted(w, 2) - 6.0 * w
            emit(v, x, step, w, dif[v] * lap + made[v])


def odd(axis):
    return lax.axis_index(axis) % 2 == 1


def two(one, other, is_odd, at):
    a, b = one[at, :], other[at, :]
    return jnp.where(is_odd, a, b), jnp.where(is_odd, b, a)


def pack_x_kernel(dims, f_ref, q1, q2):
    nv, rows_x, rows_y, _ = dims
    size = rows_x * rows_y
    for layer in range(2):
        for v in range(nv):
            low = f_ref[pl.ds(v * size + layer * rows_y, rows_y), :]
            high = f_ref[pl.ds(v * size + (rows_x - 1 - layer) * rows_y, rows_y), :]
            at = pl.ds((layer * nv + v) * rows_y, rows_y)
            q1[at, :] = jnp.where(odd("gx"), low, high)
            q2[at, :] = jnp.where(odd("gx"), high, low)


def pack_y_kernel(dims, f_ref, x1, x2, p1, p2):
    nv, rows_x, rows_y, _ = dims
    size = rows_x * rows_y

    def put(at, low, high):
        p1[at, :] = jnp.where(odd("gy"), low, high)
        p2[at, :] = jnp.where(odd("gy"), high, low)

    for layer in range(2):
        for v in range(nv):
            low = f_ref[pl.ds(v * size + layer, rows_x, stride=rows_y), :]
            high = f_ref[pl.ds(v * size + rows_y - 1 - layer, rows_x, stride=rows_y), :]
            put(pl.ds((layer * nv + v) * rows_x, rows_x), low, high)
    lows = two(x1, x2, odd("gx"), pl.ds(0, nv, stride=rows_y))
    highs = two(x1, x2, odd("gx"), pl.ds(rows_y - 1, nv, stride=rows_y))
    for side in range(2):
        put(pl.ds((2 * rows_x + side) * nv, nv), lows[side], highs[side])


def first_kernel(dims, f_ref, x1, x2, bz_ref, bv_ref, mix_ref, dif, pre, act, *outs):
    s_ref, k_ref, t_ref, u_ref, n_ref, both_ref, low_ref = outs
    nv, rows_x, rows_y, lanes = dims
    size = rows_x * rows_y
    spot = place((nv, nv), 1)
    scaled = mix_ref[...]
    for u in range(nv):
        scaled = jnp.where(spot == u, scaled * pre[u], scaled)
    wide = (nv * 8, nv)
    spread = (place(wide, 0) // 8 == place(wide, 1)).astype(jnp.float32)
    full = jnp.dot(spread, scaled, precision=HIGH, preferred_element_type=jnp.float32)
    full = lax.dot_general(
        full, spread, (((1,), (1,)), ((), ())), precision=HIGH, preferred_element_type=jnp.float32
    )
    hi, lo = split(jnp.where(place(full.shape, 0) % 8 == place(full.shape, 1) % 8, full, 0.0))
    both = jnp.concatenate([hi, hi], axis=1)
    both_ref[...], low_ref[...] = both, lo

    def emit(v, x, n, w, t):
        s_ref[pl.ds(v * size + x * rows_y, n * rows_y), :] = (w + t).reshape(n * rows_y, lanes)

    def edge(side):
        return lambda v: two(x1, x2, odd("gx"), pl.ds(v * rows_y, rows_y))[side]

    stage(f_ref, nv, rows_x, rows_y, dif, act, (both, lo), emit, edge(0), edge(1))
    bz, bv = bz_ref[...], bv_ref[...]
    rank_z, rank_v = bz.shape[0], bv.shape[0]
    width, part = rank_z * rank_v, nv * rank_z
    pick_z = (place((rank_z, width), 1) % rank_z == place((rank_z, width), 0)).astype(jnp.float32)
    pick_v = (place((rank_v, width), 1) // rank_z == place((rank_v, width), 0)).astype(jnp.float32)
    first = (((0,), (0,)), ((), ()))
    wide_z = lax.dot_general(bz, pick_z, first, precision=HIGH, preferred_element_type=jnp.float32)
    wide_v = lax.dot_general(bv, pick_v, first, precision=HIGH, preferred_element_type=jnp.float32)
    for v in range(nv):
        product = wide_z * wide_v[v : v + 1, :]
        at = slice(v * lanes, (v + 1) * lanes)
        k_ref[0, at, :], k_ref[1, at, :] = split(product)
        t_ref[0, :, at], t_ref[1, :, at] = split(product.T)
    pick_u = (place((nv, part), 1) // rank_z == place((nv, part), 0)).astype(jnp.float32)
    tall = lax.dot_general(pick_v, bv, first, precision=HIGH, preferred_element_type=jnp.float32)
    tall = jnp.dot(tall, pick_u, precision=HIGH, preferred_element_type=jnp.float32)
    same = place((width, part), 0) % rank_z == place((width, part), 1) % rank_z
    u_ref[0], u_ref[1] = split(jnp.where(same, tall, 0.0))
    held = lanes // rank_z
    spread = (place((rank_z, lanes), 1) % rank_z == place((rank_z, lanes), 0)).astype(jnp.float32)
    wide_z = lax.dot_general(bz, spread, first, precision=HIGH, preferred_element_type=jnp.float32)
    group = place((lanes, lanes), 1) // rank_z
    for j in range(held):
        at = slice(j * lanes, (j + 1) * lanes)
        n_ref[0, at, :], n_ref[1, at, :] = split(jnp.where(group == j, wide_z, 0.0))


def second_kernel(
    dims, f_ref, s_ref, y1, y2, x1, x2, bx_ref, k_ref, both_ref, low_ref, dif, act,
    state_ref, m_ref, sec, gy_ref, gx_ref,
):
    nv, rows_x, rows_y, lanes = dims
    size = rows_x * rows_y
    ix, iy = lax.axis_index("gx"), lax.axis_index("gy")
    has_x = (ix > 0, ix < lax.axis_size("gx") - 1)
    has_y = (iy > 0, iy < lax.axis_size("gy") - 1)
    mixers = (both_ref[...], low_ref[...])

    def y_ghost(layer, v):
        return jnp.stack(two(y1, y2, odd("gy"), pl.ds((layer * nv + v) * rows_x, rows_x)))

    def x_ghost(layer, v):
        return jnp.stack(two(x1, x2, odd("gx"), pl.ds((layer * nv + v) * rows_y, rows_y)))

    def corner(side, v):
        return two(y1, y2, odd("gy"), pl.ds((2 * rows_x + side) * nv + v, 1))

    def keep(value, flags):
        inside = [jnp.where(flags[i], value[i], 0.0) for i in range(2)]
        return jnp.concatenate(inside, axis=0)

    ys = [y_ghost(0, v) for v in range(nv)]
    xs = [x_ghost(0, v) for v in range(nv)]
    made = reaction([jnp.concatenate([tiles_of(ys[v]), tiles_of(xs[v])], 0) for v in range(nv)], act, *mixers)
    for v in range(nv):
        g = ys[v]
        cut = g.size // (8 * lanes)
        low = f_ref[pl.ds(v * size, rows_x, stride=rows_y), :]
        high = f_ref[pl.ds(v * size + rows_y - 1, rows_x, stride=rows_y), :]
        left, right = corner(0, v), corner(1, v)
        lap = y_ghost(1, v) + jnp.stack([low, high]) - 6.0 * g
        lap = lap + shifted(g, 1, jnp.stack(left), jnp.stack(right)) + shifted(g, 2)
        out = g + (dif[v] * lap + made[v][:cut].reshape(g.shape))
        gy_ref[pl.ds(v * 2 * rows_x, 2 * rows_x), :] = keep(out, has_y)
        sec[pl.ds(v * size, size), :] = s_ref[pl.ds(v * size, size), :]
        at = pl.ds(v * size, rows_x, stride=rows_y)
        sec[at, :] = sec[at, :] + dif[v] * g[0]
        at = pl.ds(v * size + rows_y - 1, rows_x, stride=rows_y)
        sec[at, :] = sec[at, :] + dif[v] * g[1]
        g = xs[v]
        low = f_ref[pl.ds(v * size, rows_y), :]
        high = f_ref[pl.ds(v * size + size - rows_y, rows_y), :]
        before = jnp.stack([left[0], right[0]])
        after = jnp.stack([left[1], right[1]])
        lap = x_ghost(1, v) + jnp.stack([low, high]) - 6.0 * g
        lap = lap + shifted(g, 1, before, after) + shifted(g, 2)
        out = g + (dif[v] * lap + made[v][cut:].reshape(g.shape))
        gx_ref[pl.ds(v * 2 * rows_y, 2 * rows_y), :] = keep(out, has_x)

    def emit(v, x, n, w, t):
        at = pl.ds(v * size + x * rows_y, n * rows_y)
        state_ref[at, :] = 0.5 * ((f_ref[at, :] + w.reshape(n * rows_y, lanes)) + t.reshape(n * rows_y, lanes))

    stage(
        sec, nv, rows_x, rows_y, dif, act, mixers, emit,
        lambda v: gx_ref[pl.ds(v * 2 * rows_y, rows_y), :],
        lambda v: gx_ref[pl.ds((v * 2 + 1) * rows_y, rows_y), :],
    )
    his, los = [], []
    for v in range(nv):
        half = 0.5 * dif[v]
        at = pl.ds(v * size, rows_x, stride=rows_y)
        state_ref[at, :] = state_ref[at, :] + half * gy_ref[pl.ds(v * 2 * rows_x, rows_x), :]
        at = pl.ds(v * size + rows_y - 1, rows_x, stride=rows_y)
        state_ref[at, :] = state_ref[at, :] + half * gy_ref[pl.ds((v * 2 + 1) * rows_x, rows_x), :]
        hi, lo = split(state_ref[pl.ds(v * size, size), :])
        his.append(hi)
        los.append(lo)
    total = mm3((jnp.concatenate(his, 1), jnp.concatenate(los, 1)), (k_ref[0], k_ref[1]))
    pack_message(m_ref, total, bx_ref[...])


def dense(size, width, rows_x, rank_x, lanes):
    return width % lanes * 2 == lanes and rank_x * 2 == lanes and size % 16 == 0 and rows_x % 16 == 0


def message_shape(size, width, rows_x, rank_x, lanes):
    if not dense(size, width, rows_x, rank_x, lanes):
        return (size + rows_x, max(width, rank_x))
    return (size * (width // lanes) + size // 2 + rows_x // 2, lanes)


def fold(a):
    half = a.shape[0] // 2
    return jnp.concatenate([a[:half], a[half:]], axis=1)


def unfold(a):
    half = a.shape[1] // 2
    return jnp.concatenate([a[:, :half], a[:, half:]], axis=0)


def pack_message(m_ref, values, basis):
    size, width = values.shape
    lanes = m_ref.shape[1]
    if not dense(size, width, *basis.shape, lanes):
        m_ref[:size, :width] = values
        m_ref[size:, : basis.shape[1]] = basis
        return
    whole = width // lanes
    for i in range(whole):
        m_ref[pl.ds(i * size, size), :] = values[:, i * lanes : (i + 1) * lanes]
    m_ref[pl.ds(whole * size, size // 2), :] = fold(values[:, whole * lanes :])
    m_ref[pl.ds(whole * size + size // 2, basis.shape[0] // 2), :] = fold(basis)


def unpack_message(m_ref, size, width, rows_x, rank_x):
    lanes = m_ref.shape[1]
    if not dense(size, width, rows_x, rank_x, lanes):
        return m_ref[:size, :width], m_ref[size:, :rank_x]
    whole = width // lanes
    parts = [m_ref[pl.ds(i * size, size), :] for i in range(whole)]
    parts.append(unfold(m_ref[pl.ds(whole * size, size // 2), :]))
    basis = unfold(m_ref[pl.ds(whole * size + size // 2, rows_x // 2), :])
    return jnp.concatenate(parts, axis=1), basis


def mix_blocks(sizes, refs):
    rows_x, rows_y, width, rank_x = sizes
    size = rows_x * rows_y

    def repeated(basis):
        return jnp.broadcast_to(basis[:, None, :], (rows_x, rows_y, rank_x)).reshape(size, rank_x)

    parts = [unpack_message(ref, size, width, rows_x, rank_x) for ref in refs]
    values = jnp.concatenate([values for values, _ in parts], axis=0)
    bases = jnp.concatenate([repeated(basis) for _, basis in parts], axis=0)
    hi, lo = split(bases)
    link = mm3((hi[:size], lo[:size]), (hi, lo), True)
    same = place(link.shape, 0) % rows_y == place(link.shape, 1) % rows_y
    return mm3(split(jnp.where(same, link, 0.0)), split(values))


def side_kernel(dims, rank_z, state_ref, n_ref, out_ref, w_ref, row_ref, sem):
    nv, rows_x, rows_y, lanes = dims
    size = rows_x * rows_y
    write = pltpu.make_async_copy(state_ref, out_ref, sem)
    write.start()
    held = lanes // rank_z
    basis = (n_ref[0], n_ref[1])

    def squares(a):
        return jnp.sum((a * a).reshape(size // 8, 8, lanes), axis=0)

    outside, mass = [], []
    for v in range(0, nv, held):
        state = jnp.concatenate([state_ref[pl.ds((v + j) * size, size), :] for j in range(held)], axis=1)
        coefs = mm3(split(state), basis)
        w_ref[:, (v // held) * lanes : (v // held + 1) * lanes] = coefs
        rest = state - mm3(split(coefs), basis, True)
        for j in range(held):
            outside.append(squares(rest[:, j * lanes : (j + 1) * lanes]))
            mass.append(squares(state[:, j * lanes : (j + 1) * lanes]))
    every = jnp.concatenate(outside + mass, axis=0)
    ones = jnp.ones((8, lanes), jnp.float32)
    sums = lax.dot_general(
        ones, every, (((1,), (1,)), ((), ())), precision=HIGH, preferred_element_type=jnp.float32
    )
    shape = (every.shape[0], row_ref.shape[1])
    pick = (place(shape, 0) // 8 == place(shape, 1)).astype(jnp.float32)
    row_ref[...] = jnp.dot(sums, pick, precision=HIGH, preferred_element_type=jnp.float32)
    write.wait()


def settle(mixed, w_ref, row_ref, u_ref, sums_ref, rank_z):
    gap = w_ref[...] - mm3(split(mixed), (u_ref[0], u_ref[1]))
    size, part = gap.shape
    hi, lo = split(jnp.sum((gap * gap).reshape(size // 8, 8, part), axis=0))
    shape = (part, row_ref.shape[1])
    pick = (place(shape, 0) // rank_z == place(shape, 1)).astype(jnp.float32).astype(jnp.bfloat16)
    row = jnp.sum(mm(hi, pick) + mm(lo, pick), axis=0, keepdims=True) + row_ref[0:1, :]
    sums_ref[...] = jnp.broadcast_to(row, sums_ref.shape)


def third_kernel(sizes, rank_z, n, *refs):
    w_ref, row_ref, u_ref, d_ref, sums_ref = refs[n:]
    mixed = mix_blocks(sizes, refs[:n])
    d_ref[...] = mixed
    settle(mixed, w_ref, row_ref, u_ref, sums_ref, rank_z)


def mix_kernel(sizes, n, *refs):
    refs[n][...] = mix_blocks(sizes, refs[:n])


def settle_kernel(rank_z, d_ref, w_ref, row_ref, u_ref, sums_ref):
    settle(d_ref[...], w_ref, row_ref, u_ref, sums_ref, rank_z)


def decode_kernel(dims, d_ref, t_ref, recon_ref):
    nv, rows_x, rows_y, lanes = dims
    size = rows_x * rows_y
    halves = split(d_ref[...])
    for v in range(nv):
        cols = slice(v * lanes, (v + 1) * lanes)
        recon_ref[pl.ds(v * size, size), :] = mm3(halves, (t_ref[0, :, cols], t_ref[1, :, cols]))


def pairs(n, first):
    swaps = [(i, i + 1) for i in range(first, n - 1, 2)]
    return swaps + [(j, i) for i, j in swaps]


def gather_blocks(block):
    n = lax.axis_size("gx")
    if n & (n - 1):
        every = lax.all_gather(block, "gx", axis=0)
        return [block] + [jnp.roll(every, -lax.axis_index("gx"), 0)[i] for i in range(1, n)]
    blocks = [block]
    bit = n // 2
    while bit:
        swaps = [(i, i ^ bit) for i in range(n)]
        blocks = blocks + [lax.ppermute(b, "gx", swaps) for b in blocks]
        bit //= 2
    return blocks


def program(field, diffusion, prefactor, activation, mixing, basis_x, basis_y, basis_z, basis_v):
    f32, bf16 = jnp.float32, jnp.bfloat16
    dims = field.shape
    nv, rows_x, rows_y, lanes = dims
    size = rows_x * rows_y
    rank_x, rank_z, rank_v = basis_x.shape[1], basis_z.shape[1], basis_v.shape[1]
    width, part = rank_z * rank_v, nv * rank_z
    gx, gy = lax.axis_size("gx"), lax.axis_size("gy")
    peers = gx * gy
    flat = field.reshape(nv * size, lanes)
    block = (nv * size, lanes)

    y_msg, x_msg = (2 * nv * (rows_x + 1), lanes), (2 * nv * rows_y, lanes)
    q1, q2 = call(functools.partial(pack_x_kernel, dims), [(x_msg, f32)] * 2, [VM])(flat)
    x1 = lax.ppermute(q1, "gx", pairs(gx, 0))
    x2 = lax.ppermute(q2, "gx", pairs(gx, 1))
    p1, p2 = call(functools.partial(pack_y_kernel, dims), [(y_msg, f32)] * 2, [VM] * 3)(flat, x1, x2)
    y1 = lax.ppermute(p1, "gy", pairs(gy, 0))
    y2 = lax.ppermute(p2, "gy", pairs(gy, 1))

    section, k, t, u, n, both, low = call(
        functools.partial(first_kernel, dims),
        [
            (block, f32),
            ((2, nv * lanes, width), bf16),
            ((2, width, nv * lanes), bf16),
            ((2, width, part), bf16),
            ((2, lanes // rank_z * lanes, lanes), bf16),
            ((nv * 8, nv * 16), bf16),
            ((nv * 8, nv * 8), bf16),
        ],
        [VM] * 6 + [SM] * 3,
    )(flat, x1, x2, basis_z.T, basis_v.T, mixing, diffusion, prefactor, activation)
    state, message = call(
        functools.partial(second_kernel, dims),
        [(block, f32), (message_shape(size, width, rows_x, rank_x, lanes), f32)],
        [VM] * 10 + [SM] * 2,
        [
            pltpu.VMEM(block, f32),
            pltpu.VMEM((nv * 2 * rows_x, lanes), f32),
            pltpu.VMEM((nv * 2 * rows_y, lanes), f32),
        ],
    )(flat, section, y1, y2, x1, x2, basis_x, k, both, low, diffusion, activation)
    blocks = gather_blocks(message)
    count = len(blocks)
    state, coefs, row = call(
        functools.partial(side_kernel, dims, rank_z),
        [(block, f32), ((size, part), f32), ((8, lanes), f32)],
        [VM] * 2,
        [pltpu.SemaphoreType.DMA],
        out_specs=[pl.BlockSpec(memory_space=pl.ANY), VM, VM],
    )(state, n)
    sizes = (rows_x, rows_y, width, rank_x)
    outs = [((size, width), f32), ((peers, lanes), f32)]
    if basis_y.shape[0] * gy == basis_y.shape[1]:
        mixed, sums = call(
            functools.partial(third_kernel, sizes, rank_z, count), outs, [VM] * (count + 3)
        )(*blocks, coefs, row, u)
    else:
        (mixed,) = call(functools.partial(mix_kernel, sizes, count), outs[:1], [VM] * count)(*blocks)
        mixed = mixed.reshape(rows_x, rows_y, width)
        core = lax.psum(jnp.einsum("xyk,yb->xbk", mixed, basis_y, precision=HIGH), "gy")
        mixed = jnp.einsum("xbk,yb->xyk", core, basis_y, precision=HIGH).reshape(size, width)
        (sums,) = call(functools.partial(settle_kernel, rank_z), outs[1:], [VM] * 4)(mixed, coefs, row, u)
    (recon,) = call(functools.partial(decode_kernel, dims), [(block, f32)], [VM] * 2)(mixed, t)
    if peers > 64:
        sums = lax.psum(sums[0], ("gx", "gy"))
    else:
        sums = jnp.sum(lax.all_to_all(sums, ("gx", "gy"), 0, 0, tiled=True), axis=0)
    residual = jnp.sqrt(sums[:nv] / (sums[nv : 2 * nv] + 1e-06))
    return (state.reshape(dims), recon.reshape(dims), residual)


def solution(mesh):
    return jax.shard_map(
        program,
        mesh=mesh,
        in_specs=(
            P(None, "gx", "gy", None),
            P(),
            P(),
            P(),
            P(),
            P("gx", None),
            P("gy", None),
            P(),
            P(),
        ),
        out_specs=(P(None, "gx", "gy", None), P(None, "gx", "gy", None), P()),
        check_vma=False,
    )
```

time: 50.7 us -> 43.1 us (0.85)
  Pallas kernels: 14.5 us -> 9.82 us
  local copies, waits for them, and re-layouts: 2.91 us -> 1.17 us
  starting transfers between devices: 22 us -> 21 us
    ppermute x2 -> x0, starting transfers between devices: 4.99 us -> none  [the longest x1 4.34 us: program(): c1 = lax.ppermute(c1, 'gy', pairs(gy, 0))]
    all_to_all x1, starting transfers between devices: 6.37 us -> 9.5 us  [program(): sums = jnp.sum(lax.all_to_all(sums, ('gx', 'gy'), 0, 0, tiled=True), axis=0)]
    pallas_call x6, Pallas kernels: 10.6 us -> 7.56 us  [the longest x1 2.32 us: program(): call(functools.partial(first_kernel, dims), [(block, f32), ((2, nv * lane...]
    unnamed x20 -> x16, local copies, waits for them, and re-layouts: 2.91 us -> 1.17 us
    pallas_call x1, Pallas kernels: 3.89 us -> 2.26 us  [program(): call(functools.partial(second_kernel, dims), [(block, f32), (message_shap...]
    ppermute x1, waiting for transfers between devices: 0.01 us -> 0.73 us  [program(): y1 = lax.ppermute(p1, 'gy', pairs(gy, 0))]
    ppermute x3, starting transfers between devices: 6.14 us -> 6.71 us  [gather_blocks(): blocks = blocks + [lax.ppermute(b, 'gx', swaps) for b in blocks]]
    ppermute x3, waiting for transfers between devices: 3.5 us -> 2.97 us  [gather_blocks(): blocks = blocks + [lax.ppermute(b, 'gx', swaps) for b in blocks]]
  transfers between devices with their start and end apart: 10 -> 8, of which waited for: 3 -> 4; matrix products, arithmetic and copies ran while one was open for 0% -> 0% of each run, Pallas kernels for 16% -> 13%
where the time goes in v5:
time: 43.1 us; the launch traced here: 42.9 us
  starting transfers between devices  21 us (49%)
  Pallas kernels  9.82 us (23%)
  waiting for transfers between devices  9.47 us (22%)
  local copies, waits for them, and re-layouts  1.17 us (3%)
  between operations  0.8 us (2%)
  other arithmetic  0.65 us (2%)
    all_to_all x1, starting transfers between devices, program(): sums = jnp.sum(lax.all_to_all(sums, ('gx', 'gy'), 0, 0, tiled=True), axis=0)  9.5 us
    ppermute x3, starting transfers between devices, gather_blocks(): blocks = blocks + [lax.ppermute(b, 'gx', swaps) for b in blocks]  6.71 us
    all_to_all x1, waiting for transfers between devices, program(): sums = jnp.sum(lax.all_to_all(sums, ('gx', 'gy'), 0, 0, tiled=True), axis=0)  5.49 us
    ppermute x3, waiting for transfers between devices, gather_blocks(): blocks = blocks + [lax.ppermute(b, 'gx', swaps) for b in blocks]  2.97 us
    ppermute x1, starting transfers between devices, program(): y1 = lax.ppermute(p1, 'gy', pairs(gy, 0))  2.93 us
    pallas_call x1, Pallas kernels, program(): call(functools.partial(first_kernel, dims), [(block, f32), ((2, nv * lane...  2.32 us
    pallas_call x1, Pallas kernels, program(): call(functools.partial(second_kernel, dims), [(block, f32), (message_shap...  2.26 us
    pallas_call x1, Pallas kernels, program(): call(functools.partial(side_kernel, dims, rank_z), [(block, f32), ((size,...  1.81 us
  transfers between devices with their start and end apart: 8, of which 4 were waited for; matrix products, arithmetic and copies ran while one was open for 0% of the time, Pallas kernels for 13%

profile of v5, /device:TPU:0, one launch (start us, length us, event | category | flops | bytes accessed | tf_op | source)
XLA Modules:
  0.0 42.9 jit_solution(2607160779748138168)
XLA Ops:
  0.6 0.0 copy-start.6
  0.6 0.0 copy-start.5
  0.7 0.0 copy-start.7
  0.7 0.0 copy-start
  0.7 1.1 %copy-done = f32[12,16,8,128]{3,2,1,0:T(8,128)S(1)} copy-done((f32[12,16,8,128]{3,2,1,0:T(8,128)S(1)}, f32[12,16,8,128]{3,2,1,0:T(8,128)}, u32[]{:S(2)}) %copy-start) | copy-done | bytes 786456
  1.8 0.0 copy-start.1
  1.8 0.0 copy-start.2
  1.8 0.0 copy-start.4
  1.8 0.0 copy-start.3
  1.9 0.6 %collective-permute-start = (f32[192,128]{1,0:T(8,128)S(1)}, f32[192,128]{1,0:T(8,128)S(1)}, u32[]{:S(2)}, u32[]{:S(2)}) collective-permute-start(f32[192,128]{1,0:T(8,128)S(1)} %get-tuple-element.21), channel_id=1, source_target_pairs={{0,8},{16,24},{8,0},{24,16},{1,9},{17,25},{9,1},{25,17},{2,10},{18... | collective-permute-start | bytes 294920 | tf_op jit(solution)/shard_map/ppermute | solution.py:421
  2.4 0.7 %collective-permute-start.1 = (f32[192,128]{1,0:T(8,128)S(1)}, f32[192,128]{1,0:T(8,128)S(1)}, u32[]{:S(2)}, u32[]{:S(2)}) collective-permute-start(f32[192,128]{1,0:T(8,128)S(1)} %get-tuple-element.22), channel_id=1, source_target_pairs={{8,16},{16,8},{9,17},{17,9},{10,18},{18,10},{11,19},{19,11},{12,20... | collective-permute-start | bytes 294920 | tf_op jit(solution)/shard_map/ppermute | solution.py:422
  3.1 0.3 collective-permute-done.x1
  3.4 0.0 collective-permute-done.1.x2
  3.4 0.1 shard_map.105
  3.5 2.9 %collective-permute-start.2 = (f32[408,128]{1,0:T(8,128)S(1)}, f32[408,128]{1,0:T(8,128)S(1)}, u32[]{:S(2)}, u32[]{:S(2)}) collective-permute-start(f32[408,128]{1,0:T(8,128)S(1)} %get-tuple-element.24), channel_id=1, source_target_pairs={{0,1},{2,3},{4,5},{6,7},{1,0},{3,2},{5,4},{7,6},{8,9},{10,11},{12,... | collective-permute-start | bytes 626696 | tf_op jit(solution)/shard_map/ppermute | solution.py:424
  6.4 0.7 %collective-permute-start.3 = (f32[408,128]{1,0:T(8,128)S(1)}, f32[408,128]{1,0:T(8,128)S(1)}, u32[]{:S(2)}, u32[]{:S(2)}) collective-permute-start(f32[408,128]{1,0:T(8,128)S(1)} %get-tuple-element.25), channel_id=1, source_target_pairs={{1,2},{3,4},{5,6},{2,1},{4,3},{6,5},{9,10},{11,12},{13,14},{10,9},... | collective-permute-start | bytes 626696 | tf_op jit(solution)/shard_map/ppermute | solution.py:425
  7.0 0.0 copy-done.6
  7.1 0.0 copy-done.5
  7.1 0.0 copy-done.7
  7.1 0.0 copy-done.1
  7.1 0.0 copy-done.2
  7.1 0.0 copy-done.4
  7.1 2.3 %shard_map.104 = (f32[1536,128]{1,0:T(8,128)S(1)}, bf16[2,1536,192]{2,1,0:T(8,128)(2,1)S(1)}, bf16[2,192,1536]{2,1,0:T(8,128)(2,1)S(1)}, bf16[2,192,384]{2,1,0:T...) custom-call(f32[1536,128]{1,0:T(8,128)S(1)} %bitcast.10, ...), custom_call_target="tpu_custom_call" | custom-call | flops 10000000 | bytes 1000000 | tf_op jit(solution)/shard_map/pallas_call | solution.py:427
  9.4 0.7 %collective-permute-done.2.y1 = f32[408,128]{1,0:T(8,128)S(1)} collective-permute-done((f32[408,128]{1,0:T(8,128)S(1)}, f32[408,128]{1,0:T(8,128)S(1)}, u32[]{:S(2)}, u32[]{:S(2)}) %collective-permute-start.2) | collective-permute-done | bytes 208928 | tf_op jit(solution)/shard_map/ppermute | solution.py:424
  10.2 0.0 collective-permute-done.3.y2
  10.2 0.0 copy-done.3
  10.2 2.3 %shard_map.106 = (f32[1536,128]{1,0:T(8,128)S(1)}, f32[200,128]{1,0:T(8,128)S(1)}) custom-call(f32[1536,128]{1,0:T(8,128)S(1)} %bitcast.11, f32[1536,128]{1,0:T(8,128)S(1)} %get-tuple-element.23.s_ref, f32[408,128]{1,0:T(8,128)S(1)} %collective-permute-done.2.y1, f32[408,128]{1,0:T(8,128)S(1)} %collective-permute-done.3.y2, ...), custom_call_target="tpu_custom_call" | custom-call | flops 10000000 | bytes 1000000 | tf_op jit(solution)/shard_map/pallas_call | solution.py:440
  12.4 6.7 %collective-permute-start.4 = (f32[200,128]{1,0:T(8,128)S(1)}, f32[200,128]{1,0:T(8,128)S(1)}, u32[]{:S(2)}, u32[]{:S(2)}) collective-permute-start(f32[200,128]{1,0:T(8,128)S(1)} %get-tuple-element.32.refs_0_), channel_id=1, source_target_pairs={{0,16},{8,24},{16,0},{24,8},{1,17},{9,25},{17,1},{25,9},{2,18},{10... | collective-permute-start | bytes 307208 | tf_op jit(solution)/shard_map/ppermute | solution.py:402
  19.1 0.0 collective-permute-start.5
  19.1 3.0 %collective-permute-done.4.refs_1_ = f32[200,128]{1,0:T(8,128)S(1)} collective-permute-done((f32[200,128]{1,0:T(8,128)S(1)}, f32[200,128]{1,0:T(8,128)S(1)}, u32[]{:S(2)}, u32[]{:S(2)}) %collective-permute-start.4) | collective-permute-done | bytes 102432 | tf_op jit(solution)/shard_map/ppermute | solution.py:402
  22.1 0.0 collective-permute-start.6
  22.1 1.8 %shard_map.107 = (f32[1536,128]{1,0:T(8,128)}, f32[128,384]{1,0:T(8,128)S(1)}, f32[8,128]{1,0:T(8,128)S(1)}) custom-call(f32[1536,128]{1,0:T(8,128)S(1)} %get-tuple-element.29.state_ref, bf16[2,512,128]{2,1,0:T(8,128)(2,1)S(1)} %get-tuple-element.30.n_ref), custom_call_target="tpu_custom_call" | custom-call | flops 10000000 | bytes 1000000 | tf_op jit(solution)/shard_map/pallas_call | solution.py:452
  23.9 0.0 collective-permute-done.5.refs_2_
  23.9 0.0 collective-permute-done.6.refs_3_
  23.9 1.7 %shard_map.108 = (f32[128,192]{1,0:T(8,128)S(1)}, f32[32,128]{1,0:T(8,128)}) custom-call(f32[200,128]{1,0:T(8,128)S(1)} %get-tuple-element.32.refs_0_, f32[200,128]{1,0:T(8,128)S(1)} %collective-permute-done.4.refs_1_, f32[200,128]{1,0:T(8,128)S(1)} %collective-permute-done.5.refs_2_, f32[200,128]{1,0:T(8,128)S(1)} %collective-permute-done.6.refs_3_, ...), custom_call_target="tpu_custom_call" | custom-call | flops 10000000 | bytes 1000000 | tf_op jit(solution)/shard_map/pallas_call | solution.py:462
  25.6 9.5 %all-to-all-start = ((f32[32,1,128]{2,1,0:T(1,128)}), f32[32,1,128]{2,1,0:T(1,128)S(1)}, u32[]{:S(2)}, u32[]{:S(2)}) async-start(f32[32,1,128]{2,1,0:T(1,128)} %bitcast.6), calls=%async_computation | async-start | bytes 32768 | tf_op jit(solution)/shard_map/all_to_all | solution.py:475
  35.1 1.7 %shard_map.109 = f32[1536,128]{1,0:T(8,128)} custom-call(f32[128,192]{1,0:T(8,128)S(1)} %get-tuple-element.36.d_ref, bf16[2,192,1536]{2,1,0:T(8,128)(2,1)S(1)} %get-tuple-element.37.t_ref), custom_call_target="tpu_custom_call" | custom-call | flops 10000000 | bytes 1000000 | tf_op jit(solution)/shard_map/pallas_call | solution.py:471
  36.8 5.5 %all-to-all-done = f32[32,1,128]{2,1,0:T(1,128)S(1)} async-done(((f32[32,1,128]{2,1,0:T(1,128)}), f32[32,1,128]{2,1,0:T(1,128)S(1)}, u32[]{:S(2)}, u32[]{:S(2)}) %all-to-all-start) | async-done | bytes 16416 | tf_op jit(solution)/shard_map/all_to_all | solution.py:475
  42.3 0.1 reduce_sum.9
  42.3 0.6 %fusion = f32[12]{0:T(128)} fusion(f32[128]{0:T(128)S(1)} %reduce_sum.9), kind=kLoop, calls=%fused_computation.1 | loop fusion | flops 24 | bytes 144 | tf_op jit(solution)/shard_map/sqrt | solution.py:476
  (1 shorter events, 0.0 us)
Async XLA Ops:
  0.6 6.4 %copy-start.6 = (f32[12]{0:T(128)S(1)}, f32[12]{0:T(128)}, u32[]{:S(2)}) copy-start(f32[12]{0:T(128)} %act.3) | copy-start | bytes 148
  0.6 6.4 %copy-start.5 = (f32[12]{0:T(128)S(1)}, f32[12]{0:T(128)}, u32[]{:S(2)}) copy-start(f32[12]{0:T(128)} %dif.3) | copy-start | bytes 148
  0.7 6.4 %copy-start.7 = (f32[12]{0:T(128)S(1)}, f32[12]{0:T(128)}, u32[]{:S(2)}) copy-start(f32[12]{0:T(128)} %pre.1) | copy-start | bytes 148
  0.7 1.2 %copy-start = (f32[12,16,8,128]{3,2,1,0:T(8,128)S(1)}, f32[12,16,8,128]{3,2,1,0:T(8,128)}, u32[]{:S(2)}) copy-start(f32[12,16,8,128]{3,2,1,0:T(8,128)} %param.9) | copy-start | bytes 2359300
  1.8 5.3 %copy-start.1 = (f32[128,32]{0,1:T(8,128)S(1)}, f32[128,32]{0,1:T(8,128)}, u32[]{:S(2)}) copy-start(f32[128,32]{0,1:T(8,128)} %param.15) | copy-start | bytes 49156
  1.8 5.3 %copy-start.2 = (f32[12,12]{1,0:T(8,128)S(1)}, f32[12,12]{1,0:T(8,128)}, u32[]{:S(2)}) copy-start(f32[12,12]{1,0:T(8,128)} %mix_ref.1) | copy-start | bytes 1732
  1.8 5.3 %copy-start.4 = (f32[12,6]{0,1:T(8,128)S(1)}, f32[12,6]{0,1:T(8,128)}, u32[]{:S(2)}) copy-start(f32[12,6]{0,1:T(8,128)} %param.16) | copy-start | bytes 868
  1.8 8.3 %copy-start.3 = (f32[16,64]{1,0:T(8,128)S(1)}, f32[16,64]{1,0:T(8,128)}, u32[]{:S(2)}) copy-start(f32[16,64]{1,0:T(8,128)} %bx_ref.1) | copy-start | bytes 12292
  1.9 1.5 %collective-permute-start = (f32[192,128]{1,0:T(8,128)S(1)}, f32[192,128]{1,0:T(8,128)S(1)}, u32[]{:S(2)}, u32[]{:S(2)}) collective-permute-start(f32[192,128]{1,0:T(8,128)S(1)} %get-tuple-element.21), channel_id=1, source_target_pairs={{0,8},{16,24},{8,0},{24,16},{1,9},{17,25},{9,1},{25,17},{2,10},{18... | collective-permute-start | bytes 294920 | tf_op jit(solution)/shard_map/ppermute | solution.py:421
  2.4 0.9 %collective-permute-start.1 = (f32[192,128]{1,0:T(8,128)S(1)}, f32[192,128]{1,0:T(8,128)S(1)}, u32[]{:S(2)}, u32[]{:S(2)}) collective-permute-start(f32[192,128]{1,0:T(8,128)S(1)} %get-tuple-element.22), channel_id=1, source_target_pairs={{8,16},{16,8},{9,17},{17,9},{10,18},{18,10},{11,19},{19,11},{12,20... | collective-permute-start | bytes 294920 | tf_op jit(solution)/shard_map/ppermute | solution.py:422
  3.5 6.7 %collective-permute-start.2 = (f32[408,128]{1,0:T(8,128)S(1)}, f32[408,128]{1,0:T(8,128)S(1)}, u32[]{:S(2)}, u32[]{:S(2)}) collective-permute-start(f32[408,128]{1,0:T(8,128)S(1)} %get-tuple-element.24), channel_id=1, source_target_pairs={{0,1},{2,3},{4,5},{6,7},{1,0},{3,2},{5,4},{7,6},{8,9},{10,11},{12,... | collective-permute-start | bytes 626696 | tf_op jit(solution)/shard_map/ppermute | solution.py:424
  6.4 3.8 %collective-permute-start.3 = (f32[408,128]{1,0:T(8,128)S(1)}, f32[408,128]{1,0:T(8,128)S(1)}, u32[]{:S(2)}, u32[]{:S(2)}) collective-permute-start(f32[408,128]{1,0:T(8,128)S(1)} %get-tuple-element.25), channel_id=1, source_target_pairs={{1,2},{3,4},{5,6},{2,1},{4,3},{6,5},{9,10},{11,12},{13,14},{10,9},... | collective-permute-start | bytes 626696 | tf_op jit(solution)/shard_map/ppermute | solution.py:425
  12.4 9.7 %collective-permute-start.4 = (f32[200,128]{1,0:T(8,128)S(1)}, f32[200,128]{1,0:T(8,128)S(1)}, u32[]{:S(2)}, u32[]{:S(2)}) collective-permute-start(f32[200,128]{1,0:T(8,128)S(1)} %get-tuple-element.32.refs_0_), channel_id=1, source_target_pairs={{0,16},{8,24},{16,0},{24,8},{1,17},{9,25},{17,1},{25,9},{2,18},{10... | collective-permute-start | bytes 307208 | tf_op jit(solution)/shard_map/ppermute | solution.py:402
  19.1 4.8 %collective-permute-start.5 = (f32[200,128]{1,0:T(8,128)S(1)}, f32[200,128]{1,0:T(8,128)S(1)}, u32[]{:S(2)}, u32[]{:S(2)}) collective-permute-start(f32[200,128]{1,0:T(8,128)S(1)} %get-tuple-element.32.refs_0_), channel_id=1, source_target_pairs={{0,8},{8,0},{16,24},{24,16},{1,9},{9,1},{17,25},{25,17},{2,10},{10... | collective-permute-start | bytes 307208 | tf_op jit(solution)/shard_map/ppermute | solution.py:402
  22.1 1.8 %collective-permute-start.6 = (f32[200,128]{1,0:T(8,128)S(1)}, f32[200,128]{1,0:T(8,128)S(1)}, u32[]{:S(2)}, u32[]{:S(2)}) collective-permute-start(f32[200,128]{1,0:T(8,128)S(1)} %collective-permute-done.4.refs_1_), channel_id=1, source_target_pairs={{0,8},{8,0},{16,24},{24,16},{1,9},{9,1},{17,25},{25,17},{2,10},{10... | collective-permute-start | bytes 307208 | tf_op jit(solution)/shard_map/ppermute | solution.py:402
  25.6 16.7 %all-to-all-start = ((f32[32,1,128]{2,1,0:T(1,128)}), f32[32,1,128]{2,1,0:T(1,128)S(1)}, u32[]{:S(2)}, u32[]{:S(2)}) async-start(f32[32,1,128]{2,1,0:T(1,128)} %bitcast.6), calls=%async_computation | async-start | bytes 32768 | tf_op jit(solution)/shard_map/all_to_all | solution.py:475

commit v6 on v5

--- a/solution.py
+++ b/solution.py
@@ -101,19 +101,30 @@
     return jnp.where(is_odd, a, b), jnp.where(is_odd, b, a)
 
 
-def pack_x_kernel(dims, f_ref, q1, q2):
+def far_side():
+    return odd("gx")
+
+
+def pack_x_kernel(dims, f_ref, q1, q2, low_ref, high_ref, sem):
     nv, rows_x, rows_y, _ = dims
-    size = rows_x * rows_y
+    reads = [
+        pltpu.make_async_copy(f_ref.at[:, pl.ds(0, 2)], low_ref, sem.at[0]),
+        pltpu.make_async_copy(f_ref.at[:, pl.ds(rows_x - 2, 2)], high_ref, sem.at[1]),
+    ]
+    for read in reads:
+        read.start()
+    for read in reads:
+        read.wait()
+    is_odd = odd("gx")
     for layer in range(2):
         for v in range(nv):
-            low = f_ref[pl.ds(v * size + layer * rows_y, rows_y), :]
-            high = f_ref[pl.ds(v * size + (rows_x - 1 - layer) * rows_y, rows_y), :]
+            low, high = low_ref[v, layer], high_ref[v, 1 - layer]
             at = pl.ds((layer * nv + v) * rows_y, rows_y)
-            q1[at, :] = jnp.where(odd("gx"), low, high)
-            q2[at, :] = jnp.where(odd("gx"), high, low)
-
-
-def pack_y_kernel(dims, f_ref, x1, x2, p1, p2):
+            q1[at, :] = jnp.where(is_odd, low, high)
+            q2[at, :] = jnp.where(is_odd, high, low)
+
+
+def pack_y_kernel(dims, f_ref, x1, p1, p2):
     nv, rows_x, rows_y, _ = dims
     size = rows_x * rows_y
 
@@ -126,13 +137,11 @@
             low = f_ref[pl.ds(v * size + layer, rows_x, stride=rows_y), :]
             high = f_ref[pl.ds(v * size + rows_y - 1 - layer, rows_x, stride=rows_y), :]
             put(pl.ds((layer * nv + v) * rows_x, rows_x), low, high)
-    lows = two(x1, x2, odd("gx"), pl.ds(0, nv, stride=rows_y))
-    highs = two(x1, x2, odd("gx"), pl.ds(rows_y - 1, nv, stride=rows_y))
-    for side in range(2):
-        put(pl.ds((2 * rows_x + side) * nv, nv), lows[side], highs[side])
-
-
-def first_kernel(dims, f_ref, x1, x2, bz_ref, bv_ref, mix_ref, dif, pre, act, *outs):
+    low, high = [x1[pl.ds(y, nv, stride=rows_y), :] for y in (0, rows_y - 1)]
+    put(pl.ds(2 * rows_x * nv, nv), low, high)
+
+
+def first_kernel(dims, f_ref, bz_ref, bv_ref, mix_ref, dif, pre, act, *outs):
     s_ref, k_ref, t_ref, u_ref, n_ref, both_ref, low_ref = outs
     nv, rows_x, rows_y, lanes = dims
     size = rows_x * rows_y
@@ -153,10 +162,10 @@
     def emit(v, x, n, w, t):
         s_ref[pl.ds(v * size + x * rows_y, n * rows_y), :] = (w + t).reshape(n * rows_y, lanes)
 
-    def edge(side):
-        return lambda v: two(x1, x2, odd("gx"), pl.ds(v * rows_y, rows_y))[side]
-
-    stage(f_ref, nv, rows_x, rows_y, dif, act, (both, lo), emit, edge(0), edge(1))
+    def nothing(v):
+        return jnp.zeros((rows_y, lanes), jnp.float32)
+
+    stage(f_ref, nv, rows_x, rows_y, dif, act, (both, lo), emit, nothing, nothing)
     bz, bv = bz_ref[...], bv_ref[...]
     rank_z, rank_v = bz.shape[0], bv.shape[0]
     width, part = rank_z * rank_v, nv * rank_z
@@ -201,8 +210,11 @@
     def x_ghost(layer, v):
         return jnp.stack(two(x1, x2, odd("gx"), pl.ds((layer * nv + v) * rows_y, rows_y)))
 
-    def corner(side, v):
-        return two(y1, y2, odd("gy"), pl.ds((2 * rows_x + side) * nv + v, 1))
+    far = far_side()
+
+    def corners(v):
+        near = two(y1, y2, odd("gy"), pl.ds(2 * rows_x * nv + v, 1))
+        return [jnp.where(far, a, 0.0) for a in near], [jnp.where(far, 0.0, a) for a in near]
 
     def keep(value, flags):
         inside = [jnp.where(flags[i], value[i], 0.0) for i in range(2)]
@@ -216,7 +228,7 @@
         cut = g.size // (8 * lanes)
         low = f_ref[pl.ds(v * size, rows_x, stride=rows_y), :]
         high = f_ref[pl.ds(v * size + rows_y - 1, rows_x, stride=rows_y), :]
-        left, right = corner(0, v), corner(1, v)
+        left, right = corners(v)
         lap = y_ghost(1, v) + jnp.stack([low, high]) - 6.0 * g
         lap = lap + shifted(g, 1, jnp.stack(left), jnp.stack(right)) + shifted(g, 2)
         out = g + (dif[v] * lap + made[v][:cut].reshape(g.shape))
@@ -235,6 +247,10 @@
         lap = lap + shifted(g, 1, before, after) + shifted(g, 2)
         out = g + (dif[v] * lap + made[v][cut:].reshape(g.shape))
         gx_ref[pl.ds(v * 2 * rows_y, 2 * rows_y), :] = keep(out, has_x)
+        at = pl.ds(v * size, rows_y)
+        sec[at, :] = sec[at, :] + dif[v] * g[0]
+        at = pl.ds(v * size + size - rows_y, rows_y)
+        sec[at, :] = sec[at, :] + dif[v] * g[1]
 
     def emit(v, x, n, w, t):
         at = pl.ds(v * size + x * rows_y, n * rows_y)
@@ -246,27 +262,38 @@
         lambda v: gx_ref[pl.ds((v * 2 + 1) * rows_y, rows_y), :],
     )
     his, los = [], []
+    edge = jnp.where(far, rows_x - 1, 0)
     for v in range(nv):
         half = 0.5 * dif[v]
         at = pl.ds(v * size, rows_x, stride=rows_y)
         state_ref[at, :] = state_ref[at, :] + half * gy_ref[pl.ds(v * 2 * rows_x, rows_x), :]
         at = pl.ds(v * size + rows_y - 1, rows_x, stride=rows_y)
         state_ref[at, :] = state_ref[at, :] + half * gy_ref[pl.ds((v * 2 + 1) * rows_x, rows_x), :]
-        hi, lo = split(state_ref[pl.ds(v * size, size), :])
+        ends = [dif[v] * dif[v] * a for a in two(y1, y2, odd("gy"), pl.ds(v * rows_x + edge, 1))]
+        for end in range(2):
+            m_ref[pl.ds(spots(dims, k_ref.shape[2], bx_ref.shape[1])[2] + end * nv + v, 1), :] = ends[end]
+        lack = jnp.concatenate([ends_tile(*ends, rows_y), jnp.zeros((-rows_y % 16, lanes), jnp.float32)], axis=0)
+        hi, lo = split(jnp.concatenate([state_ref[pl.ds(v * size, size), :], lack], axis=0))
         his.append(hi)
         los.append(lo)
     total = mm3((jnp.concatenate(his, 1), jnp.concatenate(los, 1)), (k_ref[0], k_ref[1]))
-    pack_message(m_ref, total, bx_ref[...])
-
-
-def dense(size, width, rows_x, rank_x, lanes):
-    return width % lanes * 2 == lanes and rank_x * 2 == lanes and size % 16 == 0 and rows_x % 16 == 0
-
-
-def message_shape(size, width, rows_x, rank_x, lanes):
-    if not dense(size, width, rows_x, rank_x, lanes):
-        return (size + rows_x, max(width, rank_x))
-    return (size * (width // lanes) + size // 2 + rows_x // 2, lanes)
+    pack_message(dims, m_ref, total[:size], bx_ref[...], total[size : size + rows_y])
+
+
+def ends_tile(first, last, rows):
+    shape = (rows, first.shape[1])
+    return jnp.where(place(shape, 0) == 0, first, jnp.where(place(shape, 0) == rows - 1, last, 0.0))
+
+
+def spots(dims, width, rank_x):
+    nv, rows_x, rows_y, lanes = dims
+    size = rows_x * rows_y
+    assert width % lanes * 2 == lanes and rank_x * 2 == lanes
+    tail = width // lanes * size
+    basis = tail + size // 2
+    ends = basis + rows_x // 2
+    made = ends + 2 * nv
+    return tail, basis, ends, made, made + -(-(width // lanes * 2 + 1) // 8) * 8
 
 
 def fold(a):
@@ -279,110 +306,200 @@
     return jnp.concatenate([a[:, :half], a[:, half:]], axis=0)
 
 
-def pack_message(m_ref, values, basis):
+def pack_message(dims, m_ref, values, basis, ends):
+    _, rows_x, rows_y, lanes = dims
     size, width = values.shape
-    lanes = m_ref.shape[1]
-    if not dense(size, width, *basis.shape, lanes):
-        m_ref[:size, :width] = values
-        m_ref[size:, : basis.shape[1]] = basis
-        return
+    tail, base, _, made, _ = spots(dims, width, basis.shape[1])
     whole = width // lanes
     for i in range(whole):
         m_ref[pl.ds(i * size, size), :] = values[:, i * lanes : (i + 1) * lanes]
-    m_ref[pl.ds(whole * size, size // 2), :] = fold(values[:, whole * lanes :])
-    m_ref[pl.ds(whole * size + size // 2, basis.shape[0] // 2), :] = fold(basis)
-
-
-def unpack_message(m_ref, size, width, rows_x, rank_x):
-    lanes = m_ref.shape[1]
-    if not dense(size, width, rows_x, rank_x, lanes):
-        return m_ref[:size, :width], m_ref[size:, :rank_x]
+        for end, row in enumerate((0, rows_y - 1)):
+            m_ref[pl.ds(made + 2 * i + end, 1), :] = ends[row : row + 1, i * lanes : (i + 1) * lanes]
+    m_ref[pl.ds(tail, size // 2), :] = fold(values[:, whole * lanes :])
+    m_ref[pl.ds(base, rows_x // 2), :] = fold(basis)
+    rest = [ends[row : row + 1, whole * lanes :] for row in (0, rows_y - 1)]
+    m_ref[pl.ds(made + 2 * whole, 1), :] = jnp.concatenate(rest, axis=1)
+
+
+def unpack_message(dims, m_ref, width, rank_x):
+    _, rows_x, rows_y, lanes = dims
+    size = rows_x * rows_y
+    tail, base, _, made, _ = spots(dims, width, rank_x)
     whole = width // lanes
     parts = [m_ref[pl.ds(i * size, size), :] for i in range(whole)]
-    parts.append(unfold(m_ref[pl.ds(whole * size, size // 2), :]))
-    basis = unfold(m_ref[pl.ds(whole * size + size // 2, rows_x // 2), :])
-    return jnp.concatenate(parts, axis=1), basis
-
-
-def mix_blocks(sizes, refs):
-    rows_x, rows_y, width, rank_x = sizes
-    size = rows_x * rows_y
+    parts.append(unfold(m_ref[pl.ds(tail, size // 2), :]))
+    basis = unfold(m_ref[pl.ds(base, rows_x // 2), :])
+    rest = m_ref[pl.ds(made + 2 * whole, 1), :]
+    half = lanes // 2
+    ends = [
+        jnp.concatenate(
+            [m_ref[pl.ds(made + 2 * i + end, 1), :] for i in range(whole)] + [rest[:, end * half : (end + 1) * half]],
+            axis=1,
+        )
+        for end in range(2)
+    ]
+    return jnp.concatenate(parts, axis=1), basis, ends_tile(*ends, rows_y)
+
+
+def from_far(me, masks, index, items):
+    block = jnp.bitwise_xor(me, masks[index])
+    far = jnp.where(block % 2 == 1, block + 1, block - 1)
+    total = None
+    mask = 3
+    while mask < len(masks):
+        other = masks.index(masks[index] ^ mask)
+        item = jnp.where(far == jnp.bitwise_xor(block, mask), items[other], 0.0)
+        total = item if total is None else total + item
+        mask = 2 * mask + 1
+    return total
+
+
+def mix_blocks(dims, width, rank_x, masks, refs):
+    _, rows_x, rows_y, _ = dims
+    size = rows_x * rows_y
+    me = lax.axis_index("gx")
 
     def repeated(basis):
         return jnp.broadcast_to(basis[:, None, :], (rows_x, rows_y, rank_x)).reshape(size, rank_x)
 
-    parts = [unpack_message(ref, size, width, rows_x, rank_x) for ref in refs]
-    values = jnp.concatenate([values for values, _ in parts], axis=0)
-    bases = jnp.concatenate([repeated(basis) for _, basis in parts], axis=0)
+    parts = [unpack_message(dims, ref, width, rank_x) for ref in refs]
+    values = []
+    for i, (value, _, _) in enumerate(parts):
+        lack = from_far(me, masks, i, [ends for _, _, ends in parts])
+        if lack is not None:
+            last = jnp.bitwise_xor(me, masks[i]) % 2 == 1
+            top = value[:rows_y] + jnp.where(last, 0.0, lack)
+            bottom = value[size - rows_y :] + jnp.where(last, lack, 0.0)
+            value = jnp.concatenate([top, value[rows_y : size - rows_y], bottom], axis=0)
+        values.append(value)
+    values = jnp.concatenate(values, axis=0)
+    bases = jnp.concatenate([repeated(basis) for _, basis, _ in parts], axis=0)
     hi, lo = split(bases)
     link = mm3((hi[:size], lo[:size]), (hi, lo), True)
     same = place(link.shape, 0) % rows_y == place(link.shape, 1) % rows_y
     return mm3(split(jnp.where(same, link, 0.0)), split(values))
 
 
-def side_kernel(dims, rank_z, state_ref, n_ref, out_ref, w_ref, row_ref, sem):
+def squares(a):
+    return jnp.sum((a * a).reshape(a.shape[0] // 8, 8, a.shape[1]), axis=0)
+
+
+def zero_one(flags):
+    return flags.astype(jnp.float32).astype(jnp.bfloat16)
+
+
+def tally(outside, mass, lanes):
+    hi, lo = split(jnp.concatenate(outside + mass, axis=0))
+    ones = jnp.ones((8, lanes), jnp.bfloat16)
+    hi, lo = split(mm(ones, hi, True) + mm(ones, lo, True))
+    shape = (hi.shape[1], lanes)
+    pick = zero_one(place(shape, 0) // 8 == place(shape, 1))
+    return mm(hi, pick) + mm(lo, pick)
+
+
+def outside_span(state, basis):
+    coefs = mm3(split(state), basis)
+    return coefs, state - mm3(split(coefs), basis, True)
+
+
+def side_kernel(dims, rank_z, state_ref, n_ref, w_ref, row_ref):
     nv, rows_x, rows_y, lanes = dims
     size = rows_x * rows_y
-    write = pltpu.make_async_copy(state_ref, out_ref, sem)
-    write.start()
     held = lanes // rank_z
-    basis = (n_ref[0], n_ref[1])
-
-    def squares(a):
-        return jnp.sum((a * a).reshape(size // 8, 8, lanes), axis=0)
-
+    last = far_side()
     outside, mass = [], []
     for v in range(0, nv, held):
         state = jnp.concatenate([state_ref[pl.ds((v + j) * size, size), :] for j in range(held)], axis=1)
-        coefs = mm3(split(state), basis)
+        top = jnp.where(last, state[:rows_y], 0.0)
+        bottom = jnp.where(last, 0.0, state[size - rows_y :])
+        state = jnp.concatenate([top, state[rows_y : size - rows_y], bottom], axis=0)
+        coefs, rest = outside_span(state, (n_ref[0], n_ref[1]))
         w_ref[:, (v // held) * lanes : (v // held + 1) * lanes] = coefs
-        rest = state - mm3(split(coefs), basis, True)
         for j in range(held):
             outside.append(squares(rest[:, j * lanes : (j + 1) * lanes]))
             mass.append(squares(state[:, j * lanes : (j + 1) * lanes]))
-    every = jnp.concatenate(outside + mass, axis=0)
-    ones = jnp.ones((8, lanes), jnp.float32)
-    sums = lax.dot_general(
-        ones, every, (((1,), (1,)), ((), ())), precision=HIGH, preferred_element_type=jnp.float32
+    row_ref[...] = tally(outside, mass, lanes)
+
+
+def edge_rows(dims, rank_z, state_ref, lack_ref, n_ref):
+    nv, rows_x, rows_y, lanes = dims
+    size = rows_x * rows_y
+    held = lanes // rank_z
+    start = jnp.where(far_side(), size - rows_y, 0)
+    whole = []
+    for v in range(nv):
+        at = pl.ds(pl.multiple_of(v * size + start, rows_y), rows_y)
+        ends = [lack_ref[pl.ds(end * nv + v, 1), :] for end in range(2)]
+        whole.append(state_ref[at, :] + ends_tile(*ends, rows_y))
+    state = jnp.concatenate(
+        [jnp.concatenate(whole[v : v + held], axis=1) for v in range(0, nv, held)], axis=0
     )
-    shape = (every.shape[0], row_ref.shape[1])
-    pick = (place(shape, 0) // 8 == place(shape, 1)).astype(jnp.float32)
-    row_ref[...] = jnp.dot(sums, pick, precision=HIGH, preferred_element_type=jnp.float32)
-    write.wait()
-
-
-def settle(mixed, w_ref, row_ref, u_ref, sums_ref, rank_z):
-    gap = w_ref[...] - mm3(split(mixed), (u_ref[0], u_ref[1]))
-    size, part = gap.shape
-    hi, lo = split(jnp.sum((gap * gap).reshape(size // 8, 8, part), axis=0))
-    shape = (part, row_ref.shape[1])
-    pick = (place(shape, 0) // rank_z == place(shape, 1)).astype(jnp.float32).astype(jnp.bfloat16)
-    row = jnp.sum(mm(hi, pick) + mm(lo, pick), axis=0, keepdims=True) + row_ref[0:1, :]
+    coefs, rest = outside_span(state, (n_ref[0], n_ref[1]))
+    outside = []
+    for v in range(nv):
+        i, j = divmod(v, held)
+        outside.append(squares(rest[i * rows_y : (i + 1) * rows_y, j * lanes : (j + 1) * lanes]))
+    row = tally(outside, [squares(a) for a in whole], lanes)
+    coefs = jnp.concatenate([coefs[i * rows_y : (i + 1) * rows_y] for i in range(nv // held)], axis=1)
+    return coefs, row
+
+
+def settle(dims, rank_z, mixed, lack_ref, state_ref, n_ref, w_ref, row_ref, u_ref, sums_ref):
+    _, _, rows_y, lanes = dims
+    coefs, edge_row = edge_rows(dims, rank_z, state_ref, lack_ref, n_ref)
+    last = far_side()
+    w = w_ref[...]
+    size, part = w.shape
+    top = w[:rows_y] + jnp.where(last, 0.0, coefs)
+    bottom = w[size - rows_y :] + jnp.where(last, coefs, 0.0)
+    w = jnp.concatenate([top, w[rows_y : size - rows_y], bottom], axis=0)
+    gap = w - mm3(split(mixed), (u_ref[0], u_ref[1]))
+    hi, lo = split(squares(gap))
+    shape = (part, lanes)
+    pick = zero_one(place(shape, 0) // rank_z == place(shape, 1))
+    row = jnp.sum(mm(hi, pick) + mm(lo, pick), axis=0, keepdims=True) + row_ref[0:1, :] + edge_row[0:1, :]
     sums_ref[...] = jnp.broadcast_to(row, sums_ref.shape)
 
 
-def third_kernel(sizes, rank_z, n, *refs):
-    w_ref, row_ref, u_ref, d_ref, sums_ref = refs[n:]
-    mixed = mix_blocks(sizes, refs[:n])
+def find_lack(dims, width, rank_x, masks, refs, lack_ref):
+    spot = spots(dims, width, rank_x)[2]
+    rows = [ref[pl.ds(spot, 2 * dims[0]), :] for ref in refs]
+    lack = from_far(lax.axis_index("gx"), masks, 0, rows)
+    lack_ref[...] = jnp.zeros(lack_ref.shape, jnp.float32) if lack is None else lack
+
+
+def third_kernel(dims, rank_z, width, rank_x, masks, *refs):
+    n = len(masks)
+    state_ref, n_ref, w_ref, row_ref, u_ref, d_ref, lack_ref, sums_ref = refs[n:]
+    find_lack(dims, width, rank_x, masks, refs[:n], lack_ref)
+    mixed = mix_blocks(dims, width, rank_x, masks, refs[:n])
     d_ref[...] = mixed
-    settle(mixed, w_ref, row_ref, u_ref, sums_ref, rank_z)
-
-
-def mix_kernel(sizes, n, *refs):
-    refs[n][...] = mix_blocks(sizes, refs[:n])
-
-
-def settle_kernel(rank_z, d_ref, w_ref, row_ref, u_ref, sums_ref):
-    settle(d_ref[...], w_ref, row_ref, u_ref, sums_ref, rank_z)
-
-
-def decode_kernel(dims, d_ref, t_ref, recon_ref):
+    settle(dims, rank_z, mixed, lack_ref, state_ref, n_ref, w_ref, row_ref, u_ref, sums_ref)
+
+
+def mix_kernel(dims, width, rank_x, masks, *refs):
+    n = len(masks)
+    find_lack(dims, width, rank_x, masks, refs[:n], refs[n + 1])
+    refs[n][...] = mix_blocks(dims, width, rank_x, masks, refs[:n])
+
+
+def settle_kernel(dims, rank_z, d_ref, lack_ref, state_ref, n_ref, w_ref, row_ref, u_ref, sums_ref):
+    settle(dims, rank_z, d_ref[...], lack_ref, state_ref, n_ref, w_ref, row_ref, u_ref, sums_ref)
+
+
+def decode_kernel(dims, d_ref, t_ref, lack_ref, state_ref, recon_ref, out_ref):
     nv, rows_x, rows_y, lanes = dims
     size = rows_x * rows_y
     halves = split(d_ref[...])
+    start = jnp.where(far_side(), size - rows_y, 0)
     for v in range(nv):
+        whole = pl.ds(v * size, size)
+        out_ref[whole, :] = state_ref[whole, :]
+        at = pl.ds(pl.multiple_of(v * size + start, rows_y), rows_y)
+        ends = [lack_ref[pl.ds(end * nv + v, 1), :] for end in range(2)]
+        out_ref[at, :] = state_ref[at, :] + ends_tile(*ends, rows_y)
         cols = slice(v * lanes, (v + 1) * lanes)
-        recon_ref[pl.ds(v * size, size), :] = mm3(halves, (t_ref[0, :, cols], t_ref[1, :, cols]))
+        recon_ref[whole, :] = mm3(halves, (t_ref[0, :, cols], t_ref[1, :, cols]))
 
 
 def pairs(n, first):
@@ -392,16 +509,15 @@
 
 def gather_blocks(block):
     n = lax.axis_size("gx")
-    if n & (n - 1):
-        every = lax.all_gather(block, "gx", axis=0)
-        return [block] + [jnp.roll(every, -lax.axis_index("gx"), 0)[i] for i in range(1, n)]
-    blocks = [block]
+    assert n & (n - 1) == 0
+    blocks, masks = [block], [0]
     bit = n // 2
     while bit:
         swaps = [(i, i ^ bit) for i in range(n)]
         blocks = blocks + [lax.ppermute(b, "gx", swaps) for b in blocks]
+        masks = masks + [mask ^ bit for mask in masks]
         bit //= 2
-    return blocks
+    return blocks, tuple(masks)
 
 
 def program(field, diffusion, prefactor, activation, mixing, basis_x, basis_y, basis_z, basis_v):
@@ -416,11 +532,17 @@
     flat = field.reshape(nv * size, lanes)
     block = (nv * size, lanes)
 
-    y_msg, x_msg = (2 * nv * (rows_x + 1), lanes), (2 * nv * rows_y, lanes)
-    q1, q2 = call(functools.partial(pack_x_kernel, dims), [(x_msg, f32)] * 2, [VM])(flat)
+    y_msg, x_msg = (nv * (2 * rows_x + 1), lanes), (2 * nv * rows_y, lanes)
+    edges = (nv, 2, rows_y, lanes)
+    q1, q2 = call(
+        functools.partial(pack_x_kernel, dims),
+        [(x_msg, f32)] * 2,
+        [pl.BlockSpec(memory_space=pltpu.HBM)],
+        [pltpu.VMEM(edges, f32)] * 2 + [pltpu.SemaphoreType.DMA((2,))],
+    )(field)
+    x2 = lax.ppermute(q2, "gx", pairs(gx, 1))
     x1 = lax.ppermute(q1, "gx", pairs(gx, 0))
-    x2 = lax.ppermute(q2, "gx", pairs(gx, 1))
-    p1, p2 = call(functools.partial(pack_y_kernel, dims), [(y_msg, f32)] * 2, [VM] * 3)(flat, x1, x2)
+    p1, p2 = call(functools.partial(pack_y_kernel, dims), [(y_msg, f32)] * 2, [VM] * 2)(flat, x1)
     y1 = lax.ppermute(p1, "gy", pairs(gy, 0))
     y2 = lax.ppermute(p2, "gy", pairs(gy, 1))
 
@@ -435,11 +557,11 @@
             ((nv * 8, nv * 16), bf16),
             ((nv * 8, nv * 8), bf16),
         ],
-        [VM] * 6 + [SM] * 3,
-    )(flat, x1, x2, basis_z.T, basis_v.T, mixing, diffusion, prefactor, activation)
+        [VM] * 4 + [SM] * 3,
+    )(flat, basis_z.T, basis_v.T, mixing, diffusion, prefactor, activation)
     state, message = call(
         functools.partial(second_kernel, dims),
-        [(block, f32), (message_shape(size, width, rows_x, rank_x, lanes), f32)],
+        [(block, f32), ((spots(dims, width, rank_x)[4], lanes), f32)],
         [VM] * 10 + [SM] * 2,
         [
             pltpu.VMEM(block, f32),
@@ -447,28 +569,27 @@
             pltpu.VMEM((nv * 2 * rows_y, lanes), f32),
         ],
     )(flat, section, y1, y2, x1, x2, basis_x, k, both, low, diffusion, activation)
-    blocks = gather_blocks(message)
+    blocks, masks = gather_blocks(message)
     count = len(blocks)
-    state, coefs, row = call(
-        functools.partial(side_kernel, dims, rank_z),
-        [(block, f32), ((size, part), f32), ((8, lanes), f32)],
-        [VM] * 2,
-        [pltpu.SemaphoreType.DMA],
-        out_specs=[pl.BlockSpec(memory_space=pl.ANY), VM, VM],
+    coefs, row = call(
+        functools.partial(side_kernel, dims, rank_z), [((size, part), f32), ((8, lanes), f32)], [VM] * 2
     )(state, n)
-    sizes = (rows_x, rows_y, width, rank_x)
-    outs = [((size, width), f32), ((peers, lanes), f32)]
+    outs = [((size, width), f32), ((2 * nv, lanes), f32), ((peers, lanes), f32)]
+    mixing_args = (width, rank_x, masks)
+    rest = (state, n, coefs, row, u)
     if basis_y.shape[0] * gy == basis_y.shape[1]:
-        mixed, sums = call(
-            functools.partial(third_kernel, sizes, rank_z, count), outs, [VM] * (count + 3)
-        )(*blocks, coefs, row, u)
+        mixed, lack, sums = call(
+            functools.partial(third_kernel, dims, rank_z, *mixing_args), outs, [VM] * (count + 5)
+        )(*blocks, *rest)
     else:
-        (mixed,) = call(functools.partial(mix_kernel, sizes, count), outs[:1], [VM] * count)(*blocks)
+        mixed, lack = call(functools.partial(mix_kernel, dims, *mixing_args), outs[:2], [VM] * count)(*blocks)
         mixed = mixed.reshape(rows_x, rows_y, width)
         core = lax.psum(jnp.einsum("xyk,yb->xbk", mixed, basis_y, precision=HIGH), "gy")
         mixed = jnp.einsum("xbk,yb->xyk", core, basis_y, precision=HIGH).reshape(size, width)
-        (sums,) = call(functools.partial(settle_kernel, rank_z), outs[1:], [VM] * 4)(mixed, coefs, row, u)
-    (recon,) = call(functools.partial(decode_kernel, dims), [(block, f32)], [VM] * 2)(mixed, t)
+        (sums,) = call(functools.partial(settle_kernel, dims, rank_z), outs[2:], [VM] * 7)(
+            mixed, lack, *rest
+        )
+    recon, state = call(functools.partial(decode_kernel, dims), [(block, f32)] * 2, [VM] * 4)(mixed, t, lack, state)
     if peers > 64:
         sums = lax.psum(sums[0], ("gx", "gy"))
     else:

time: 43.1 us -> 40.1 us (0.930)
  starting transfers between devices: 21 us -> 12.3 us
  waiting for transfers between devices: 9.47 us -> 14.9 us
    ppermute x3, starting transfers between devices: 6.71 us -> 1.56 us  [gather_blocks(): blocks = blocks + [lax.ppermute(b, 'gx', swaps) for b in blocks]]
    ppermute x1, waiting for transfers between devices: 0.73 us -> 5.32 us  [program(): y1 = lax.ppermute(p1, 'gy', pairs(gy, 0))]
    all_to_all x1, starting transfers between devices: 9.5 us -> 5.96 us  [program(): sums = jnp.sum(lax.all_to_all(sums, ('gx', 'gy'), 0, 0, tiled=True), axis=0)]
    ppermute x1, waiting for transfers between devices: 0.28 us -> 0.94 us  [program(): x1 = lax.ppermute(q1, 'gx', pairs(gx, 0))]
  transfers between devices with their start and end apart: 8 -> 8, of which waited for: 4 -> 4; matrix products, arithmetic and copies ran while one was open for 0% -> 0% of each run, Pallas kernels for 13% -> 14%
where the time goes in v6:
time: 40.1 us; the launch traced here: 39.9 us
  waiting for transfers between devices  14.9 us (37%)
  starting transfers between devices  12.3 us (31%)
  Pallas kernels  10.1 us (25%)
  local copies, waits for them, and re-layouts  1.15 us (3%)
  between operations  0.78 us (2%)
  other arithmetic  0.65 us (2%)
    all_to_all x1, starting transfers between devices, program(): sums = jnp.sum(lax.all_to_all(sums, ('gx', 'gy'), 0, 0, tiled=True), axis=0)  5.96 us
    ppermute x1, waiting for transfers between devices, program(): y1 = lax.ppermute(p1, 'gy', pairs(gy, 0))  5.32 us
    all_to_all x1, waiting for transfers between devices, program(): sums = jnp.sum(lax.all_to_all(sums, ('gx', 'gy'), 0, 0, tiled=True), axis=0)  5.29 us
    ppermute x3, waiting for transfers between devices, gather_blocks(): blocks = blocks + [lax.ppermute(b, 'gx', swaps) for b in blocks]  3.35 us
    ppermute x1, starting transfers between devices, program(): y1 = lax.ppermute(p1, 'gy', pairs(gy, 0))  2.93 us
    pallas_call x1, Pallas kernels, program(): call(functools.partial(second_kernel, dims), [(block, f32), ((spots(dims,...  2.33 us
    pallas_call x1, Pallas kernels, program(): call(functools.partial(first_kernel, dims), [(block, f32), ((2, nv * lane...  2.3 us
    pallas_call x1, Pallas kernels, program(): call(functools.partial(third_kernel, dims, rank_z, *mixing_args), outs, [...  2.02 us
  transfers between devices with their start and end apart: 8, of which 4 were waited for; matrix products, arithmetic and copies ran while one was open for 0% of the time, Pallas kernels for 14%

profile of v6, /device:TPU:0, one launch (start us, length us, event | category | flops | bytes accessed | tf_op | source)
XLA Modules:
  0.0 39.9 jit_solution(11119479227097715812)
XLA Ops:
  0.6 0.0 copy-start
  0.6 1.1 %copy-done = f32[12,16,8,128]{3,2,1,0:T(8,128)S(1)} copy-done((f32[12,16,8,128]{3,2,1,0:T(8,128)S(1)}, f32[12,16,8,128]{3,2,1,0:T(8,128)}, u32[]{:S(2)}) %copy-start) | copy-done | bytes 786456
  1.8 0.0 copy-start.1
  1.8 0.0 copy-start.2
  1.8 0.0 copy-start.4
  1.8 0.0 copy-start.5
  1.8 0.0 copy-start.6
  1.8 0.0 copy-start.7
  1.8 0.0 copy-start.3
  1.8 0.1 shard_map.104
  1.9 0.6 %collective-permute-start = (f32[192,128]{1,0:T(8,128)S(1)}, f32[192,128]{1,0:T(8,128)S(1)}, u32[]{:S(2)}, u32[]{:S(2)}) collective-permute-start(f32[192,128]{1,0:T(8,128)S(1)} %get-tuple-element.24), channel_id=1, source_target_pairs={{0,8},{16,24},{8,0},{24,16},{1,9},{17,25},{9,1},{25,17},{2,10},{18... | collective-permute-start | bytes 294920 | tf_op jit(solution)/shard_map/ppermute | solution.py:544
  2.5 0.9 %collective-permute-done.x1 = f32[192,128]{1,0:T(8,128)S(1)} collective-permute-done((f32[192,128]{1,0:T(8,128)S(1)}, f32[192,128]{1,0:T(8,128)S(1)}, u32[]{:S(2)}, u32[]{:S(2)}) %collective-permute-start) | collective-permute-done | bytes 98336 | tf_op jit(solution)/shard_map/ppermute | solution.py:544
  3.4 0.1 shard_map.105
  3.5 2.9 %collective-permute-start.1 = (f32[396,128]{1,0:T(8,128)S(1)}, f32[396,128]{1,0:T(8,128)S(1)}, u32[]{:S(2)}, u32[]{:S(2)}) collective-permute-start(f32[396,128]{1,0:T(8,128)S(1)} %get-tuple-element.25), channel_id=1, source_target_pairs={{0,1},{2,3},{4,5},{6,7},{1,0},{3,2},{5,4},{7,6},{8,9},{10,11},{12,... | collective-permute-start | bytes 608264 | tf_op jit(solution)/shard_map/ppermute | solution.py:546
  6.4 0.7 %collective-permute-start.2 = (f32[396,128]{1,0:T(8,128)S(1)}, f32[396,128]{1,0:T(8,128)S(1)}, u32[]{:S(2)}, u32[]{:S(2)}) collective-permute-start(f32[396,128]{1,0:T(8,128)S(1)} %get-tuple-element.26), channel_id=1, source_target_pairs={{1,2},{3,4},{5,6},{2,1},{4,3},{6,5},{9,10},{11,12},{13,14},{10,9},... | collective-permute-start | bytes 608264 | tf_op jit(solution)/shard_map/ppermute | solution.py:547
  7.1 0.7 %collective-permute-start.3 = (f32[192,128]{1,0:T(8,128)S(1)}, f32[192,128]{1,0:T(8,128)S(1)}, u32[]{:S(2)}, u32[]{:S(2)}) collective-permute-start(f32[192,128]{1,0:T(8,128)S(1)} %get-tuple-element.27), channel_id=1, source_target_pairs={{8,16},{16,8},{9,17},{17,9},{10,18},{18,10},{11,19},{19,11},{12,20... | collective-permute-start | bytes 294920 | tf_op jit(solution)/shard_map/ppermute | solution.py:543
  7.7 0.0 copy-done.1
  7.8 0.0 copy-done.2
  7.8 0.0 copy-done.4
  7.8 0.0 copy-done.5
  7.8 0.0 copy-done.6
  7.8 0.0 copy-done.7
  7.8 2.3 %shard_map.103 = (f32[1536,128]{1,0:T(8,128)S(1)}, bf16[2,1536,192]{2,1,0:T(8,128)(2,1)S(1)}, bf16[2,192,1536]{2,1,0:T(8,128)(2,1)S(1)}, bf16[2,192,384]{2,1,0:T...) custom-call(f32[1536,128]{1,0:T(8,128)S(1)} %bitcast.9, ...), custom_call_target="tpu_custom_call" | custom-call | flops 10000000 | bytes 1000000 | tf_op jit(solution)/shard_map/pallas_call | solution.py:549
  10.1 0.0 collective-permute-done.3.x2
  10.1 5.3 %collective-permute-done.1.y1 = f32[396,128]{1,0:T(8,128)S(1)} collective-permute-done((f32[396,128]{1,0:T(8,128)S(1)}, f32[396,128]{1,0:T(8,128)S(1)}, u32[]{:S(2)}, u32[]{:S(2)}) %collective-permute-start.1) | collective-permute-done | bytes 202784 | tf_op jit(solution)/shard_map/ppermute | solution.py:546
  15.4 0.0 collective-permute-done.2.y2
  15.4 0.0 copy-done.3
  15.4 2.3 %shard_map.106 = (f32[1536,128]{1,0:T(8,128)S(1)}, f32[232,128]{1,0:T(8,128)S(1)}) custom-call(f32[1536,128]{1,0:T(8,128)S(1)} %bitcast.10, f32[1536,128]{1,0:T(8,128)S(1)} %get-tuple-element.23.s_ref, f32[396,128]{1,0:T(8,128)S(1)} %collective-permute-done.1.y1, f32[396,128]{1,0:T(8,128)S(1)} %collective-permute-done.2.y2, ...), custom_call_target="tpu_custom_call" | custom-call | flops 10000000 | bytes 1000000 | tf_op jit(solution)/shard_map/pallas_call | solution.py:562
  17.8 1.6 %collective-permute-start.4 = (f32[232,128]{1,0:T(8,128)S(1)}, f32[232,128]{1,0:T(8,128)S(1)}, u32[]{:S(2)}, u32[]{:S(2)}) collective-permute-start(f32[232,128]{1,0:T(8,128)S(1)} %get-tuple-element.31.refs_0_), channel_id=1, source_target_pairs={{0,16},{8,24},{16,0},{24,8},{1,17},{9,25},{17,1},{25,9},{2,18},{10... | collective-permute-start | bytes 356360 | tf_op jit(solution)/shard_map/ppermute | solution.py:517
  19.3 0.0 collective-permute-start.5
  19.3 3.3 %collective-permute-done.4.refs_1_ = f32[232,128]{1,0:T(8,128)S(1)} collective-permute-done((f32[232,128]{1,0:T(8,128)S(1)}, f32[232,128]{1,0:T(8,128)S(1)}, u32[]{:S(2)}, u32[]{:S(2)}) %collective-permute-start.4) | collective-permute-done | bytes 118816 | tf_op jit(solution)/shard_map/ppermute | solution.py:517
  22.7 0.0 collective-permute-start.6
  22.7 1.5 %shard_map.107 = (f32[128,384]{1,0:T(8,128)S(1)}, f32[8,128]{1,0:T(8,128)S(1)}) custom-call(f32[1536,128]{1,0:T(8,128)S(1)} %get-tuple-element.32.state_ref.refs_4_, bf16[2,512,128]{2,1,0:T(8,128)(2,1)S(1)} %get-tuple-element.33.n_ref.refs_5_), custom_call_target="tpu_custom_call" | custom-call | flops 10000000 | bytes 1000000 | tf_op jit(solution)/shard_map/pallas_call | solution.py:574
  24.2 0.0 collective-permute-done.5.refs_2_
  24.2 0.0 collective-permute-done.6.refs_3_
  24.2 2.0 %shard_map.108 = (f32[128,192]{1,0:T(8,128)S(1)}, f32[24,128]{1,0:T(8,128)S(1)}, f32[32,128]{1,0:T(8,128)}) custom-call(f32[232,128]{1,0:T(8,128)S(1)} %get-tuple-element.31.refs_0_, f32[232,128]{1,0:T(8,128)S(1)} %collective-permute-done.4.refs_1_, f32[232,128]{1,0:T(8,128)S(1)} %collective-permute-done.5.refs_2_, ...), custom_call_target="tpu_custom_call" | custom-call | flops 10000000 | bytes 1000000 | tf_op jit(solution)/shard_map/pallas_call | solution.py:581
  26.2 6.0 %all-to-all-start = ((f32[32,1,128]{2,1,0:T(1,128)}), f32[32,1,128]{2,1,0:T(1,128)S(1)}, u32[]{:S(2)}, u32[]{:S(2)}) async-start(f32[32,1,128]{2,1,0:T(1,128)} %bitcast.6), calls=%async_computation | async-start | bytes 32768 | tf_op jit(solution)/shard_map/all_to_all | solution.py:596
  32.1 1.9 %shard_map.109 = (f32[1536,128]{1,0:T(8,128)}, f32[1536,128]{1,0:T(8,128)}) custom-call(f32[128,192]{1,0:T(8,128)S(1)} %get-tuple-element.37.d_ref, bf16[2,192,1536]{2,1,0:T(8,128)(2,1)S(1)} %get-tuple-element.38.t_ref, f32[24,128]{1,0:T(8,128)S(1)} %get-tuple-element.39.lack_ref, f32[1536,128]{1,0:T(8,128)S(1)} %get-tuple-element.32.state_ref.refs_4_), custom_call_target="tpu_custom_call" | custom-call | flops 10000000 | bytes 1000000 | tf_op jit(solution)/shard_map/pallas_call | solution.py:592
  34.0 5.3 %all-to-all-done = f32[32,1,128]{2,1,0:T(1,128)S(1)} async-done(((f32[32,1,128]{2,1,0:T(1,128)}), f32[32,1,128]{2,1,0:T(1,128)S(1)}, u32[]{:S(2)}, u32[]{:S(2)}) %all-to-all-start) | async-done | bytes 16416 | tf_op jit(solution)/shard_map/all_to_all | solution.py:596
  39.3 0.1 reduce_sum.9
  39.3 0.6 %fusion = f32[12]{0:T(128)} fusion(f32[128]{0:T(128)S(1)} %reduce_sum.9), kind=kLoop, calls=%fused_computation.1 | loop fusion | flops 24 | bytes 144 | tf_op jit(solution)/shard_map/sqrt | solution.py:597
Async XLA Ops:
  0.6 1.1 %copy-start = (f32[12,16,8,128]{3,2,1,0:T(8,128)S(1)}, f32[12,16,8,128]{3,2,1,0:T(8,128)}, u32[]{:S(2)}) copy-start(f32[12,16,8,128]{3,2,1,0:T(8,128)} %f_ref.1) | copy-start | bytes 2359300
  1.8 6.0 %copy-start.1 = (f32[128,32]{0,1:T(8,128)S(1)}, f32[128,32]{0,1:T(8,128)}, u32[]{:S(2)}) copy-start(f32[128,32]{0,1:T(8,128)} %param.15) | copy-start | bytes 49156
  1.8 6.0 %copy-start.2 = (f32[12,12]{1,0:T(8,128)S(1)}, f32[12,12]{1,0:T(8,128)}, u32[]{:S(2)}) copy-start(f32[12,12]{1,0:T(8,128)} %mix_ref.1) | copy-start | bytes 1732
  1.8 6.0 %copy-start.4 = (f32[12,6]{0,1:T(8,128)S(1)}, f32[12,6]{0,1:T(8,128)}, u32[]{:S(2)}) copy-start(f32[12,6]{0,1:T(8,128)} %param.16) | copy-start | bytes 868
  1.8 6.0 %copy-start.5 = (f32[12]{0:T(128)S(1)}, f32[12]{0:T(128)}, u32[]{:S(2)}) copy-start(f32[12]{0:T(128)} %dif.3) | copy-start | bytes 148
  1.8 6.0 %copy-start.6 = (f32[12]{0:T(128)S(1)}, f32[12]{0:T(128)}, u32[]{:S(2)}) copy-start(f32[12]{0:T(128)} %act.3) | copy-start | bytes 148
  1.8 6.0 %copy-start.7 = (f32[12]{0:T(128)S(1)}, f32[12]{0:T(128)}, u32[]{:S(2)}) copy-start(f32[12]{0:T(128)} %pre.1) | copy-start | bytes 148
  1.8 13.6 %copy-start.3 = (f32[16,64]{1,0:T(8,128)S(1)}, f32[16,64]{1,0:T(8,128)}, u32[]{:S(2)}) copy-start(f32[16,64]{1,0:T(8,128)} %bx_ref.1) | copy-start | bytes 12292
  1.9 1.5 %collective-permute-start = (f32[192,128]{1,0:T(8,128)S(1)}, f32[192,128]{1,0:T(8,128)S(1)}, u32[]{:S(2)}, u32[]{:S(2)}) collective-permute-start(f32[192,128]{1,0:T(8,128)S(1)} %get-tuple-element.24), channel_id=1, source_target_pairs={{0,8},{16,24},{8,0},{24,16},{1,9},{17,25},{9,1},{25,17},{2,10},{18... | collective-permute-start | bytes 294920 | tf_op jit(solution)/shard_map/ppermute | solution.py:544
  3.5 12.0 %collective-permute-start.1 = (f32[396,128]{1,0:T(8,128)S(1)}, f32[396,128]{1,0:T(8,128)S(1)}, u32[]{:S(2)}, u32[]{:S(2)}) collective-permute-start(f32[396,128]{1,0:T(8,128)S(1)} %get-tuple-element.25), channel_id=1, source_target_pairs={{0,1},{2,3},{4,5},{6,7},{1,0},{3,2},{5,4},{7,6},{8,9},{10,11},{12,... | collective-permute-start | bytes 608264 | tf_op jit(solution)/shard_map/ppermute | solution.py:546
  6.4 9.0 %collective-permute-start.2 = (f32[396,128]{1,0:T(8,128)S(1)}, f32[396,128]{1,0:T(8,128)S(1)}, u32[]{:S(2)}, u32[]{:S(2)}) collective-permute-start(f32[396,128]{1,0:T(8,128)S(1)} %get-tuple-element.26), channel_id=1, source_target_pairs={{1,2},{3,4},{5,6},{2,1},{4,3},{6,5},{9,10},{11,12},{13,14},{10,9},... | collective-permute-start | bytes 608264 | tf_op jit(solution)/shard_map/ppermute | solution.py:547
  7.1 3.0 %collective-permute-start.3 = (f32[192,128]{1,0:T(8,128)S(1)}, f32[192,128]{1,0:T(8,128)S(1)}, u32[]{:S(2)}, u32[]{:S(2)}) collective-permute-start(f32[192,128]{1,0:T(8,128)S(1)} %get-tuple-element.27), channel_id=1, source_target_pairs={{8,16},{16,8},{9,17},{17,9},{10,18},{18,10},{11,19},{19,11},{12,20... | collective-permute-start | bytes 294920 | tf_op jit(solution)/shard_map/ppermute | solution.py:543
  17.8 4.9 %collective-permute-start.4 = (f32[232,128]{1,0:T(8,128)S(1)}, f32[232,128]{1,0:T(8,128)S(1)}, u32[]{:S(2)}, u32[]{:S(2)}) collective-permute-start(f32[232,128]{1,0:T(8,128)S(1)} %get-tuple-element.31.refs_0_), channel_id=1, source_target_pairs={{0,16},{8,24},{16,0},{24,8},{1,17},{9,25},{17,1},{25,9},{2,18},{10... | collective-permute-start | bytes 356360 | tf_op jit(solution)/shard_map/ppermute | solution.py:517
  19.3 4.8 %collective-permute-start.5 = (f32[232,128]{1,0:T(8,128)S(1)}, f32[232,128]{1,0:T(8,128)S(1)}, u32[]{:S(2)}, u32[]{:S(2)}) collective-permute-start(f32[232,128]{1,0:T(8,128)S(1)} %get-tuple-element.31.refs_0_), channel_id=1, source_target_pairs={{0,8},{8,0},{16,24},{24,16},{1,9},{9,1},{17,25},{25,17},{2,10},{10... | collective-permute-start | bytes 356360 | tf_op jit(solution)/shard_map/ppermute | solution.py:517
  22.7 1.5 %collective-permute-start.6 = (f32[232,128]{1,0:T(8,128)S(1)}, f32[232,128]{1,0:T(8,128)S(1)}, u32[]{:S(2)}, u32[]{:S(2)}) collective-permute-start(f32[232,128]{1,0:T(8,128)S(1)} %collective-permute-done.4.refs_1_), channel_id=1, source_target_pairs={{0,8},{8,0},{16,24},{24,16},{1,9},{9,1},{17,25},{25,17},{2,10},{10... | collective-permute-start | bytes 356360 | tf_op jit(solution)/shard_map/ppermute | solution.py:517
  26.2 13.1 %all-to-all-start = ((f32[32,1,128]{2,1,0:T(1,128)}), f32[32,1,128]{2,1,0:T(1,128)S(1)}, u32[]{:S(2)}, u32[]{:S(2)}) async-start(f32[32,1,128]{2,1,0:T(1,128)} %bitcast.6), calls=%async_computation | async-start | bytes 32768 | tf_op jit(solution)/shard_map/all_to_all | solution.py:596

commit v7 on v6

--- a/solution.py
+++ b/solution.py
@@ -13,7 +13,7 @@
 SM = pl.BlockSpec(memory_space=pltpu.SMEM)
 
 
-def call(kernel, outs, in_specs, scratch=(), flops=10**7, vmem=12, out_specs=None):
+def call(kernel, outs, in_specs, scratch=(), vmem=12, out_specs=None):
     return pl.pallas_call(
         kernel,
         out_shape=[jax.ShapeDtypeStruct(s, d) for s, d in outs],
@@ -21,7 +21,7 @@
         out_specs=out_specs or [VM] * len(outs),
         scratch_shapes=list(scratch),
         compiler_params=pltpu.CompilerParams(vmem_limit_bytes=vmem << 20),
-        cost_estimate=pl.CostEstimate(flops=flops, bytes_accessed=10**6, transcendentals=0),
+        cost_estimate=pl.CostEstimate(flops=10**7, bytes_accessed=10**6, transcendentals=0),
     )
 
 
@@ -105,43 +105,31 @@
     return odd("gx")
 
 
-def pack_x_kernel(dims, f_ref, q1, q2, low_ref, high_ref, sem):
+def pack_y_kernel(dims, f_ref, p1, p2):
     nv, rows_x, rows_y, _ = dims
-    reads = [
-        pltpu.make_async_copy(f_ref.at[:, pl.ds(0, 2)], low_ref, sem.at[0]),
-        pltpu.make_async_copy(f_ref.at[:, pl.ds(rows_x - 2, 2)], high_ref, sem.at[1]),
-    ]
-    for read in reads:
-        read.start()
-    for read in reads:
-        read.wait()
-    is_odd = odd("gx")
-    for layer in range(2):
-        for v in range(nv):
-            low, high = low_ref[v, layer], high_ref[v, 1 - layer]
-            at = pl.ds((layer * nv + v) * rows_y, rows_y)
-            q1[at, :] = jnp.where(is_odd, low, high)
-            q2[at, :] = jnp.where(is_odd, high, low)
-
-
-def pack_y_kernel(dims, f_ref, x1, p1, p2):
-    nv, rows_x, rows_y, _ = dims
-    size = rows_x * rows_y
-
-    def put(at, low, high):
-        p1[at, :] = jnp.where(odd("gy"), low, high)
-        p2[at, :] = jnp.where(odd("gy"), high, low)
-
+    size = rows_x * rows_y
     for layer in range(2):
         for v in range(nv):
             low = f_ref[pl.ds(v * size + layer, rows_x, stride=rows_y), :]
             high = f_ref[pl.ds(v * size + rows_y - 1 - layer, rows_x, stride=rows_y), :]
-            put(pl.ds((layer * nv + v) * rows_x, rows_x), low, high)
-    low, high = [x1[pl.ds(y, nv, stride=rows_y), :] for y in (0, rows_y - 1)]
-    put(pl.ds(2 * rows_x * nv, nv), low, high)
-
-
-def first_kernel(dims, f_ref, bz_ref, bv_ref, mix_ref, dif, pre, act, *outs):
+            at = pl.ds((layer * nv + v) * rows_x, rows_x)
+            p1[at, :] = jnp.where(odd("gy"), low, high)
+            p2[at, :] = jnp.where(odd("gy"), high, low)
+
+
+def pack_x_kernel(dims, f_ref, q1, q2):
+    nv, rows_x, rows_y, _ = dims
+    size = rows_x * rows_y
+    for layer in range(2):
+        for v in range(nv):
+            low = f_ref[pl.ds(v * size + layer * rows_y, rows_y), :]
+            high = f_ref[pl.ds(v * size + (rows_x - 1 - layer) * rows_y, rows_y), :]
+            at = pl.ds((layer * nv + v) * rows_y, rows_y)
+            q1[at, :] = jnp.where(odd("gx"), low, high)
+            q2[at, :] = jnp.where(odd("gx"), high, low)
+
+
+def first_kernel(dims, f_ref, x1, bz_ref, bv_ref, mix_ref, dif, pre, act, *outs):
     s_ref, k_ref, t_ref, u_ref, n_ref, both_ref, low_ref = outs
     nv, rows_x, rows_y, lanes = dims
     size = rows_x * rows_y
@@ -162,10 +150,11 @@
     def emit(v, x, n, w, t):
         s_ref[pl.ds(v * size + x * rows_y, n * rows_y), :] = (w + t).reshape(n * rows_y, lanes)
 
-    def nothing(v):
-        return jnp.zeros((rows_y, lanes), jnp.float32)
-
-    stage(f_ref, nv, rows_x, rows_y, dif, act, (both, lo), emit, nothing, nothing)
+    def near(is_low):
+        is_near = odd("gx") if is_low else jnp.logical_not(odd("gx"))
+        return lambda v: jnp.where(is_near, x1[pl.ds(v * rows_y, rows_y), :], 0.0)
+
+    stage(f_ref, nv, rows_x, rows_y, dif, act, (both, lo), emit, near(True), near(False))
     bz, bv = bz_ref[...], bv_ref[...]
     rank_z, rank_v = bz.shape[0], bv.shape[0]
     width, part = rank_z * rank_v, nv * rank_z
@@ -195,7 +184,7 @@
 
 def second_kernel(
     dims, f_ref, s_ref, y1, y2, x1, x2, bx_ref, k_ref, both_ref, low_ref, dif, act,
-    state_ref, m_ref, sec, gy_ref, gx_ref,
+    state_ref, m_ref, near_ref, sec, gy_ref, gx_ref,
 ):
     nv, rows_x, rows_y, lanes = dims
     size = rows_x * rows_y
@@ -211,10 +200,7 @@
         return jnp.stack(two(x1, x2, odd("gx"), pl.ds((layer * nv + v) * rows_y, rows_y)))
 
     far = far_side()
-
-    def corners(v):
-        near = two(y1, y2, odd("gy"), pl.ds(2 * rows_x * nv + v, 1))
-        return [jnp.where(far, a, 0.0) for a in near], [jnp.where(far, 0.0, a) for a in near]
+    edges = (jnp.where(far, rows_x - 1, 0), jnp.where(far, 0, rows_x - 1))
 
     def keep(value, flags):
         inside = [jnp.where(flags[i], value[i], 0.0) for i in range(2)]
@@ -228,9 +214,8 @@
         cut = g.size // (8 * lanes)
         low = f_ref[pl.ds(v * size, rows_x, stride=rows_y), :]
         high = f_ref[pl.ds(v * size + rows_y - 1, rows_x, stride=rows_y), :]
-        left, right = corners(v)
         lap = y_ghost(1, v) + jnp.stack([low, high]) - 6.0 * g
-        lap = lap + shifted(g, 1, jnp.stack(left), jnp.stack(right)) + shifted(g, 2)
+        lap = lap + shifted(g, 1) + shifted(g, 2)
         out = g + (dif[v] * lap + made[v][:cut].reshape(g.shape))
         gy_ref[pl.ds(v * 2 * rows_x, 2 * rows_x), :] = keep(out, has_y)
         sec[pl.ds(v * size, size), :] = s_ref[pl.ds(v * size, size), :]
@@ -241,16 +226,12 @@
         g = xs[v]
         low = f_ref[pl.ds(v * size, rows_y), :]
         high = f_ref[pl.ds(v * size + size - rows_y, rows_y), :]
-        before = jnp.stack([left[0], right[0]])
-        after = jnp.stack([left[1], right[1]])
         lap = x_ghost(1, v) + jnp.stack([low, high]) - 6.0 * g
-        lap = lap + shifted(g, 1, before, after) + shifted(g, 2)
+        lap = lap + shifted(g, 1) + shifted(g, 2)
         out = g + (dif[v] * lap + made[v][cut:].reshape(g.shape))
         gx_ref[pl.ds(v * 2 * rows_y, 2 * rows_y), :] = keep(out, has_x)
-        at = pl.ds(v * size, rows_y)
-        sec[at, :] = sec[at, :] + dif[v] * g[0]
-        at = pl.ds(v * size + size - rows_y, rows_y)
-        sec[at, :] = sec[at, :] + dif[v] * g[1]
+        at = pl.ds(pl.multiple_of(v * size + edges[0] * rows_y, rows_y), rows_y)
+        sec[at, :] = sec[at, :] + dif[v] * x2[pl.ds(v * rows_y, rows_y), :]
 
     def emit(v, x, n, w, t):
         at = pl.ds(v * size + x * rows_y, n * rows_y)
@@ -262,22 +243,24 @@
         lambda v: gx_ref[pl.ds((v * 2 + 1) * rows_y, rows_y), :],
     )
     his, los = [], []
-    edge = jnp.where(far, rows_x - 1, 0)
+    spot = spots(dims, k_ref.shape[2], bx_ref.shape[1])[2]
     for v in range(nv):
         half = 0.5 * dif[v]
         at = pl.ds(v * size, rows_x, stride=rows_y)
         state_ref[at, :] = state_ref[at, :] + half * gy_ref[pl.ds(v * 2 * rows_x, rows_x), :]
         at = pl.ds(v * size + rows_y - 1, rows_x, stride=rows_y)
         state_ref[at, :] = state_ref[at, :] + half * gy_ref[pl.ds((v * 2 + 1) * rows_x, rows_x), :]
-        ends = [dif[v] * dif[v] * a for a in two(y1, y2, odd("gy"), pl.ds(v * rows_x + edge, 1))]
-        for end in range(2):
-            m_ref[pl.ds(spots(dims, k_ref.shape[2], bx_ref.shape[1])[2] + end * nv + v, 1), :] = ends[end]
-        lack = jnp.concatenate([ends_tile(*ends, rows_y), jnp.zeros((-rows_y % 16, lanes), jnp.float32)], axis=0)
-        hi, lo = split(jnp.concatenate([state_ref[pl.ds(v * size, size), :], lack], axis=0))
+        rows = [state_ref[pl.ds(v * size, size), :]]
+        for out, start, edge in ((m_ref, spot, edges[0]), (near_ref, 0, edges[1])):
+            ends = [dif[v] * dif[v] * a for a in two(y1, y2, odd("gy"), pl.ds(v * rows_x + edge, 1))]
+            for end in range(2):
+                out[pl.ds(start + end * nv + v, 1), :] = ends[end]
+            rows.append(ends_tile(*ends, rows_y))
+        hi, lo = split(jnp.concatenate(rows, axis=0))
         his.append(hi)
         los.append(lo)
     total = mm3((jnp.concatenate(his, 1), jnp.concatenate(los, 1)), (k_ref[0], k_ref[1]))
-    pack_message(dims, m_ref, total[:size], bx_ref[...], total[size : size + rows_y])
+    pack_message(dims, m_ref, total[:size], bx_ref[...], total[size:])
 
 
 def ends_tile(first, last, rows):
@@ -293,7 +276,7 @@
     basis = tail + size // 2
     ends = basis + rows_x // 2
     made = ends + 2 * nv
-    return tail, basis, ends, made, made + -(-(width // lanes * 2 + 1) // 8) * 8
+    return tail, basis, ends, made, made + -(-(width // lanes * 4 + 2) // 8) * 8
 
 
 def fold(a):
@@ -311,14 +294,16 @@
     size, width = values.shape
     tail, base, _, made, _ = spots(dims, width, basis.shape[1])
     whole = width // lanes
+    ends = [ends[row : row + 1] for row in (0, rows_y - 1, rows_y, 2 * rows_y - 1)]
     for i in range(whole):
         m_ref[pl.ds(i * size, size), :] = values[:, i * lanes : (i + 1) * lanes]
-        for end, row in enumerate((0, rows_y - 1)):
-            m_ref[pl.ds(made + 2 * i + end, 1), :] = ends[row : row + 1, i * lanes : (i + 1) * lanes]
+        for end in range(4):
+            m_ref[pl.ds(made + 4 * i + end, 1), :] = ends[end][:, i * lanes : (i + 1) * lanes]
     m_ref[pl.ds(tail, size // 2), :] = fold(values[:, whole * lanes :])
     m_ref[pl.ds(base, rows_x // 2), :] = fold(basis)
-    rest = [ends[row : row + 1, whole * lanes :] for row in (0, rows_y - 1)]
-    m_ref[pl.ds(made + 2 * whole, 1), :] = jnp.concatenate(rest, axis=1)
+    for end in range(0, 4, 2):
+        rest = [ends[end][:, whole * lanes :], ends[end + 1][:, whole * lanes :]]
+        m_ref[pl.ds(made + 4 * whole + end // 2, 1), :] = jnp.concatenate(rest, axis=1)
 
 
 def unpack_message(dims, m_ref, width, rank_x):
@@ -329,16 +314,14 @@
     parts = [m_ref[pl.ds(i * size, size), :] for i in range(whole)]
     parts.append(unfold(m_ref[pl.ds(tail, size // 2), :]))
     basis = unfold(m_ref[pl.ds(base, rows_x // 2), :])
-    rest = m_ref[pl.ds(made + 2 * whole, 1), :]
     half = lanes // 2
-    ends = [
-        jnp.concatenate(
-            [m_ref[pl.ds(made + 2 * i + end, 1), :] for i in range(whole)] + [rest[:, end * half : (end + 1) * half]],
-            axis=1,
-        )
-        for end in range(2)
-    ]
-    return jnp.concatenate(parts, axis=1), basis, ends_tile(*ends, rows_y)
+    ends = []
+    for end in range(4):
+        rest = m_ref[pl.ds(made + 4 * whole + end // 2, 1), :]
+        rest = rest[:, end % 2 * half : (end % 2 + 1) * half]
+        ends.append(jnp.concatenate([m_ref[pl.ds(made + 4 * i + end, 1), :] for i in range(whole)] + [rest], axis=1))
+    tiles = ends_tile(*ends[:2], rows_y), ends_tile(*ends[2:], rows_y)
+    return jnp.concatenate(parts, axis=1), basis, tiles
 
 
 def from_far(me, masks, index, items):
@@ -354,30 +337,56 @@
     return total
 
 
-def mix_blocks(dims, width, rank_x, masks, refs):
+def repeated(basis, rows_y):
+    rows_x, rank_x = basis.shape
+    return jnp.broadcast_to(basis[:, None, :], (rows_x, rows_y, rank_x)).reshape(rows_x * rows_y, rank_x)
+
+
+def link_to(own, bases, rows_y):
+    link = mm3(split(own), split(bases), True)
+    return split(jnp.where(same_row(link, rows_y), link, 0.0))
+
+
+def same_row(link, rows_y):
+    return place(link.shape, 0) % rows_y == place(link.shape, 1) % rows_y
+
+
+def mix_blocks(dims, width, rank_x, own_ref, refs):
+    rows_y = dims[2]
+    own = repeated(unpack_message(dims, own_ref, width, rank_x)[1], rows_y)
+    parts = [unpack_message(dims, ref, width, rank_x) for ref in refs]
+    values = jnp.concatenate([values for values, _, _ in parts], axis=0)
+    bases = jnp.concatenate([repeated(basis, rows_y) for _, basis, _ in parts], axis=0)
+    return mm3(link_to(own, bases, rows_y), split(values))
+
+
+def premix_kernel(dims, width, rank_x, n, own_ref, *refs):
+    refs[n][...] = mix_blocks(dims, width, rank_x, own_ref, refs[:n])
+
+
+def second_premix_kernel(dims, width, rank_x, n, own_ref, *refs):
+    d_ref, w_ref, u_ref, out_ref, gap_ref = refs[n:]
+    mixed = d_ref[...] + mix_blocks(dims, width, rank_x, own_ref, refs[:n])
+    out_ref[...] = mixed
+    gap_ref[...] = w_ref[...] - mm3(split(mixed), (u_ref[0], u_ref[1]))
+
+
+def last_values(dims, width, rank_x, masks, refs):
     _, rows_x, rows_y, _ = dims
-    size = rows_x * rows_y
     me = lax.axis_index("gx")
-
-    def repeated(basis):
-        return jnp.broadcast_to(basis[:, None, :], (rows_x, rows_y, rank_x)).reshape(size, rank_x)
-
     parts = [unpack_message(dims, ref, width, rank_x) for ref in refs]
-    values = []
-    for i, (value, _, _) in enumerate(parts):
-        lack = from_far(me, masks, i, [ends for _, _, ends in parts])
-        if lack is not None:
-            last = jnp.bitwise_xor(me, masks[i]) % 2 == 1
-            top = value[:rows_y] + jnp.where(last, 0.0, lack)
-            bottom = value[size - rows_y :] + jnp.where(last, lack, 0.0)
-            value = jnp.concatenate([top, value[rows_y : size - rows_y], bottom], axis=0)
-        values.append(value)
-    values = jnp.concatenate(values, axis=0)
-    bases = jnp.concatenate([repeated(basis) for _, basis, _ in parts], axis=0)
-    hi, lo = split(bases)
-    link = mm3((hi[:size], lo[:size]), (hi, lo), True)
-    same = place(link.shape, 0) % rows_y == place(link.shape, 1) % rows_y
-    return mm3(split(jnp.where(same, link, 0.0)), split(values))
+    values, bases = [parts[-1][0]], [repeated(parts[-1][1], rows_y)]
+    for i, (_, basis, _) in enumerate(parts):
+        last = jnp.bitwise_xor(me, masks[i]) % 2 == 1
+        near = parts[masks.index(masks[i] ^ 1)][2][1]
+        lacks = (from_far(me, masks, i, [ends[0] for _, _, ends in parts]), near)
+        rows = (jnp.where(last, basis[rows_x - 1 :], basis[:1]), jnp.where(last, basis[:1], basis[rows_x - 1 :]))
+        for lack, row in zip(lacks, rows):
+            if lack is not None:
+                values.append(lack)
+                bases.append(jnp.broadcast_to(row, (rows_y, rank_x)))
+    own = repeated(parts[0][1], rows_y)
+    return split(jnp.concatenate(values, axis=0)), own, jnp.concatenate(bases, axis=0)
 
 
 def squares(a):
@@ -402,7 +411,11 @@
     return coefs, state - mm3(split(coefs), basis, True)
 
 
-def side_kernel(dims, rank_z, state_ref, n_ref, w_ref, row_ref):
+def tile_of(ref, nv, v, rows_y):
+    return ends_tile(ref[pl.ds(v, 1), :], ref[pl.ds(nv + v, 1), :], rows_y)
+
+
+def side_kernel(dims, rank_z, state_ref, near_ref, n_ref, w_ref, row_ref):
     nv, rows_x, rows_y, lanes = dims
     size = rows_x * rows_y
     held = lanes // rank_z
@@ -410,8 +423,9 @@
     outside, mass = [], []
     for v in range(0, nv, held):
         state = jnp.concatenate([state_ref[pl.ds((v + j) * size, size), :] for j in range(held)], axis=1)
-        top = jnp.where(last, state[:rows_y], 0.0)
-        bottom = jnp.where(last, 0.0, state[size - rows_y :])
+        near = jnp.concatenate([tile_of(near_ref, nv, v + j, rows_y) for j in range(held)], axis=1)
+        top = jnp.where(last, state[:rows_y] + near, 0.0)
+        bottom = jnp.where(last, 0.0, state[size - rows_y :] + near)
         state = jnp.concatenate([top, state[rows_y : size - rows_y], bottom], axis=0)
         coefs, rest = outside_span(state, (n_ref[0], n_ref[1]))
         w_ref[:, (v // held) * lanes : (v // held + 1) * lanes] = coefs
@@ -421,83 +435,106 @@
     row_ref[...] = tally(outside, mass, lanes)
 
 
-def edge_rows(dims, rank_z, state_ref, lack_ref, n_ref):
+def edge_state(dims, rank_z, state_ref, lack):
     nv, rows_x, rows_y, lanes = dims
-    size = rows_x * rows_y
+    start = jnp.where(far_side(), (rows_x - 1) * rows_y, 0)
     held = lanes // rank_z
-    start = jnp.where(far_side(), size - rows_y, 0)
     whole = []
     for v in range(nv):
-        at = pl.ds(pl.multiple_of(v * size + start, rows_y), rows_y)
-        ends = [lack_ref[pl.ds(end * nv + v, 1), :] for end in range(2)]
+        at = pl.ds(pl.multiple_of(v * rows_x * rows_y + start, rows_y), rows_y)
+        ends = [lack[end * nv + v : end * nv + v + 1] for end in range(2)]
         whole.append(state_ref[at, :] + ends_tile(*ends, rows_y))
-    state = jnp.concatenate(
-        [jnp.concatenate(whole[v : v + held], axis=1) for v in range(0, nv, held)], axis=0
-    )
-    coefs, rest = outside_span(state, (n_ref[0], n_ref[1]))
+    packed = [jnp.concatenate(whole[v : v + held], axis=1) for v in range(0, nv, held)]
+    return whole, jnp.concatenate(packed, axis=0)
+
+
+def edge_sums(dims, rank_z, whole, rest):
+    nv, _, rows_y, lanes = dims
+    held = lanes // rank_z
     outside = []
     for v in range(nv):
         i, j = divmod(v, held)
         outside.append(squares(rest[i * rows_y : (i + 1) * rows_y, j * lanes : (j + 1) * lanes]))
-    row = tally(outside, [squares(a) for a in whole], lanes)
-    coefs = jnp.concatenate([coefs[i * rows_y : (i + 1) * rows_y] for i in range(nv // held)], axis=1)
-    return coefs, row
-
-
-def settle(dims, rank_z, mixed, lack_ref, state_ref, n_ref, w_ref, row_ref, u_ref, sums_ref):
-    _, _, rows_y, lanes = dims
-    coefs, edge_row = edge_rows(dims, rank_z, state_ref, lack_ref, n_ref)
-    last = far_side()
-    w = w_ref[...]
-    size, part = w.shape
+    return tally(outside, [squares(a) for a in whole], lanes)[0:1, :]
+
+
+def edge_coefs(rows_y, coefs):
+    count = coefs.shape[0] // rows_y
+    return jnp.concatenate([coefs[i * rows_y : (i + 1) * rows_y] for i in range(count)], axis=1)
+
+
+def put_edge(w, coefs):
+    rows_y, last = coefs.shape[0], far_side()
+    size = w.shape[0]
     top = w[:rows_y] + jnp.where(last, 0.0, coefs)
     bottom = w[size - rows_y :] + jnp.where(last, coefs, 0.0)
-    w = jnp.concatenate([top, w[rows_y : size - rows_y], bottom], axis=0)
-    gap = w - mm3(split(mixed), (u_ref[0], u_ref[1]))
+    return jnp.concatenate([top, w[rows_y : size - rows_y], bottom], axis=0)
+
+
+def total_sums(gap, rows, sums_ref, rank_z):
     hi, lo = split(squares(gap))
-    shape = (part, lanes)
+    shape = (gap.shape[1], sums_ref.shape[1])
     pick = zero_one(place(shape, 0) // rank_z == place(shape, 1))
-    row = jnp.sum(mm(hi, pick) + mm(lo, pick), axis=0, keepdims=True) + row_ref[0:1, :] + edge_row[0:1, :]
+    row = jnp.sum(mm(hi, pick) + mm(lo, pick), axis=0, keepdims=True) + rows[0] + rows[1]
     sums_ref[...] = jnp.broadcast_to(row, sums_ref.shape)
 
 
-def find_lack(dims, width, rank_x, masks, refs, lack_ref):
+def find_lack(dims, width, rank_x, masks, refs):
     spot = spots(dims, width, rank_x)[2]
     rows = [ref[pl.ds(spot, 2 * dims[0]), :] for ref in refs]
     lack = from_far(lax.axis_index("gx"), masks, 0, rows)
-    lack_ref[...] = jnp.zeros(lack_ref.shape, jnp.float32) if lack is None else lack
+    return jnp.zeros_like(rows[0]) if lack is None else lack
 
 
 def third_kernel(dims, rank_z, width, rank_x, masks, *refs):
     n = len(masks)
-    state_ref, n_ref, w_ref, row_ref, u_ref, d_ref, lack_ref, sums_ref = refs[n:]
-    find_lack(dims, width, rank_x, masks, refs[:n], lack_ref)
-    mixed = mix_blocks(dims, width, rank_x, masks, refs[:n])
-    d_ref[...] = mixed
-    settle(dims, rank_z, mixed, lack_ref, state_ref, n_ref, w_ref, row_ref, u_ref, sums_ref)
+    state_ref, n_ref, row_ref, u_ref, part_ref, gap_ref, d_ref, lack_ref, sums_ref = refs[n:]
+    rows_y = dims[2]
+    values, own, bases = last_values(dims, width, rank_x, masks, refs[:n])
+    lack = find_lack(dims, width, rank_x, masks, refs[:n])
+    whole, edge = edge_state(dims, rank_z, state_ref, lack)
+    basis = (n_ref[0], n_ref[1])
+    link = mm3(split(own), split(bases), True)
+    coefs = mm3(split(edge), basis)
+    spread = mm3(values, (u_ref[0], u_ref[1]))
+    link = split(jnp.where(same_row(link, rows_y), link, 0.0))
+    rest = edge - mm3(split(coefs), basis, True)
+    gap = mm3(link, split(spread))
+    row = edge_sums(dims, rank_z, whole, rest)
+    gap = put_edge(gap_ref[...], edge_coefs(rows_y, coefs)) - gap
+    total_sums(gap, (row_ref[0:1, :], row), sums_ref, rank_z)
+    lack_ref[...] = lack
+    d_ref[...] = part_ref[...] + mm3(link, values)
 
 
 def mix_kernel(dims, width, rank_x, masks, *refs):
     n = len(masks)
-    find_lack(dims, width, rank_x, masks, refs[:n], refs[n + 1])
-    refs[n][...] = mix_blocks(dims, width, rank_x, masks, refs[:n])
-
-
-def settle_kernel(dims, rank_z, d_ref, lack_ref, state_ref, n_ref, w_ref, row_ref, u_ref, sums_ref):
-    settle(dims, rank_z, d_ref[...], lack_ref, state_ref, n_ref, w_ref, row_ref, u_ref, sums_ref)
-
-
-def decode_kernel(dims, d_ref, t_ref, lack_ref, state_ref, recon_ref, out_ref):
+    part_ref, d_ref, lack_ref = refs[n:]
+    lack_ref[...] = find_lack(dims, width, rank_x, masks, refs[:n])
+    values, own, bases = last_values(dims, width, rank_x, masks, refs[:n])
+    d_ref[...] = part_ref[...] + mm3(link_to(own, bases, dims[2]), values)
+
+
+def settle_kernel(dims, rank_z, d_ref, lack_ref, state_ref, n_ref, row_ref, u_ref, w_ref, sums_ref):
+    whole, edge = edge_state(dims, rank_z, state_ref, lack_ref[...])
+    coefs, rest = outside_span(edge, (n_ref[0], n_ref[1]))
+    row = edge_sums(dims, rank_z, whole, rest)
+    gap = put_edge(w_ref[...], edge_coefs(dims[2], coefs)) - mm3(split(d_ref[...]), (u_ref[0], u_ref[1]))
+    total_sums(gap, (row_ref[0:1, :], row), sums_ref, rank_z)
+
+
+def decode_kernel(dims, d_ref, t_ref, lack_ref, near_ref, state_ref, recon_ref, out_ref):
     nv, rows_x, rows_y, lanes = dims
     size = rows_x * rows_y
     halves = split(d_ref[...])
-    start = jnp.where(far_side(), size - rows_y, 0)
+    far = far_side()
+    starts = (jnp.where(far, size - rows_y, 0), jnp.where(far, 0, size - rows_y))
     for v in range(nv):
         whole = pl.ds(v * size, size)
         out_ref[whole, :] = state_ref[whole, :]
-        at = pl.ds(pl.multiple_of(v * size + start, rows_y), rows_y)
-        ends = [lack_ref[pl.ds(end * nv + v, 1), :] for end in range(2)]
-        out_ref[at, :] = state_ref[at, :] + ends_tile(*ends, rows_y)
+        for start, ref in zip(starts, (lack_ref, near_ref)):
+            at = pl.ds(pl.multiple_of(v * size + start, rows_y), rows_y)
+            out_ref[at, :] = state_ref[at, :] + tile_of(ref, nv, v, rows_y)
         cols = slice(v * lanes, (v + 1) * lanes)
         recon_ref[whole, :] = mm3(halves, (t_ref[0, :, cols], t_ref[1, :, cols]))
 
@@ -532,19 +569,13 @@
     flat = field.reshape(nv * size, lanes)
     block = (nv * size, lanes)
 
-    y_msg, x_msg = (nv * (2 * rows_x + 1), lanes), (2 * nv * rows_y, lanes)
-    edges = (nv, 2, rows_y, lanes)
-    q1, q2 = call(
-        functools.partial(pack_x_kernel, dims),
-        [(x_msg, f32)] * 2,
-        [pl.BlockSpec(memory_space=pltpu.HBM)],
-        [pltpu.VMEM(edges, f32)] * 2 + [pltpu.SemaphoreType.DMA((2,))],
-    )(field)
+    y_msg, x_msg = (2 * nv * rows_x, lanes), (2 * nv * rows_y, lanes)
+    p1, p2 = call(functools.partial(pack_y_kernel, dims), [(y_msg, f32)] * 2, [VM])(flat)
+    y1 = lax.ppermute(p1, "gy", pairs(gy, 0))
+    y2 = lax.ppermute(p2, "gy", pairs(gy, 1))
+    q1, q2 = call(functools.partial(pack_x_kernel, dims), [(x_msg, f32)] * 2, [VM])(flat)
     x2 = lax.ppermute(q2, "gx", pairs(gx, 1))
     x1 = lax.ppermute(q1, "gx", pairs(gx, 0))
-    p1, p2 = call(functools.partial(pack_y_kernel, dims), [(y_msg, f32)] * 2, [VM] * 2)(flat, x1)
-    y1 = lax.ppermute(p1, "gy", pairs(gy, 0))
-    y2 = lax.ppermute(p2, "gy", pairs(gy, 1))
 
     section, k, t, u, n, both, low = call(
         functools.partial(first_kernel, dims),
@@ -557,11 +588,11 @@
             ((nv * 8, nv * 16), bf16),
             ((nv * 8, nv * 8), bf16),
         ],
-        [VM] * 4 + [SM] * 3,
-    )(flat, basis_z.T, basis_v.T, mixing, diffusion, prefactor, activation)
-    state, message = call(
+        [VM] * 5 + [SM] * 3,
+    )(flat, x1, basis_z.T, basis_v.T, mixing, diffusion, prefactor, activation)
+    state, message, near = call(
         functools.partial(second_kernel, dims),
-        [(block, f32), ((spots(dims, width, rank_x)[4], lanes), f32)],
+        [(block, f32), ((spots(dims, width, rank_x)[4], lanes), f32), ((2 * nv, lanes), f32)],
         [VM] * 10 + [SM] * 2,
         [
             pltpu.VMEM(block, f32),
@@ -570,26 +601,40 @@
         ],
     )(flat, section, y1, y2, x1, x2, basis_x, k, both, low, diffusion, activation)
     blocks, masks = gather_blocks(message)
+    near = lax.ppermute(near, "gx", pairs(gx, 0))
     count = len(blocks)
     coefs, row = call(
-        functools.partial(side_kernel, dims, rank_z), [((size, part), f32), ((8, lanes), f32)], [VM] * 2
-    )(state, n)
-    outs = [((size, width), f32), ((2 * nv, lanes), f32), ((peers, lanes), f32)]
+        functools.partial(side_kernel, dims, rank_z), [((size, part), f32), ((8, lanes), f32)], [VM] * 3
+    )(state, near, n)
+    mixed_type, sums_type = ((size, width), f32), ((peers, lanes), f32)
+    outs = [mixed_type, ((2 * nv, lanes), f32), sums_type]
+    close = [blocks[i] for i in range(count - 1) if masks[i] in (0, 1)]
+    others = [blocks[i] for i in range(count - 1) if masks[i] not in (0, 1)]
+    (premixed,) = call(
+        functools.partial(premix_kernel, dims, width, rank_x, len(close)), [mixed_type], [VM] * (len(close) + 1)
+    )(message, *close)
+    premixed, gap = call(
+        functools.partial(second_premix_kernel, dims, width, rank_x, len(others)),
+        [mixed_type, ((size, part), f32)],
+        [VM] * (len(others) + 4),
+    )(message, *others, premixed, coefs, u)
     mixing_args = (width, rank_x, masks)
-    rest = (state, n, coefs, row, u)
+    rest = (state, n, row, u)
     if basis_y.shape[0] * gy == basis_y.shape[1]:
         mixed, lack, sums = call(
-            functools.partial(third_kernel, dims, rank_z, *mixing_args), outs, [VM] * (count + 5)
-        )(*blocks, *rest)
+            functools.partial(third_kernel, dims, rank_z, *mixing_args), outs, [VM] * (count + 6)
+        )(*blocks, *rest, premixed, gap)
     else:
-        mixed, lack = call(functools.partial(mix_kernel, dims, *mixing_args), outs[:2], [VM] * count)(*blocks)
+        mixed, lack = call(
+            functools.partial(mix_kernel, dims, *mixing_args), outs[:2], [VM] * (count + 1)
+        )(*blocks, premixed)
         mixed = mixed.reshape(rows_x, rows_y, width)
         core = lax.psum(jnp.einsum("xyk,yb->xbk", mixed, basis_y, precision=HIGH), "gy")
         mixed = jnp.einsum("xbk,yb->xyk", core, basis_y, precision=HIGH).reshape(size, width)
-        (sums,) = call(functools.partial(settle_kernel, dims, rank_z), outs[2:], [VM] * 7)(
-            mixed, lack, *rest
-        )
-    recon, state = call(functools.partial(decode_kernel, dims), [(block, f32)] * 2, [VM] * 4)(mixed, t, lack, state)
+        (sums,) = call(functools.partial(settle_kernel, dims, rank_z), outs[2:], [VM] * 7)(mixed, lack, *rest, coefs)
+    recon, state = call(functools.partial(decode_kernel, dims), [(block, f32)] * 2, [VM] * 5)(
+        mixed, t, lack, near, state
+    )
     if peers > 64:
         sums = lax.psum(sums[0], ("gx", "gy"))
     else:

time: 40.1 us -> 40.4 us (level)
  Pallas kernels: 10.1 us -> 11.1 us
  waiting for transfers between devices: 14.9 us -> 14 us
    ppermute x1, waiting for transfers between devices: 5.32 us -> 3.93 us  [program(): y1 = lax.ppermute(p1, 'gy', pairs(gy, 0))]
    pallas_call x3 -> x5, Pallas kernels: 2 us -> 3.2 us  [the longest x1 1.88 us: program(): call(functools.partial(decode_kernel, dims), [(block, f32)] * 2, [VM] * 5)]
    ppermute x0 -> x1, waiting for transfers between devices: none -> 0.84 us  [program(): near = lax.ppermute(near, 'gx', pairs(gx, 0))]
    ppermute x0 -> x1, starting transfers between devices: none -> 0.51 us  [program(): near = lax.ppermute(near, 'gx', pairs(gx, 0))]
    ppermute x1, starting transfers between devices: 0.56 us -> 0.07 us  [program(): x1 = lax.ppermute(q1, 'gx', pairs(gx, 0))]
  transfers between devices with their start and end apart: 8 -> 9, of which waited for: 4 -> 5; matrix products, arithmetic and copies ran while one was open for 0% -> 0% of each run, Pallas kernels for 14% -> 17%
where the time goes in v7:
time: 40.4 us; the launch traced here: 40.2 us
  waiting for transfers between devices  14 us (35%)
  starting transfers between devices  12.5 us (31%)
  Pallas kernels  11.1 us (27%)
  local copies, waits for them, and re-layouts  1.17 us (3%)
  between operations  0.79 us (2%)
  other arithmetic  0.65 us (2%)
    all_to_all x1, starting transfers between devices, program(): sums = jnp.sum(lax.all_to_all(sums, ('gx', 'gy'), 0, 0, tiled=True), axis=0)  5.95 us
    all_to_all x1, waiting for transfers between devices, program(): sums = jnp.sum(lax.all_to_all(sums, ('gx', 'gy'), 0, 0, tiled=True), axis=0)  5.26 us
    ppermute x1, waiting for transfers between devices, program(): y1 = lax.ppermute(p1, 'gy', pairs(gy, 0))  3.93 us
    ppermute x3, waiting for transfers between devices, gather_blocks(): blocks = blocks + [lax.ppermute(b, 'gx', swaps) for b in blocks]  3.34 us
    ppermute x1, starting transfers between devices, program(): y1 = lax.ppermute(p1, 'gy', pairs(gy, 0))  3.06 us
    pallas_call x1, Pallas kernels, program(): call(functools.partial(second_kernel, dims), [(block, f32), ((spots(dims,...  2.36 us
    pallas_call x1, Pallas kernels, program(): call(functools.partial(first_kernel, dims), [(block, f32), ((2, nv * lane...  2.3 us
    pallas_call x1, Pallas kernels, program(): call(functools.partial(decode_kernel, dims), [(block, f32)] * 2, [VM] * 5)  1.88 us
  transfers between devices with their start and end apart: 9, of which 5 were waited for; matrix products, arithmetic and copies ran while one was open for 0% of the time, Pallas kernels for 17%

profile of v7, /device:TPU:0, one launch (start us, length us, event | category | flops | bytes accessed | tf_op | source)
XLA Modules:
  0.0 40.2 jit_solution(6162655348685574631)
XLA Ops:
  0.6 0.0 copy-start.6
  0.6 0.0 copy-start.5
  0.7 0.0 copy-start.7
  0.7 0.0 copy-start
  0.7 1.1 %copy-done = f32[12,16,8,128]{3,2,1,0:T(8,128)S(1)} copy-done((f32[12,16,8,128]{3,2,1,0:T(8,128)S(1)}, f32[12,16,8,128]{3,2,1,0:T(8,128)}, u32[]{:S(2)}) %copy-start) | copy-done | bytes 786456
  1.8 0.0 copy-start.1
  1.8 0.0 copy-start.2
  1.8 0.0 copy-start.4
  1.8 0.0 copy-start.3
  1.8 0.1 shard_map.105
  1.9 3.1 %collective-permute-start.1 = (f32[384,128]{1,0:T(8,128)S(1)}, f32[384,128]{1,0:T(8,128)S(1)}, u32[]{:S(2)}, u32[]{:S(2)}) collective-permute-start(f32[384,128]{1,0:T(8,128)S(1)} %get-tuple-element.28), channel_id=1, source_target_pairs={{0,1},{2,3},{4,5},{6,7},{1,0},{3,2},{5,4},{7,6},{8,9},{10,11},{12,... | collective-permute-start | bytes 589832 | tf_op jit(solution)/shard_map/ppermute | solution.py:574
  5.0 0.7 %collective-permute-start.2 = (f32[384,128]{1,0:T(8,128)S(1)}, f32[384,128]{1,0:T(8,128)S(1)}, u32[]{:S(2)}, u32[]{:S(2)}) collective-permute-start(f32[384,128]{1,0:T(8,128)S(1)} %get-tuple-element.29), channel_id=1, source_target_pairs={{1,2},{3,4},{5,6},{2,1},{4,3},{6,5},{9,10},{11,12},{13,14},{10,9},... | collective-permute-start | bytes 589832 | tf_op jit(solution)/shard_map/ppermute | solution.py:575
  5.7 0.1 collective-permute-start
  5.8 0.7 %collective-permute-start.3 = (f32[192,128]{1,0:T(8,128)S(1)}, f32[192,128]{1,0:T(8,128)S(1)}, u32[]{:S(2)}, u32[]{:S(2)}) collective-permute-start(f32[192,128]{1,0:T(8,128)S(1)} %get-tuple-element.30), channel_id=1, source_target_pairs={{8,16},{16,8},{9,17},{17,9},{10,18},{18,10},{11,19},{19,11},{12,20... | collective-permute-start | bytes 294920 | tf_op jit(solution)/shard_map/ppermute | solution.py:577
  6.4 0.6 %collective-permute-done.x1 = f32[192,128]{1,0:T(8,128)S(1)} collective-permute-done((f32[192,128]{1,0:T(8,128)S(1)}, f32[192,128]{1,0:T(8,128)S(1)}, u32[]{:S(2)}, u32[]{:S(2)}) %collective-permute-start) | collective-permute-done | bytes 98336 | tf_op jit(solution)/shard_map/ppermute | solution.py:578
  7.0 0.0 copy-done.6
  7.0 0.0 copy-done.5
  7.0 0.0 copy-done.7
  7.0 0.0 copy-done.1
  7.1 0.0 copy-done.2
  7.1 0.0 copy-done.4
  7.1 2.3 %shard_map.104 = (f32[1536,128]{1,0:T(8,128)S(1)}, bf16[2,1536,192]{2,1,0:T(8,128)(2,1)S(1)}, bf16[2,192,1536]{2,1,0:T(8,128)(2,1)S(1)}, bf16[2,192,384]{2,1,0:T...) custom-call(f32[1536,128]{1,0:T(8,128)S(1)} %bitcast.10, ...), custom_call_target="tpu_custom_call" | custom-call | flops 10000000 | bytes 1000000 | tf_op jit(solution)/shard_map/pallas_call | solution.py:580
  9.4 0.0 collective-permute-done.3.x2
  9.4 3.9 %collective-permute-done.1.y1 = f32[384,128]{1,0:T(8,128)S(1)} collective-permute-done((f32[384,128]{1,0:T(8,128)S(1)}, f32[384,128]{1,0:T(8,128)S(1)}, u32[]{:S(2)}, u32[]{:S(2)}) %collective-permute-start.1) | collective-permute-done | bytes 196640 | tf_op jit(solution)/shard_map/ppermute | solution.py:574
  13.3 0.0 collective-permute-done.2.y2
  13.3 0.0 copy-done.3
  13.3 2.4 %shard_map.106 = (f32[1536,128]{1,0:T(8,128)S(1)}, f32[232,128]{1,0:T(8,128)S(1)}, f32[24,128]{1,0:T(8,128)S(1)}) custom-call(f32[1536,128]{1,0:T(8,128)S(1)} %bitcast.11, f32[1536,128]{1,0:T(8,128)S(1)} %get-tuple-element.27.s_ref, f32[384,128]{1,0:T(8,128)S(1)} %collective-permute-done.1.y1, f32[384,128]{1,0:T(8,128)S(1)} %collective-permute-done.2.y2, ...), custom_call_target="tpu_custom_call" | custom-call | flops 10000000 | bytes 1000000 | tf_op jit(solution)/shard_map/pallas_call | solution.py:593
  15.7 1.6 %collective-permute-start.4 = (f32[232,128]{1,0:T(8,128)S(1)}, f32[232,128]{1,0:T(8,128)S(1)}, u32[]{:S(2)}, u32[]{:S(2)}) collective-permute-start(f32[232,128]{1,0:T(8,128)S(1)} %get-tuple-element.34.own_ref.refs_0_), channel_id=1, source_target_pairs={{0,16},{8,24},{16,0},{24,8},{1,17},{9,25},{17,1},{25,9},{2,18},{10... | collective-permute-start | bytes 356360 | tf_op jit(solution)/shard_map/ppermute | solution.py:554
  17.3 0.0 collective-permute-start.5
  17.3 3.3 %collective-permute-done.4.refs_0_.refs_1_ = f32[232,128]{1,0:T(8,128)S(1)} collective-permute-done((f32[232,128]{1,0:T(8,128)S(1)}, f32[232,128]{1,0:T(8,128)S(1)}, u32[]{:S(2)}, u32[]{:S(2)}) %collective-permute-start.4) | collective-permute-done | bytes 118816 | tf_op jit(solution)/shard_map/ppermute | solution.py:554
  20.6 0.0 collective-permute-start.6
  20.6 0.5 %collective-permute-start.7 = (f32[24,128]{1,0:T(8,128)S(1)}, f32[24,128]{1,0:T(8,128)S(1)}, u32[]{:S(2)}, u32[]{:S(2)}) collective-permute-start(f32[24,128]{1,0:T(8,128)S(1)} %get-tuple-element.37), channel_id=1, source_target_pairs={{0,8},{16,24},{8,0},{24,16},{1,9},{17,25},{9,1},{25,17},{2,10},{18... | collective-permute-start | bytes 36872 | tf_op jit(solution)/shard_map/ppermute | solution.py:604
  21.1 0.8 %collective-permute-done.7.near_ref = f32[24,128]{1,0:T(8,128)S(1)} collective-permute-done((f32[24,128]{1,0:T(8,128)S(1)}, f32[24,128]{1,0:T(8,128)S(1)}, u32[]{:S(2)}, u32[]{:S(2)}) %collective-permute-start.7) | collective-permute-done | bytes 12320 | tf_op jit(solution)/shard_map/ppermute | solution.py:604
  22.0 1.5 %shard_map.107 = (f32[128,384]{1,0:T(8,128)S(1)}, f32[8,128]{1,0:T(8,128)S(1)}) custom-call(f32[1536,128]{1,0:T(8,128)S(1)} %get-tuple-element.35.state_ref.refs_4_, f32[24,128]{1,0:T(8,128)S(1)} %collective-permute-done.7.near_ref, bf16[2,512,128]{2,1,0:T(8,128)(2,1)S(1)} %get-tuple-element.36.n_ref.refs_5_), custom_call_target="tpu_custom_call" | custom-call | flops 10000000 | bytes 1000000 | tf_op jit(solution)/shard_map/pallas_call | solution.py:606
  23.4 0.0 collective-permute-done.5.refs_1_.refs_2_
  23.4 0.5 %shard_map.108.refs_1_ = f32[128,192]{1,0:T(8,128)S(1)} custom-call(f32[232,128]{1,0:T(8,128)S(1)} %get-tuple-element.34.own_ref.refs_0_, f32[232,128]{1,0:T(8,128)S(1)} %get-tuple-element.34.own_ref.refs_0_, f32[232,128]{1,0:T(8,128)S(1)} %collective-permute-done.5.refs_1_.refs_2_), custom_call_target="tpu_custom_call" | custom-call | flops 10000000 | bytes 1000000 | tf_op jit(solution)/shard_map/pallas_call | solution.py:613
  24.0 0.7 %shard_map.109 = (f32[128,192]{1,0:T(8,128)S(1)}, f32[128,384]{1,0:T(8,128)S(1)}) custom-call(f32[232,128]{1,0:T(8,128)S(1)} %get-tuple-element.34.own_ref.refs_0_, f32[232,128]{1,0:T(8,128)S(1)} %collective-permute-done.4.refs_0_.refs_1_, f32[128,192]{1,0:T(8,128)S(1)} %shard_map.108.refs_1_, f32[128,384]{1,0:T(8,128)S(1)} %get-tuple-element.40.refs_2_, ...), custom_call_target="tpu_custom_call" | custom-call | flops 10000000 | bytes 1000000 | tf_op jit(solution)/shard_map/pallas_call | solution.py:616
  24.7 0.0 collective-permute-done.6.refs_3_
  24.7 1.8 %shard_map.110 = (f32[128,192]{1,0:T(8,128)S(1)}, f32[24,128]{1,0:T(8,128)S(1)}, f32[32,128]{1,0:T(8,128)}) custom-call(f32[232,128]{1,0:T(8,128)S(1)} %get-tuple-element.34.own_ref.refs_0_, f32[232,128]{1,0:T(8,128)S(1)} %collective-permute-done.4.refs_0_.refs_1_, f32[232,128]{1,0:T(8,128)S(1)} %collective-permute-done.5.refs_1_.refs_2_, ...), custom_call_target="tpu_custom_call" | custom-call | flops 10000000 | bytes 1000000 | tf_op jit(solution)/shard_map/pallas_call | solution.py:624
  26.4 5.9 %all-to-all-start = ((f32[32,1,128]{2,1,0:T(1,128)}), f32[32,1,128]{2,1,0:T(1,128)S(1)}, u32[]{:S(2)}, u32[]{:S(2)}) async-start(f32[32,1,128]{2,1,0:T(1,128)} %bitcast.6), calls=%async_computation | async-start | bytes 32768 | tf_op jit(solution)/shard_map/all_to_all | solution.py:641
  32.4 1.9 %shard_map.111 = (f32[1536,128]{1,0:T(8,128)}, f32[1536,128]{1,0:T(8,128)}) custom-call(f32[128,192]{1,0:T(8,128)S(1)} %get-tuple-element.43.d_ref, bf16[2,192,1536]{2,1,0:T(8,128)(2,1)S(1)} %get-tuple-element.44.t_ref, f32[24,128]{1,0:T(8,128)S(1)} %get-tuple-element.45.lack_ref, f32[24,128]{1,0:T(8,128)S(1)} %collective-permute-done.7.near_ref, ...), custom_call_target="tpu_custom_call" | custom-call | flops 10000000 | bytes 1000000 | tf_op jit(solution)/shard_map/pallas_call | solution.py:635
  34.3 5.3 %all-to-all-done = f32[32,1,128]{2,1,0:T(1,128)S(1)} async-done(((f32[32,1,128]{2,1,0:T(1,128)}), f32[32,1,128]{2,1,0:T(1,128)S(1)}, u32[]{:S(2)}, u32[]{:S(2)}) %all-to-all-start) | async-done | bytes 16416 | tf_op jit(solution)/shard_map/all_to_all | solution.py:641
  39.5 0.1 reduce_sum.9
  39.6 0.6 %fusion = f32[12]{0:T(128)} fusion(f32[128]{0:T(128)S(1)} %reduce_sum.9), kind=kLoop, calls=%fused_computation.1 | loop fusion | flops 24 | bytes 144 | tf_op jit(solution)/shard_map/sqrt | solution.py:642
  (1 shorter events, 0.0 us)
Async XLA Ops:
  0.6 6.4 %copy-start.6 = (f32[12]{0:T(128)S(1)}, f32[12]{0:T(128)}, u32[]{:S(2)}) copy-start(f32[12]{0:T(128)} %act.3) | copy-start | bytes 148
  0.6 6.4 %copy-start.5 = (f32[12]{0:T(128)S(1)}, f32[12]{0:T(128)}, u32[]{:S(2)}) copy-start(f32[12]{0:T(128)} %dif.3) | copy-start | bytes 148
  0.7 6.4 %copy-start.7 = (f32[12]{0:T(128)S(1)}, f32[12]{0:T(128)}, u32[]{:S(2)}) copy-start(f32[12]{0:T(128)} %pre.1) | copy-start | bytes 148
  0.7 1.2 %copy-start = (f32[12,16,8,128]{3,2,1,0:T(8,128)S(1)}, f32[12,16,8,128]{3,2,1,0:T(8,128)}, u32[]{:S(2)}) copy-start(f32[12,16,8,128]{3,2,1,0:T(8,128)} %param.9) | copy-start | bytes 2359300
  1.8 5.2 %copy-start.1 = (f32[128,32]{0,1:T(8,128)S(1)}, f32[128,32]{0,1:T(8,128)}, u32[]{:S(2)}) copy-start(f32[128,32]{0,1:T(8,128)} %param.15) | copy-start | bytes 49156
  1.8 5.2 %copy-start.2 = (f32[12,12]{1,0:T(8,128)S(1)}, f32[12,12]{1,0:T(8,128)}, u32[]{:S(2)}) copy-start(f32[12,12]{1,0:T(8,128)} %mix_ref.1) | copy-start | bytes 1732
  1.8 5.3 %copy-start.4 = (f32[12,6]{0,1:T(8,128)S(1)}, f32[12,6]{0,1:T(8,128)}, u32[]{:S(2)}) copy-start(f32[12,6]{0,1:T(8,128)} %param.16) | copy-start | bytes 868
  1.8 11.5 %copy-start.3 = (f32[16,64]{1,0:T(8,128)S(1)}, f32[16,64]{1,0:T(8,128)}, u32[]{:S(2)}) copy-start(f32[16,64]{1,0:T(8,128)} %bx_ref.1) | copy-start | bytes 12292
  1.9 11.4 %collective-permute-start.1 = (f32[384,128]{1,0:T(8,128)S(1)}, f32[384,128]{1,0:T(8,128)S(1)}, u32[]{:S(2)}, u32[]{:S(2)}) collective-permute-start(f32[384,128]{1,0:T(8,128)S(1)} %get-tuple-element.28), channel_id=1, source_target_pairs={{0,1},{2,3},{4,5},{6,7},{1,0},{3,2},{5,4},{7,6},{8,9},{10,11},{12,... | collective-permute-start | bytes 589832 | tf_op jit(solution)/shard_map/ppermute | solution.py:574
  5.0 8.4 %collective-permute-start.2 = (f32[384,128]{1,0:T(8,128)S(1)}, f32[384,128]{1,0:T(8,128)S(1)}, u32[]{:S(2)}, u32[]{:S(2)}) collective-permute-start(f32[384,128]{1,0:T(8,128)S(1)} %get-tuple-element.29), channel_id=1, source_target_pairs={{1,2},{3,4},{5,6},{2,1},{4,3},{6,5},{9,10},{11,12},{13,14},{10,9},... | collective-permute-start | bytes 589832 | tf_op jit(solution)/shard_map/ppermute | solution.py:575
  5.7 1.4 %collective-permute-start = (f32[192,128]{1,0:T(8,128)S(1)}, f32[192,128]{1,0:T(8,128)S(1)}, u32[]{:S(2)}, u32[]{:S(2)}) collective-permute-start(f32[192,128]{1,0:T(8,128)S(1)} %get-tuple-element.26), channel_id=1, source_target_pairs={{0,8},{16,24},{8,0},{24,16},{1,9},{17,25},{9,1},{25,17},{2,10},{18... | collective-permute-start | bytes 294920 | tf_op jit(solution)/shard_map/ppermute | solution.py:578
  5.8 3.6 %collective-permute-start.3 = (f32[192,128]{1,0:T(8,128)S(1)}, f32[192,128]{1,0:T(8,128)S(1)}, u32[]{:S(2)}, u32[]{:S(2)}) collective-permute-start(f32[192,128]{1,0:T(8,128)S(1)} %get-tuple-element.30), channel_id=1, source_target_pairs={{8,16},{16,8},{9,17},{17,9},{10,18},{18,10},{11,19},{19,11},{12,20... | collective-permute-start | bytes 294920 | tf_op jit(solution)/shard_map/ppermute | solution.py:577
  15.7 4.9 %collective-permute-start.4 = (f32[232,128]{1,0:T(8,128)S(1)}, f32[232,128]{1,0:T(8,128)S(1)}, u32[]{:S(2)}, u32[]{:S(2)}) collective-permute-start(f32[232,128]{1,0:T(8,128)S(1)} %get-tuple-element.34.own_ref.refs_0_), channel_id=1, source_target_pairs={{0,16},{8,24},{16,0},{24,8},{1,17},{9,25},{17,1},{25,9},{2,18},{10... | collective-permute-start | bytes 356360 | tf_op jit(solution)/shard_map/ppermute | solution.py:554
  17.3 6.2 %collective-permute-start.5 = (f32[232,128]{1,0:T(8,128)S(1)}, f32[232,128]{1,0:T(8,128)S(1)}, u32[]{:S(2)}, u32[]{:S(2)}) collective-permute-start(f32[232,128]{1,0:T(8,128)S(1)} %get-tuple-element.34.own_ref.refs_0_), channel_id=1, source_target_pairs={{0,8},{8,0},{16,24},{24,16},{1,9},{9,1},{17,25},{25,17},{2,10},{10... | collective-permute-start | bytes 356360 | tf_op jit(solution)/shard_map/ppermute | solution.py:554
  20.6 4.1 %collective-permute-start.6 = (f32[232,128]{1,0:T(8,128)S(1)}, f32[232,128]{1,0:T(8,128)S(1)}, u32[]{:S(2)}, u32[]{:S(2)}) collective-permute-start(f32[232,128]{1,0:T(8,128)S(1)} %collective-permute-done.4.refs_0_.refs_1_), channel_id=1, source_target_pairs={{0,8},{8,0},{16,24},{24,16},{1,9},{9,1},{17,25},{25,17},{2,10},{10... | collective-permute-start | bytes 356360 | tf_op jit(solution)/shard_map/ppermute | solution.py:554
  20.6 1.3 %collective-permute-start.7 = (f32[24,128]{1,0:T(8,128)S(1)}, f32[24,128]{1,0:T(8,128)S(1)}, u32[]{:S(2)}, u32[]{:S(2)}) collective-permute-start(f32[24,128]{1,0:T(8,128)S(1)} %get-tuple-element.37), channel_id=1, source_target_pairs={{0,8},{16,24},{8,0},{24,16},{1,9},{17,25},{9,1},{25,17},{2,10},{18... | collective-permute-start | bytes 36872 | tf_op jit(solution)/shard_map/ppermute | solution.py:604
  26.4 13.1 %all-to-all-start = ((f32[32,1,128]{2,1,0:T(1,128)}), f32[32,1,128]{2,1,0:T(1,128)S(1)}, u32[]{:S(2)}, u32[]{:S(2)}) async-start(f32[32,1,128]{2,1,0:T(1,128)} %bitcast.6), calls=%async_computation | async-start | bytes 32768 | tf_op jit(solution)/shard_map/all_to_all | solution.py:641

commit v8 on v7

--- a/solution.py
+++ b/solution.py
@@ -1,4 +1,5 @@
 import functools
+import math
 
 import jax
 import jax.numpy as jnp
@@ -58,8 +59,8 @@
 
 def reaction(ws, act, both, low):
     n = len(ws)
-    cold = -1.0 / (1.5 + jnp.tanh(ws[0]))
-    rates = [tiles_of(jnp.exp(act[v] * cold) * ws[v]) for v in range(n)]
+    cold = -math.log2(math.e) / (1.5 + jnp.tanh(ws[0]))
+    rates = [tiles_of(jnp.exp2(act[v] * cold) * ws[v]) for v in range(n)]
     count, lanes = rates[0].shape[0], rates[0].shape[2]
     stacked = jnp.concatenate(
         [jnp.concatenate([rates[v][t] for v in range(n)], axis=0) for t in range(count)], axis=1
@@ -88,8 +89,9 @@
             first = rows(v, x - 1, 1) if x > 0 else low_edge(v)[None]
             last = rows(v, x + step, 1) if x + step < rows_x else high_edge(v)[None]
             beside = jnp.concatenate([first, w[:-1]], 0) + jnp.concatenate([w[1:], last], 0)
-            lap = beside + shifted(w, 1) + shifted(w, 2) - 6.0 * w
-            emit(v, x, step, w, dif[v] * lap + made[v])
+            around = beside + shifted(w, 1) + shifted(w, 2)
+            kept = (1.0 - 6.0 * dif[v]) * w
+            emit(v, x, step, kept + (dif[v] * around + made[v]))
 
 
 def odd(axis):
@@ -147,8 +149,8 @@
     both = jnp.concatenate([hi, hi], axis=1)
     both_ref[...], low_ref[...] = both, lo
 
-    def emit(v, x, n, w, t):
-        s_ref[pl.ds(v * size + x * rows_y, n * rows_y), :] = (w + t).reshape(n * rows_y, lanes)
+    def emit(v, x, n, made):
+        s_ref[pl.ds(v * size + x * rows_y, n * rows_y), :] = made.reshape(n * rows_y, lanes)
 
     def near(is_low):
         is_near = odd("gx") if is_low else jnp.logical_not(odd("gx"))
@@ -233,16 +235,16 @@
         at = pl.ds(pl.multiple_of(v * size + edges[0] * rows_y, rows_y), rows_y)
         sec[at, :] = sec[at, :] + dif[v] * x2[pl.ds(v * rows_y, rows_y), :]
 
-    def emit(v, x, n, w, t):
+    def emit(v, x, n, made):
         at = pl.ds(v * size + x * rows_y, n * rows_y)
-        state_ref[at, :] = 0.5 * ((f_ref[at, :] + w.reshape(n * rows_y, lanes)) + t.reshape(n * rows_y, lanes))
+        state_ref[at, :] = 0.5 * (f_ref[at, :] + made.reshape(n * rows_y, lanes))
 
     stage(
         sec, nv, rows_x, rows_y, dif, act, mixers, emit,
         lambda v: gx_ref[pl.ds(v * 2 * rows_y, rows_y), :],
         lambda v: gx_ref[pl.ds((v * 2 + 1) * rows_y, rows_y), :],
     )
-    his, los = [], []
+    total, his, los = 0.0, [], []
     spot = spots(dims, k_ref.shape[2], bx_ref.shape[1])[2]
     for v in range(nv):
         half = 0.5 * dif[v]
@@ -259,7 +261,10 @@
         hi, lo = split(jnp.concatenate(rows, axis=0))
         his.append(hi)
         los.append(lo)
-    total = mm3((jnp.concatenate(his, 1), jnp.concatenate(los, 1)), (k_ref[0], k_ref[1]))
+        if len(his) == 2 or v == nv - 1:
+            at = pl.ds((v + 1 - len(his)) * lanes, len(his) * lanes)
+            part = mm3((jnp.concatenate(his, 1), jnp.concatenate(los, 1)), (k_ref[0, at, :], k_ref[1, at, :]))
+            total, his, los = total + part, [], []
     pack_message(dims, m_ref, total[:size], bx_ref[...], total[size:])
 
 
@@ -488,7 +493,7 @@
 
 def third_kernel(dims, rank_z, width, rank_x, masks, *refs):
     n = len(masks)
-    state_ref, n_ref, row_ref, u_ref, part_ref, gap_ref, d_ref, lack_ref, sums_ref = refs[n:]
+    state_ref, n_ref, row_ref, u_ref, gap_ref, lack_ref, sums_ref = refs[n:]
     rows_y = dims[2]
     values, own, bases = last_values(dims, width, rank_x, masks, refs[:n])
     lack = find_lack(dims, width, rank_x, masks, refs[:n])
@@ -504,7 +509,6 @@
     gap = put_edge(gap_ref[...], edge_coefs(rows_y, coefs)) - gap
     total_sums(gap, (row_ref[0:1, :], row), sums_ref, rank_z)
     lack_ref[...] = lack
-    d_ref[...] = part_ref[...] + mm3(link, values)
 
 
 def mix_kernel(dims, width, rank_x, masks, *refs):
@@ -523,10 +527,10 @@
     total_sums(gap, (row_ref[0:1, :], row), sums_ref, rank_z)
 
 
-def decode_kernel(dims, d_ref, t_ref, lack_ref, near_ref, state_ref, recon_ref, out_ref):
+def decode_into(dims, mixed, t_ref, lack_ref, near_ref, state_ref, recon_ref, out_ref):
     nv, rows_x, rows_y, lanes = dims
     size = rows_x * rows_y
-    halves = split(d_ref[...])
+    halves = split(mixed)
     far = far_side()
     starts = (jnp.where(far, size - rows_y, 0), jnp.where(far, 0, size - rows_y))
     for v in range(nv):
@@ -537,6 +541,16 @@
             out_ref[at, :] = state_ref[at, :] + tile_of(ref, nv, v, rows_y)
         cols = slice(v * lanes, (v + 1) * lanes)
         recon_ref[whole, :] = mm3(halves, (t_ref[0, :, cols], t_ref[1, :, cols]))
+
+
+def decode_kernel(dims, d_ref, *refs):
+    decode_into(dims, d_ref[...], *refs)
+
+
+def finish_kernel(dims, width, rank_x, masks, *refs):
+    n = len(masks)
+    values, own, bases = last_values(dims, width, rank_x, masks, refs[:n])
+    decode_into(dims, refs[n][...] + mm3(link_to(own, bases, dims[2]), values), *refs[n + 1 :])
 
 
 def pairs(n, first):
@@ -621,9 +635,10 @@
     mixing_args = (width, rank_x, masks)
     rest = (state, n, row, u)
     if basis_y.shape[0] * gy == basis_y.shape[1]:
-        mixed, lack, sums = call(
-            functools.partial(third_kernel, dims, rank_z, *mixing_args), outs, [VM] * (count + 6)
-        )(*blocks, *rest, premixed, gap)
+        lack, sums = call(
+            functools.partial(third_kernel, dims, rank_z, *mixing_args), outs[1:], [VM] * (count + 5)
+        )(*blocks, *rest, gap)
+        decode, given = functools.partial(finish_kernel, dims, *mixing_args), (*blocks, premixed)
     else:
         mixed, lack = call(
             functools.partial(mix_kernel, dims, *mixing_args), outs[:2], [VM] * (count + 1)
@@ -632,8 +647,9 @@
         core = lax.psum(jnp.einsum("xyk,yb->xbk", mixed, basis_y, precision=HIGH), "gy")
         mixed = jnp.einsum("xbk,yb->xyk", core, basis_y, precision=HIGH).reshape(size, width)
         (sums,) = call(functools.partial(settle_kernel, dims, rank_z), outs[2:], [VM] * 7)(mixed, lack, *rest, coefs)
-    recon, state = call(functools.partial(decode_kernel, dims), [(block, f32)] * 2, [VM] * 5)(
-        mixed, t, lack, near, state
+        decode, given = functools.partial(decode_kernel, dims), (mixed,)
+    recon, state = call(decode, [(block, f32)] * 2, [VM] * (len(given) + 4))(
+        *given, t, lack, near, state
     )
     if peers > 64:
         sums = lax.psum(sums[0], ("gx", "gy"))

time: 40.4 us -> 40.2 us (level)
  waiting for transfers between devices: 14 us -> 13.5 us
    all_to_all x1, waiting for transfers between devices: 5.26 us -> 4.72 us  [program(): sums = jnp.sum(lax.all_to_all(sums, ('gx', 'gy'), 0, 0, tiled=True), axis=0)]
    pallas_call x2, Pallas kernels: 3.64 us -> 4.04 us  [the longest x1 2.42 us: program(): call(decode, [(block, f32)] * 2, [VM] * (len(given) + 4))]
  transfers between devices with their start and end apart: 9 -> 9, of which waited for: 5 -> 5; matrix products, arithmetic and copies ran while one was open for 0% -> 0% of each run, Pallas kernels for 17% -> 19%
where the time goes in v8:
time: 40.2 us; the launch traced here: 40 us
  waiting for transfers between devices  13.5 us (34%)
  starting transfers between devices  12.5 us (31%)
  Pallas kernels  11.4 us (28%)
  local copies, waits for them, and re-layouts  1.17 us (3%)
  between operations  0.79 us (2%)
  other arithmetic  0.65 us (2%)
    all_to_all x1, starting transfers between devices, program(): sums = jnp.sum(lax.all_to_all(sums, ('gx', 'gy'), 0, 0, tiled=True), axis=0)  5.96 us
    all_to_all x1, waiting for transfers between devices, program(): sums = jnp.sum(lax.all_to_all(sums, ('gx', 'gy'), 0, 0, tiled=True), axis=0)  4.72 us
    ppermute x1, waiting for transfers between devices, program(): y1 = lax.ppermute(p1, 'gy', pairs(gy, 0))  3.97 us
    ppermute x3, waiting for transfers between devices, gather_blocks(): blocks = blocks + [lax.ppermute(b, 'gx', swaps) for b in blocks]  3.34 us
    ppermute x1, starting transfers between devices, program(): y1 = lax.ppermute(p1, 'gy', pairs(gy, 0))  3.06 us
    pallas_call x1, Pallas kernels, program(): call(decode, [(block, f32)] * 2, [VM] * (len(given) + 4))  2.42 us
    pallas_call x1, Pallas kernels, program(): call(functools.partial(first_kernel, dims), [(block, f32), ((2, nv * lane...  2.27 us
    pallas_call x1, Pallas kernels, program(): call(functools.partial(second_kernel, dims), [(block, f32), ((spots(dims,...  2.26 us
  transfers between devices with their start and end apart: 9, of which 5 were waited for; matrix products, arithmetic and copies ran while one was open for 0% of the time, Pallas kernels for 19%

profile of v8, /device:TPU:0, one launch (start us, length us, event | category | flops | bytes accessed | tf_op | source)
XLA Modules:
  0.0 40.0 jit_solution(16546449768815374898)
XLA Ops:
  0.6 0.0 copy-start.6
  0.6 0.0 copy-start.5
  0.7 0.0 copy-start.7
  0.7 0.0 copy-start
  0.7 1.1 %copy-done = f32[12,16,8,128]{3,2,1,0:T(8,128)S(1)} copy-done((f32[12,16,8,128]{3,2,1,0:T(8,128)S(1)}, f32[12,16,8,128]{3,2,1,0:T(8,128)}, u32[]{:S(2)}) %copy-start) | copy-done | bytes 786456
  1.8 0.0 copy-start.1
  1.8 0.0 copy-start.2
  1.8 0.0 copy-start.4
  1.8 0.0 copy-start.3
  1.8 0.1 shard_map.105
  1.9 3.1 %collective-permute-start.1 = (f32[384,128]{1,0:T(8,128)S(1)}, f32[384,128]{1,0:T(8,128)S(1)}, u32[]{:S(2)}, u32[]{:S(2)}) collective-permute-start(f32[384,128]{1,0:T(8,128)S(1)} %get-tuple-element.27), channel_id=1, source_target_pairs={{0,1},{2,3},{4,5},{6,7},{1,0},{3,2},{5,4},{7,6},{8,9},{10,11},{12,... | collective-permute-start | bytes 589832 | tf_op jit(solution)/shard_map/ppermute | solution.py:588
  5.0 0.7 %collective-permute-start.2 = (f32[384,128]{1,0:T(8,128)S(1)}, f32[384,128]{1,0:T(8,128)S(1)}, u32[]{:S(2)}, u32[]{:S(2)}) collective-permute-start(f32[384,128]{1,0:T(8,128)S(1)} %get-tuple-element.28), channel_id=1, source_target_pairs={{1,2},{3,4},{5,6},{2,1},{4,3},{6,5},{9,10},{11,12},{13,14},{10,9},... | collective-permute-start | bytes 589832 | tf_op jit(solution)/shard_map/ppermute | solution.py:589
  5.7 0.1 collective-permute-start
  5.8 0.7 %collective-permute-start.3 = (f32[192,128]{1,0:T(8,128)S(1)}, f32[192,128]{1,0:T(8,128)S(1)}, u32[]{:S(2)}, u32[]{:S(2)}) collective-permute-start(f32[192,128]{1,0:T(8,128)S(1)} %get-tuple-element.29), channel_id=1, source_target_pairs={{8,16},{16,8},{9,17},{17,9},{10,18},{18,10},{11,19},{19,11},{12,20... | collective-permute-start | bytes 294920 | tf_op jit(solution)/shard_map/ppermute | solution.py:591
  6.4 0.6 %collective-permute-done.x1 = f32[192,128]{1,0:T(8,128)S(1)} collective-permute-done((f32[192,128]{1,0:T(8,128)S(1)}, f32[192,128]{1,0:T(8,128)S(1)}, u32[]{:S(2)}, u32[]{:S(2)}) %collective-permute-start) | collective-permute-done | bytes 98336 | tf_op jit(solution)/shard_map/ppermute | solution.py:592
  7.0 0.0 copy-done.6
  7.0 0.0 copy-done.5
  7.0 0.0 copy-done.7
  7.0 0.0 copy-done.1
  7.1 0.0 copy-done.2
  7.1 0.0 copy-done.4
  7.1 2.3 %shard_map.104 = (f32[1536,128]{1,0:T(8,128)S(1)}, bf16[2,1536,192]{2,1,0:T(8,128)(2,1)S(1)}, bf16[2,192,1536]{2,1,0:T(8,128)(2,1)S(1)}, bf16[2,192,384]{2,1,0:T...) custom-call(f32[1536,128]{1,0:T(8,128)S(1)} %bitcast.10, ...), custom_call_target="tpu_custom_call" | custom-call | flops 10000000 | bytes 1000000 | tf_op jit(solution)/shard_map/pallas_call | solution.py:594
  9.4 0.0 collective-permute-done.3.x2
  9.4 4.0 %collective-permute-done.1.y1 = f32[384,128]{1,0:T(8,128)S(1)} collective-permute-done((f32[384,128]{1,0:T(8,128)S(1)}, f32[384,128]{1,0:T(8,128)S(1)}, u32[]{:S(2)}, u32[]{:S(2)}) %collective-permute-start.1) | collective-permute-done | bytes 196640 | tf_op jit(solution)/shard_map/ppermute | solution.py:588
  13.3 0.0 collective-permute-done.2.y2
  13.3 0.0 copy-done.3
  13.3 2.3 %shard_map.106 = (f32[1536,128]{1,0:T(8,128)S(1)}, f32[232,128]{1,0:T(8,128)S(1)}, f32[24,128]{1,0:T(8,128)S(1)}) custom-call(f32[1536,128]{1,0:T(8,128)S(1)} %bitcast.11, f32[1536,128]{1,0:T(8,128)S(1)} %get-tuple-element.26.s_ref, f32[384,128]{1,0:T(8,128)S(1)} %collective-permute-done.1.y1, f32[384,128]{1,0:T(8,128)S(1)} %collective-permute-done.2.y2, ...), custom_call_target="tpu_custom_call" | custom-call | flops 10000000 | bytes 1000000 | tf_op jit(solution)/shard_map/pallas_call | solution.py:607
  15.6 1.6 %collective-permute-start.4 = (f32[232,128]{1,0:T(8,128)S(1)}, f32[232,128]{1,0:T(8,128)S(1)}, u32[]{:S(2)}, u32[]{:S(2)}) collective-permute-start(f32[232,128]{1,0:T(8,128)S(1)} %get-tuple-element.33.own_ref.refs_0_), channel_id=1, source_target_pairs={{0,16},{8,24},{16,0},{24,8},{1,17},{9,25},{17,1},{25,9},{2,18},{10... | collective-permute-start | bytes 356360 | tf_op jit(solution)/shard_map/ppermute | solution.py:568
  17.2 0.0 collective-permute-start.5
  17.2 3.3 %collective-permute-done.4.refs_0_.refs_1_ = f32[232,128]{1,0:T(8,128)S(1)} collective-permute-done((f32[232,128]{1,0:T(8,128)S(1)}, f32[232,128]{1,0:T(8,128)S(1)}, u32[]{:S(2)}, u32[]{:S(2)}) %collective-permute-start.4) | collective-permute-done | bytes 118816 | tf_op jit(solution)/shard_map/ppermute | solution.py:568
  20.5 0.0 collective-permute-start.6
  20.5 0.5 %collective-permute-start.7 = (f32[24,128]{1,0:T(8,128)S(1)}, f32[24,128]{1,0:T(8,128)S(1)}, u32[]{:S(2)}, u32[]{:S(2)}) collective-permute-start(f32[24,128]{1,0:T(8,128)S(1)} %get-tuple-element.35), channel_id=1, source_target_pairs={{0,8},{16,24},{8,0},{24,16},{1,9},{17,25},{9,1},{25,17},{2,10},{18... | collective-permute-start | bytes 36872 | tf_op jit(solution)/shard_map/ppermute | solution.py:618
  21.0 0.8 %collective-permute-done.7.near_ref.refs_7_ = f32[24,128]{1,0:T(8,128)S(1)} collective-permute-done((f32[24,128]{1,0:T(8,128)S(1)}, f32[24,128]{1,0:T(8,128)S(1)}, u32[]{:S(2)}, u32[]{:S(2)}) %collective-permute-start.7) | collective-permute-done | bytes 12320 | tf_op jit(solution)/shard_map/ppermute | solution.py:618
  21.9 1.5 %shard_map.108 = (f32[128,384]{1,0:T(8,128)S(1)}, f32[8,128]{1,0:T(8,128)S(1)}) custom-call(f32[1536,128]{1,0:T(8,128)S(1)} %get-tuple-element.34.state_ref.refs_4_.refs_8_, f32[24,128]{1,0:T(8,128)S(1)} %collective-permute-done.7.near_ref.refs_7_, bf16[2,512,128]{2,1,0:T(8,128)(2,1)S(1)} %get-tuple-element.36.n_ref.refs_5_), custom_call_target="tpu_custom_call" | custom-call | flops 10000000 | bytes 1000000 | tf_op jit(solution)/shard_map/pallas_call | solution.py:620
  23.3 0.0 collective-permute-done.5.refs_1_.refs_2_
  23.3 0.5 %shard_map.107.refs_1_ = f32[128,192]{1,0:T(8,128)S(1)} custom-call(f32[232,128]{1,0:T(8,128)S(1)} %get-tuple-element.33.own_ref.refs_0_, f32[232,128]{1,0:T(8,128)S(1)} %get-tuple-element.33.own_ref.refs_0_, f32[232,128]{1,0:T(8,128)S(1)} %collective-permute-done.5.refs_1_.refs_2_), custom_call_target="tpu_custom_call" | custom-call | flops 10000000 | bytes 1000000 | tf_op jit(solution)/shard_map/pallas_call | solution.py:627
  23.8 0.7 %shard_map.109 = (f32[128,192]{1,0:T(8,128)S(1)}, f32[128,384]{1,0:T(8,128)S(1)}) custom-call(f32[232,128]{1,0:T(8,128)S(1)} %get-tuple-element.33.own_ref.refs_0_, f32[232,128]{1,0:T(8,128)S(1)} %collective-permute-done.4.refs_0_.refs_1_, f32[128,192]{1,0:T(8,128)S(1)} %shard_map.107.refs_1_, f32[128,384]{1,0:T(8,128)S(1)} %get-tuple-element.37.refs_2_, ...), custom_call_target="tpu_custom_call" | custom-call | flops 10000000 | bytes 1000000 | tf_op jit(solution)/shard_map/pallas_call | solution.py:630
  24.6 0.0 collective-permute-done.6.refs_3_
  24.6 1.6 %shard_map.110 = (f32[24,128]{1,0:T(8,128)S(1)}, f32[32,128]{1,0:T(8,128)}) custom-call(f32[232,128]{1,0:T(8,128)S(1)} %get-tuple-element.33.own_ref.refs_0_, f32[232,128]{1,0:T(8,128)S(1)} %collective-permute-done.4.refs_0_.refs_1_, f32[232,128]{1,0:T(8,128)S(1)} %collective-permute-done.5.refs_1_.refs_2_, f32[232,128]{1,0:T(8,128)S(1)} %collective-permute-done.6.refs_3_, ...), custom_call_target="tpu_custom_call" | custom-call | flops 10000000 | bytes 1000000 | tf_op jit(solution)/shard_map/pallas_call | solution.py:638
  26.2 6.0 %all-to-all-start = ((f32[32,1,128]{2,1,0:T(1,128)}), f32[32,1,128]{2,1,0:T(1,128)S(1)}, u32[]{:S(2)}, u32[]{:S(2)}) async-start(f32[32,1,128]{2,1,0:T(1,128)} %bitcast.6), calls=%async_computation | async-start | bytes 32768 | tf_op jit(solution)/shard_map/all_to_all | solution.py:657
  32.2 2.4 %shard_map.111 = (f32[1536,128]{1,0:T(8,128)}, f32[1536,128]{1,0:T(8,128)}) custom-call(f32[232,128]{1,0:T(8,128)S(1)} %get-tuple-element.33.own_ref.refs_0_, f32[232,128]{1,0:T(8,128)S(1)} %collective-permute-done.4.refs_0_.refs_1_, f32[232,128]{1,0:T(8,128)S(1)} %collective-permute-done.5.refs_1_.refs_2_, f32[232,128]{1,0:T(8,128)S(1)} %collective-permute-done.6.refs_3_, ...), custom_call_target="tpu_custom_call" | custom-call | flops 10000000 | bytes 1000000 | tf_op jit(solution)/shard_map/pallas_call | solution.py:651
  34.6 4.7 %all-to-all-done = f32[32,1,128]{2,1,0:T(1,128)S(1)} async-done(((f32[32,1,128]{2,1,0:T(1,128)}), f32[32,1,128]{2,1,0:T(1,128)S(1)}, u32[]{:S(2)}, u32[]{:S(2)}) %all-to-all-start) | async-done | bytes 16416 | tf_op jit(solution)/shard_map/all_to_all | solution.py:657
  39.3 0.1 reduce_sum.9
  39.4 0.6 %fusion = f32[12]{0:T(128)} fusion(f32[128]{0:T(128)S(1)} %reduce_sum.9), kind=kLoop, calls=%fused_computation.1 | loop fusion | flops 24 | bytes 144 | tf_op jit(solution)/shard_map/sqrt | solution.py:658
  (1 shorter events, 0.0 us)
Async XLA Ops:
  0.6 6.4 %copy-start.6 = (f32[12]{0:T(128)S(1)}, f32[12]{0:T(128)}, u32[]{:S(2)}) copy-start(f32[12]{0:T(128)} %act.3) | copy-start | bytes 148
  0.6 6.4 %copy-start.5 = (f32[12]{0:T(128)S(1)}, f32[12]{0:T(128)}, u32[]{:S(2)}) copy-start(f32[12]{0:T(128)} %dif.3) | copy-start | bytes 148
  0.7 6.4 %copy-start.7 = (f32[12]{0:T(128)S(1)}, f32[12]{0:T(128)}, u32[]{:S(2)}) copy-start(f32[12]{0:T(128)} %pre.1) | copy-start | bytes 148
  0.7 1.2 %copy-start = (f32[12,16,8,128]{3,2,1,0:T(8,128)S(1)}, f32[12,16,8,128]{3,2,1,0:T(8,128)}, u32[]{:S(2)}) copy-start(f32[12,16,8,128]{3,2,1,0:T(8,128)} %param.9) | copy-start | bytes 2359300
  1.8 5.2 %copy-start.1 = (f32[128,32]{0,1:T(8,128)S(1)}, f32[128,32]{0,1:T(8,128)}, u32[]{:S(2)}) copy-start(f32[128,32]{0,1:T(8,128)} %param.15) | copy-start | bytes 49156
  1.8 5.2 %copy-start.2 = (f32[12,12]{1,0:T(8,128)S(1)}, f32[12,12]{1,0:T(8,128)}, u32[]{:S(2)}) copy-start(f32[12,12]{1,0:T(8,128)} %mix_ref.1) | copy-start | bytes 1732
  1.8 5.3 %copy-start.4 = (f32[12,6]{0,1:T(8,128)S(1)}, f32[12,6]{0,1:T(8,128)}, u32[]{:S(2)}) copy-start(f32[12,6]{0,1:T(8,128)} %param.16) | copy-start | bytes 868
  1.8 11.5 %copy-start.3 = (f32[16,64]{1,0:T(8,128)S(1)}, f32[16,64]{1,0:T(8,128)}, u32[]{:S(2)}) copy-start(f32[16,64]{1,0:T(8,128)} %bx_ref.1) | copy-start | bytes 12292
  1.9 11.4 %collective-permute-start.1 = (f32[384,128]{1,0:T(8,128)S(1)}, f32[384,128]{1,0:T(8,128)S(1)}, u32[]{:S(2)}, u32[]{:S(2)}) collective-permute-start(f32[384,128]{1,0:T(8,128)S(1)} %get-tuple-element.27), channel_id=1, source_target_pairs={{0,1},{2,3},{4,5},{6,7},{1,0},{3,2},{5,4},{7,6},{8,9},{10,11},{12,... | collective-permute-start | bytes 589832 | tf_op jit(solution)/shard_map/ppermute | solution.py:588
  5.0 8.4 %collective-permute-start.2 = (f32[384,128]{1,0:T(8,128)S(1)}, f32[384,128]{1,0:T(8,128)S(1)}, u32[]{:S(2)}, u32[]{:S(2)}) collective-permute-start(f32[384,128]{1,0:T(8,128)S(1)} %get-tuple-element.28), channel_id=1, source_target_pairs={{1,2},{3,4},{5,6},{2,1},{4,3},{6,5},{9,10},{11,12},{13,14},{10,9},... | collective-permute-start | bytes 589832 | tf_op jit(solution)/shard_map/ppermute | solution.py:589
  5.7 1.4 %collective-permute-start = (f32[192,128]{1,0:T(8,128)S(1)}, f32[192,128]{1,0:T(8,128)S(1)}, u32[]{:S(2)}, u32[]{:S(2)}) collective-permute-start(f32[192,128]{1,0:T(8,128)S(1)} %get-tuple-element.25), channel_id=1, source_target_pairs={{0,8},{16,24},{8,0},{24,16},{1,9},{17,25},{9,1},{25,17},{2,10},{18... | collective-permute-start | bytes 294920 | tf_op jit(solution)/shard_map/ppermute | solution.py:592
  5.8 3.6 %collective-permute-start.3 = (f32[192,128]{1,0:T(8,128)S(1)}, f32[192,128]{1,0:T(8,128)S(1)}, u32[]{:S(2)}, u32[]{:S(2)}) collective-permute-start(f32[192,128]{1,0:T(8,128)S(1)} %get-tuple-element.29), channel_id=1, source_target_pairs={{8,16},{16,8},{9,17},{17,9},{10,18},{18,10},{11,19},{19,11},{12,20... | collective-permute-start | bytes 294920 | tf_op jit(solution)/shard_map/ppermute | solution.py:591
  15.6 4.9 %collective-permute-start.4 = (f32[232,128]{1,0:T(8,128)S(1)}, f32[232,128]{1,0:T(8,128)S(1)}, u32[]{:S(2)}, u32[]{:S(2)}) collective-permute-start(f32[232,128]{1,0:T(8,128)S(1)} %get-tuple-element.33.own_ref.refs_0_), channel_id=1, source_target_pairs={{0,16},{8,24},{16,0},{24,8},{1,17},{9,25},{17,1},{25,9},{2,18},{10... | collective-permute-start | bytes 356360 | tf_op jit(solution)/shard_map/ppermute | solution.py:568
  17.2 6.2 %collective-permute-start.5 = (f32[232,128]{1,0:T(8,128)S(1)}, f32[232,128]{1,0:T(8,128)S(1)}, u32[]{:S(2)}, u32[]{:S(2)}) collective-permute-start(f32[232,128]{1,0:T(8,128)S(1)} %get-tuple-element.33.own_ref.refs_0_), channel_id=1, source_target_pairs={{0,8},{8,0},{16,24},{24,16},{1,9},{9,1},{17,25},{25,17},{2,10},{10... | collective-permute-start | bytes 356360 | tf_op jit(solution)/shard_map/ppermute | solution.py:568
  20.5 4.1 %collective-permute-start.6 = (f32[232,128]{1,0:T(8,128)S(1)}, f32[232,128]{1,0:T(8,128)S(1)}, u32[]{:S(2)}, u32[]{:S(2)}) collective-permute-start(f32[232,128]{1,0:T(8,128)S(1)} %collective-permute-done.4.refs_0_.refs_1_), channel_id=1, source_target_pairs={{0,8},{8,0},{16,24},{24,16},{1,9},{9,1},{17,25},{25,17},{2,10},{10... | collective-permute-start | bytes 356360 | tf_op jit(solution)/shard_map/ppermute | solution.py:568
  20.5 1.3 %collective-permute-start.7 = (f32[24,128]{1,0:T(8,128)S(1)}, f32[24,128]{1,0:T(8,128)S(1)}, u32[]{:S(2)}, u32[]{:S(2)}) collective-permute-start(f32[24,128]{1,0:T(8,128)S(1)} %get-tuple-element.35), channel_id=1, source_target_pairs={{0,8},{16,24},{8,0},{24,16},{1,9},{17,25},{9,1},{25,17},{2,10},{18... | collective-permute-start | bytes 36872 | tf_op jit(solution)/shard_map/ppermute | solution.py:618
  26.2 13.1 %all-to-all-start = ((f32[32,1,128]{2,1,0:T(1,128)}), f32[32,1,128]{2,1,0:T(1,128)S(1)}, u32[]{:S(2)}, u32[]{:S(2)}) async-start(f32[32,1,128]{2,1,0:T(1,128)} %bitcast.6), calls=%async_computation | async-start | bytes 32768 | tf_op jit(solution)/shard_map/all_to_all | solution.py:657
